TPU v7x, 32 devices: a whole 2x2x4 slice. The times are simulated.
32 devices in a mesh: grp: 2 (over x), ev: 4 (over y, core), hd: 4 (over z).
Axes of the slice: x: 2, y: 2, z: 4, core: 2. Of those that a mesh axis runs over, the one named last changes fastest.
Arguments:
- hist_keys: bfloat16 [8, 16384, 1024], P('grp', 'ev', 'hd'), parts along dimension 0, may hold values from -6 to 6
- hist_values: bfloat16 [8, 16384, 1024], P('grp', 'ev', 'hd'), parts along dimension 0, may hold values from -6 to 6
- hist_len: int32 [8], P('grp'), parts along dimension 0, may hold values from 4096 to 16384
- new_queries: bfloat16 [8, 1024, 1024], P('grp', 'ev', 'hd'), parts along dimension 0, may hold values from -6 to 6
- event_gate: bfloat16 [8, 1024, 1024], P('grp', 'ev', 'hd'), parts along dimension 0, may hold values from -6 to 6
- key_weight: bfloat16 [1024, 1024], P(None, 'hd'), may hold values from -0.1875 to 0.1875
- value_weight: bfloat16 [1024, 1024], P(None, 'hd'), may hold values from -0.1875 to 0.1875
- event_gain: float32 [1024], P('hd'), may hold values from 0.25 to 1.75
- cand_queries: bfloat16 [4096, 1024], P(('grp', 'ev'), 'hd'), parts along dimension 0, may hold values from -6 to 6
- cand_gate: bfloat16 [4096, 1024], P(('grp', 'ev'), 'hd'), parts along dimension 0, may hold values from -6 to 6
- cand_gain: float32 [1024], P('hd'), may hold values from 0.25 to 1.75
- block_user: int32 [32], P(('grp', 'ev')), parts along dimension 0, may hold values from 0 to 3, as said below
- cand_count: int32 [8], P('grp'), parts along dimension 0, may hold values from 1 to 1024, as said below
Outputs:
- event_out: bfloat16 [8, 1024, 1024], P('grp', 'ev', 'hd'), parts along dimension 0
- cand_out: bfloat16 [4096, 1024], P(('grp', 'ev'), 'hd'), parts along dimension 0
There are 2 independent parts, one for each index of `grp`. A program takes and returns all parts, laid end to end along the dimension named above; an argument that names none is the same for every part. Nothing has to cross between parts.
Inputs may be any that keep to these rules, and one draw needn't show every extreme that they name: `block_user`: blocks belong to users in order: the first ceil(cand_count[0] / 128) blocks to user 0, the next ceil(cand_count[1] / 128) to user 1, and so on; every user has at least one block and all 16 blocks are used. `cand_count`: the blocks of users add up to 16 as stated for block_user; one user has exactly 8 full blocks.
All inputs are finite; a program needn't handle non-finite values.
Results may differ from a plain program's by a relative error of at most 0.0072.
Values may be sent and summed in bfloat16 or wider, within the bound.
No kernel may reach another device: no remote copies, remote signals or barrier semaphores. Data moves between devices by JAX's collectives and lax.ppermute only.
A program may use at most 128 MiB of HBM per device.

v0:
```python
import jax
import jax.numpy as jnp
from jax import lax
from jax.experimental import pallas as pl
from jax.experimental.pallas import tpu as pltpu
from jax.sharding import PartitionSpec as P


HEAD = 128
BLOCK = 128
EPSILON = 1e-05
SCALE = HEAD ** (-0.5)
HALF = 0.5 * SCALE
BF16 = jnp.bfloat16
F32 = jnp.float32
ANY = pl.BlockSpec(memory_space=pl.ANY)
SMALL = pltpu.CompilerParams(vmem_limit_bytes=12 << 20)
LARGE = pltpu.CompilerParams(vmem_limit_bytes=20 << 20)


def qk(q, k):
    return lax.dot_general(q, k, (((1,), (1,)), ((), ())), preferred_element_type=F32)


def head_norm(values, gain):
    centre = jnp.mean(values, axis=-1, keepdims=True)
    shifted = values - centre
    spread = jnp.mean(shifted * shifted, axis=-1, keepdims=True)
    return shifted * lax.rsqrt(spread + EPSILON) * gain


def swap(x, axis, size, j):
    return lax.ppermute(x, axis, [(i, i ^ j) for i in range(size)])


def full(shape):
    return pl.BlockSpec(shape, lambda *_: (0,) * len(shape))


def weigh(q, k, v, left):
    hist_rows = k[1]
    tile = min(hist_rows, 256)
    o = jnp.zeros((q.shape[0], HEAD), F32)
    for t in range(0, hist_rows, tile):
        row = t + lax.broadcasted_iota(jnp.int32, (tile, HEAD), 0)
        some = jnp.where(row < left, v[0](t, t + tile), jnp.zeros((tile, HEAD), BF16))
        u = qk(q, k[0](t, t + tile)) * HALF
        w = (u + u * jnp.tanh(u)).astype(BF16)
        o = o + jnp.dot(w, some, preferred_element_type=F32)
    return o


def join(parts):
    return parts[0] if len(parts) == 1 else jnp.concatenate(parts, axis=0)


def attend_cost(rows, hist_rows, width, hist_bytes):
    return pl.CostEstimate(
        flops=8 * rows * hist_rows * width,
        transcendentals=rows * hist_rows * width // HEAD,
        bytes_accessed=hist_bytes,
    )


def attend_near(users, queries, hist_len, place, keys, values):
    n = len(queries)
    _, rows, width = queries[0].shape
    hist_rows = keys.shape[1]

    def kern(len_ref, place_ref, *refs):
        q_refs, k_ref, v_ref, o_refs = refs[:n], refs[n], refs[n + 1], refs[n + 2 :]
        left = len_ref[pl.program_id(1)] - place_ref[0] * hist_rows

        @pl.when(left > 0)
        def _():
            q = join([r[0] for r in q_refs])
            k = (lambda a, b: k_ref[0, a:b], hist_rows)
            v = (lambda a, b: v_ref[0, a:b], hist_rows)
            o = weigh(q, k, v, left)
            for m, o_ref in enumerate(o_refs):
                o_ref[...] = o[m * rows : (m + 1) * rows].astype(o_ref.dtype)

        @pl.when(left <= 0)
        def _():
            for o_ref in o_refs:
                o_ref[...] = jnp.zeros(o_ref.shape, o_ref.dtype)

    piece = pl.BlockSpec((1, rows, HEAD), lambda h, g, *_: (g, 0, h))
    hist = pl.BlockSpec((1, hist_rows, HEAD), lambda h, g, *_: (g, 0, h))
    return pl.pallas_call(
        kern,
        grid_spec=pltpu.PrefetchScalarGridSpec(
            num_scalar_prefetch=2,
            grid=(width // HEAD, users),
            in_specs=[piece] * n + [hist, hist],
            out_specs=[pl.BlockSpec((rows, HEAD), lambda h, g, *_: (g, h))] * n,
        ),
        out_shape=[jax.ShapeDtypeStruct((users * rows, width), BF16 if i else F32) for i in range(n)],
        cost_estimate=attend_cost(users * n * rows, hist_rows, width, 4 * users * hist_rows * width),
        compiler_params=LARGE,
    )(hist_len, place, *queries, keys, values)


def attend(first_user, counts, half_rows, start, together, queries, own_first, hist_len, place, keys, values, after):
    n = len(queries)
    width = queries[0].shape[2]
    hist_rows = keys.shape[1]
    users = len(counts)
    take = max(counts)
    total = sum(counts) * half_rows
    n_after = len(after)
    block = width if together else HEAD

    def kern(len_ref, place_ref, *refs):
        q_refs, k_ref, v_ref = refs[:n], refs[n], refs[n + 1]
        o_refs = refs[n + 2 + n_after :]
        for g in range(users):
            user = first_user + g
            rows = counts[g] * half_rows
            at = sum(counts[:g]) * half_rows
            left = len_ref[user] - place_ref[0] * hist_rows

            @pl.when(left > 0)
            def _(g=g, user=user, rows=rows, at=at, left=left):
                for h in range(block // HEAD):
                    cols = slice(h * HEAD, (h + 1) * HEAD)
                    head = cols if together else pl.ds(pl.multiple_of(pl.program_id(0) * HEAD, HEAD), HEAD)
                    q = join([r[g, :rows, cols] for r in q_refs])
                    k = (lambda a, b, head=head: k_ref[user, a:b, head], hist_rows)
                    v = (lambda a, b, head=head: v_ref[user, a:b, head], hist_rows)
                    o = weigh(q, k, v, left)
                    for m, o_ref in enumerate(o_refs):
                        o_ref[at : at + rows, cols] = o[m * rows : (m + 1) * rows].astype(o_ref.dtype)

            @pl.when(left <= 0)
            def _(rows=rows, at=at):
                for o_ref in o_refs:
                    o_ref[at : at + rows, :] = jnp.zeros((rows, block), o_ref.dtype)

    assert first_user % users == 0
    piece = pl.BlockSpec((users, take * half_rows, block), lambda h, *_: (first_user // users, start, h))
    resident = pl.BlockSpec(memory_space=pltpu.VMEM)
    kinds = [F32 if own_first and i == 0 else BF16 for i in range(n)]
    return pl.pallas_call(
        kern,
        grid_spec=pltpu.PrefetchScalarGridSpec(
            num_scalar_prefetch=2,
            grid=(width // block,),
            in_specs=[piece] * n + [resident, resident] + [ANY] * n_after,
            out_specs=[pl.BlockSpec((total, block), lambda h, *_: (0, h))] * n,
        ),
        out_shape=[jax.ShapeDtypeStruct((total, width), kind) for kind in kinds],
        cost_estimate=attend_cost(n * total, hist_rows, width, 4 * users * hist_rows * width),
        compiler_params=LARGE,
    )(hist_len, place, *queries, keys, values, *after)


def gate_events(own, others, rows, gate_at, gain, gate):
    n = len(others)
    width = gate.shape[1]

    def kern(own_ref, *refs):
        p_refs, gain_ref, gate_ref, o_ref = refs[:n], refs[n], refs[n + 1], refs[n + 2]
        for h in range(width // HEAD):
            cols = slice(h * HEAD, (h + 1) * HEAD)
            total = own_ref[:, cols]
            for p in p_refs:
                total = total + p[:, cols].astype(F32)
            o_ref[:, cols] = (
                head_norm(total, gain_ref[:, cols]) * gate_ref[:, cols].astype(F32)
            ).astype(BF16)

    def at(offset):
        return pl.BlockSpec((pl.Element(rows), pl.Element(width)), lambda i: (offset, 0))

    return pl.pallas_call(
        kern,
        grid=(1,),
        in_specs=[at(offset) for _, offset in [own, *others]] + [full((1, width)), at(gate_at)],
        out_specs=full((rows, width)),
        out_shape=jax.ShapeDtypeStruct((rows, width), BF16),
        compiler_params=SMALL,
    )(*[array for array, _ in [own, *others]], gain, gate)


def user_of(block, count_ref, n_users):
    end = jnp.int32(0)
    user = jnp.int32(0)
    first = jnp.int32(0)
    for u in range(n_users - 1):
        end = end + lax.shift_right_logical(count_ref[u] + (BLOCK - 1), 7)
        past = block >= end
        user = jnp.where(past, u + 1, user)
        first = jnp.where(past, end, first)
    return user, first


def project(e_refs, n_hd, sizes, col_ref, wk, wv, k_ref, v_ref, at):
    part = wk.shape[0] // n_hd
    for c, size in enumerate(sizes):
        k = jnp.zeros((size, wk.shape[1]), F32)
        v = jnp.zeros((size, wk.shape[1]), F32)
        for j in range(n_hd):
            from_row = pl.ds(pl.multiple_of((col_ref[0] ^ j) * part, part), part)
            e = e_refs[c * n_hd + j][...]
            k += jnp.dot(e, wk[from_row, :], preferred_element_type=F32)
            v += jnp.dot(e, wv[from_row, :], preferred_element_type=F32)
        k_ref[at : at + size, :] = k.astype(BF16)
        v_ref[at : at + size, :] = v.astype(BF16)
        at += size


def early_keys(chunks, column, key_weight, value_weight):
    n_hd = len(chunks[0])
    flat = [p for c in chunks for p in c]
    sizes = [c[0].shape[0] for c in chunks]
    shape = (sum(sizes), key_weight.shape[1])

    def kern(col_ref, *refs):
        project(refs[: len(flat)], n_hd, sizes, col_ref, *refs[len(flat) :], 0)

    return pl.pallas_call(
        kern,
        grid_spec=pltpu.PrefetchScalarGridSpec(
            num_scalar_prefetch=1,
            grid=(1,),
            in_specs=[full(e.shape) for e in flat] + [full(key_weight.shape)] * 2,
            out_specs=[full(shape)] * 2,
        ),
        out_shape=[jax.ShapeDtypeStruct(shape, BF16)] * 2,
        compiler_params=SMALL,
        name="early_keys",
    )(column, *flat, key_weight, value_weight)


def cand_sums(n_users, early, chunks, cands, cand_count, place, column, key_weight, value_weight):
    n = len(cands)
    n_hd = len(chunks[0])
    width = key_weight.shape[1]
    flat = [p for c in chunks for p in c]
    sizes = [c[0].shape[0] for c in chunks]
    done = early[0].shape[0]
    rows = (done + sum(sizes)) // n_users
    blocks = cands[0].shape[0] // BLOCK

    def kern(count_ref, place_ref, col_ref, *refs):
        e_refs, refs = refs[: len(flat)], refs[len(flat) :]
        wk, wv, early_k, early_v = refs[:4]
        q_refs = refs[4 : 4 + n]
        keep_ref, send_ref, k_ref, v_ref = refs[-4:]
        k_ref[:done, :] = early_k[...]
        v_ref[:done, :] = early_v[...]
        project(e_refs, n_hd, sizes, col_ref, wk, wv, k_ref, v_ref, done)
        for j in range(n):
            o_ref = send_ref if j & 1 else keep_ref
            for i in range(blocks):
                user, _ = user_of((place_ref[0] ^ j) * blocks + i, count_ref, n_users)
                rws = slice(i * BLOCK, (i + 1) * BLOCK)
                own = pl.ds(pl.multiple_of(user * rows, rows), rows)
                for h in range(width // HEAD):
                    cols = slice(h * HEAD, (h + 1) * HEAD)
                    t = qk(q_refs[j][rws, cols], k_ref[own, cols]) * HALF
                    w = (t + t * jnp.tanh(t)).astype(BF16)
                    o = jnp.dot(w, v_ref[own, cols], preferred_element_type=F32)
                    o_ref[j // 2, rws, cols] = o.astype(o_ref.dtype)

    shape = (max(n // 2, 1), blocks * BLOCK, width)
    return pl.pallas_call(
        kern,
        grid_spec=pltpu.PrefetchScalarGridSpec(
            num_scalar_prefetch=3,
            grid=(1,),
            in_specs=[full(e.shape) for e in flat]
            + [full(key_weight.shape)] * 2
            + [full(early[0].shape)] * 2
            + [full(c.shape) for c in cands],
            out_specs=[full(shape)] * 2,
            scratch_shapes=[pltpu.VMEM((rows * n_users, width), BF16)] * 2,
        ),
        out_shape=[jax.ShapeDtypeStruct(shape, F32), jax.ShapeDtypeStruct(shape, BF16)],
        compiler_params=SMALL,
        name="cand_sums",
    )(cand_count, place, column, *flat, key_weight, value_weight, *early, *cands)


def gate_cands(own, others, cand_count, place, gain, gate):
    n = 1 + len(others)
    n_users = cand_count.shape[0]
    rows, width = gate.shape

    def kern(count_ref, place_ref, *refs):
        p_refs, gain_ref, gate_ref, o_ref = refs[:n], refs[n], refs[n + 1], refs[n + 2]
        for i in range(rows // BLOCK):
            rws = slice(i * BLOCK, (i + 1) * BLOCK)
            block = place_ref[0] * (rows // BLOCK) + i
            user, first = user_of(block, count_ref, n_users)
            limit = count_ref[user] - (block - first) * BLOCK
            live = lax.broadcasted_iota(jnp.int32, (BLOCK, HEAD), 0) < limit
            for h in range(width // HEAD):
                cols = slice(h * HEAD, (h + 1) * HEAD)
                total = p_refs[0][0, rws, cols].astype(F32)
                for p in p_refs[1:]:
                    total = total + p[0, rws, cols].astype(F32)
                out = head_norm(total, gain_ref[:, cols]) * gate_ref[rws, cols].astype(F32)
                o_ref[rws, cols] = jnp.where(live, out, 0.0).astype(BF16)

    part = pl.BlockSpec((1, rows, width), lambda i, *_: (0, 0, 0))
    block = full((rows, width))
    return pl.pallas_call(
        kern,
        grid_spec=pltpu.PrefetchScalarGridSpec(
            num_scalar_prefetch=2,
            grid=(1,),
            in_specs=[part] * n + [full((1, width)), block],
            out_specs=block,
        ),
        out_shape=jax.ShapeDtypeStruct((rows, width), BF16),
        compiler_params=SMALL,
        name="gate_cands",
    )(cand_count, place, own, *others, gain, gate)


def gather_pieces(x, axis, size):
    pieces = [x] + [None] * (size - 1)
    bit = size // 2
    while bit:
        for j in range(0, size, 2 * bit):
            pieces[j + bit] = swap(pieces[j], axis, size, bit)
        bit //= 2
    return pieces


def make_local(n_ev, n_hd):
    def local(
        hist_keys,
        hist_values,
        hist_len,
        new_queries,
        event_gate,
        key_weight,
        value_weight,
        event_gain,
        cand_queries,
        cand_gate,
        cand_gain,
        block_user,
        cand_count,
    ):
        n_users, rows, width = new_queries.shape
        half = rows // 2
        place = lax.axis_index("ev").astype(jnp.int32).reshape(1)
        column = lax.axis_index("hd").astype(jnp.int32).reshape(1)
        event_gain = event_gain.reshape(1, width)
        cand_gain = cand_gain.reshape(1, width)
        gates = event_gate.reshape(n_users * rows, width)
        queries = gather_pieces(new_queries, "ev", n_ev)
        queries[0], *in_hbm = [
            pltpu.with_memory_space_constraint(x, pltpu.HBM) for x in (new_queries, hist_keys, hist_values)
        ]
        cands = gather_pieces(cand_queries, "ev", n_ev)
        keys, values = [pltpu.with_memory_space_constraint(x, pltpu.VMEM) for x in (hist_keys, hist_values)]
        hist = (hist_len, place, keys, values)

        def exchange(pieces, first):
            return [swap(p, "ev", n_ev, first + j) for j, p in enumerate(pieces)]

        def gate_chunk(own, others, halves, gate_at):
            return gate_events(own, others, halves * half, gate_at * half, event_gain, gates)

        own01, *near01 = attend_near(2, queries[:2], hist_len, place, *in_hbm)
        got01 = exchange(near01, 1)
        far0 = attend(0, (2,), half, 0, True, queries[2:], False, *hist, (own01,))
        far1 = attend(1, (2,), half, 0, True, queries[2:], False, *hist, (far0[0],))
        got0, got1 = exchange(far0, 2), exchange(far1, 2)
        gated0 = gate_chunk((own01, 0), [(x, 0) for x in got01 + got0], 2, 0)
        out2 = attend(2, (2, 1), half, 0, False, queries, True, *hist, (gated0, far1[0]))
        gated1 = gate_chunk((own01, rows), [(x, rows) for x in got01] + [(x, 0) for x in got1], 2, 2)
        out3 = attend(3, (1,), half, 1, True, queries, True, *hist, (gated1, out2[0]))
        got2, got3 = exchange(out2[1:], 1), exchange(out3[1:], 1)
        gated2 = gate_chunk((out2[0], 0), [(x, 0) for x in got2], 3, 4)
        gated3 = gate_chunk((out3[0], 0), [(x, 0) for x in got3], 1, 7)
        gated = [gated0, gated1, gated2, gated3]
        all_columns = [gather_pieces(g, "hd", n_hd) for g in gated]
        early = early_keys(all_columns[:2], column, key_weight, value_weight)
        keep, send = cand_sums(
            n_users, early, all_columns[2:], cands, cand_count, place, column, key_weight, value_weight
        )
        if n_ev == 1:
            cand_out = gate_cands(keep, [], cand_count, place, cand_gain, cand_gate)
        else:
            came = swap(send, "ev", n_ev, 1)
            bit = 2
            while bit < n_ev:
                total = keep + came.astype(F32)
                keep = total[0::2]
                came = swap(total[1::2].astype(BF16), "ev", n_ev, bit)
                bit *= 2
            cand_out = gate_cands(keep, [came], cand_count, place, cand_gain, cand_gate)
        event_out = jnp.concatenate(gated, axis=0)
        return event_out.reshape(n_users, rows, width), cand_out

    return local


def solution(mesh):
    return jax.shard_map(
        make_local(mesh.shape["ev"], mesh.shape["hd"]),
        mesh=mesh,
        in_specs=(
            P("grp", "ev", "hd"),
            P("grp", "ev", "hd"),
            P("grp"),
            P("grp", "ev", "hd"),
            P("grp", "ev", "hd"),
            P(None, "hd"),
            P(None, "hd"),
            P("hd"),
            P(("grp", "ev"), "hd"),
            P(("grp", "ev"), "hd"),
            P("hd"),
            P(("grp", "ev")),
            P("grp"),
        ),
        out_specs=(P("grp", "ev", "hd"), P(("grp", "ev"), "hd")),
        check_vma=False,
    )
```

profile of v0, /device:TPU:0, one launch (start us, length us, event | category | flops | bytes accessed | tf_op | source)
XLA Modules:
  0.0 133.9 jit_solution(2664758314284775207)
XLA Ops:
  0.6 3.1 %collective-permute-start.2 = (bf16[4,256,256]{2,1,0:T(8,128)(2,1)}, bf16[4,256,256]{2,1,0:T(8,128)(2,1)S(1)}, u32[]{:S(2)}, u32[]{:S(2)}) collective-permute-start(bf16[4,256,256]{2,1,0:T(8,128)(2,1)} %refs_0_.5), channel_id=1, source_target_pairs={{0,8},{4,12},{8,0},{12,4},{1,9},{5,13},{9,1},{13,5},{2,10},{6,14},... | collective-permute-start | bytes 1572872 | tf_op jit(solution)/shard_map/ppermute | solution.py:33
  4.2 12.5 %collective-permute-done.2.refs_0_.refs_2_ = bf16[4,256,256]{2,1,0:T(8,128)(2,1)S(1)} collective-permute-done((bf16[4,256,256]{2,1,0:T(8,128)(2,1)}, bf16[4,256,256]{2,1,0:T(8,128)(2,1)S(1)}, u32[]{:S(2)}, u32[]{:S(2)}) %collective-permute-start.2) | collective-permute-done | bytes 524320 | tf_op jit(solution)/shard_map/ppermute | solution.py:33
  17.3 13.3 %shard_map.131 = (f32[512,256]{1,0:T(8,128)S(1)}, bf16[512,256]{1,0:T(8,128)(2,1)S(1)}) custom-call(s32[4]{0:T(128)S(1)} %copy-done.20, s32[1]{0:T(128)} %bitcast.place_ref, bf16[4,256,256]{2,1,0:T(8,128)(2,1)} %refs_0_.5, bf16[4,256,256]{2,1,0:T(8,128)(2,1)S(1)} %collective-permute-done.refs_1_, bf16[4,4096,256]{2,1,0:T(8,128)(2,1)} %refs_4_.3, ...), custom_call_target="tpu_custom_call" | custom-call | flops 8589934592 | bytes 8388608 | tf_op jit(solution)/shard_map/pallas_call | solution.py:90
  30.8 5.7 %shard_map.132 = (bf16[256,256]{1,0:T(8,128)(2,1)S(1)}, bf16[256,256]{1,0:T(8,128)(2,1)S(1)}) custom-call(s32[4]{0:T(128)S(1)} %copy-done.20, s32[1]{0:T(128)} %bitcast.place_ref, bf16[4,256,256]{2,1,0:T(8,128)(2,1)S(1)} %collective-permute-done.2.refs_0_.refs_2_, bf16[4,256,256]{2,1,0:T(8,128)(2,1)S(1)} %collective-permute-done.3.refs_1_.refs_3_, ...), custom_call_target="tpu_custom_call" | custom-call | flops 4294967296 | bytes 4194304 | tf_op jit(solution)/shard_map/pallas_call | solution.py:144
  36.6 6.1 %shard_map.134 = (bf16[256,256]{1,0:T(8,128)(2,1)S(1)}, bf16[256,256]{1,0:T(8,128)(2,1)S(1)}) custom-call(s32[4]{0:T(128)S(1)} %copy-done.20, s32[1]{0:T(128)} %bitcast.place_ref, bf16[4,256,256]{2,1,0:T(8,128)(2,1)S(1)} %collective-permute-done.2.refs_0_.refs_2_, bf16[4,256,256]{2,1,0:T(8,128)(2,1)S(1)} %collective-permute-done.3.refs_1_.refs_3_, ...), custom_call_target="tpu_custom_call" | custom-call | flops 4294967296 | bytes 4194304 | tf_op jit(solution)/shard_map/pallas_call | solution.py:144
  42.7 2.0 %collective-permute-start.6 = (bf16[256,256]{1,0:T(8,128)(2,1)S(1)}, bf16[256,256]{1,0:T(8,128)(2,1)S(1)}, u32[]{:S(2)}, u32[]{:S(2)}) collective-permute-start(bf16[256,256]{1,0:T(8,128)(2,1)S(1)} %get-tuple-element.24.refs_7_), channel_id=1, source_target_pairs={{0,8},{4,12},{8,0},{12,4},{1,9},{5,13},{9,1},{13,5},{2,10},{6,14},... | collective-permute-start | bytes 393224 | tf_op jit(solution)/shard_map/ppermute | solution.py:33
  44.6 1.5 %collective-permute-start.7 = (bf16[256,256]{1,0:T(8,128)(2,1)S(1)}, bf16[256,256]{1,0:T(8,128)(2,1)S(1)}, u32[]{:S(2)}, u32[]{:S(2)}) collective-permute-start(bf16[256,256]{1,0:T(8,128)(2,1)S(1)} %get-tuple-element.25), channel_id=1, source_target_pairs={{0,12},{4,8},{8,4},{12,0},{1,13},{5,9},{9,5},{13,1},{2,14},{6,10},... | collective-permute-start | bytes 393224 | tf_op jit(solution)/shard_map/ppermute | solution.py:33
  46.4 16.9 %shard_map.136 = (f32[384,256]{1,0:T(8,128)S(1)}, bf16[384,256]{1,0:T(8,128)(2,1)S(1)}, bf16[384,256]{1,0:T(8,128)(2,1)S(1)}, bf16[384,256]{1,0:T(8,128)(2,1)S(1)}) custom-call(s32[4]{0:T(128)S(1)} %copy-done.20, s32[1]{0:T(128)} %bitcast.place_ref, bf16[4,256,256]{2,1,0:T(8,128)(2,1)} %refs_0_.5, bf16[4,256,256]{2,1,0:T(8,128)(2,1)S(1)} %collective-permute-done.refs_1_, ...), custom_call_target="tpu_custom_call" | custom-call | flops 12884901888 | bytes 8388608 | tf_op jit(solution)/shard_map/pallas_call | solution.py:144
  63.9 1.7 %collective-permute-start.9 = (bf16[384,256]{1,0:T(8,128)(2,1)S(1)}, bf16[384,256]{1,0:T(8,128)(2,1)S(1)}, u32[]{:S(2)}, u32[]{:S(2)}) collective-permute-start(bf16[384,256]{1,0:T(8,128)(2,1)S(1)} %get-tuple-element.28), channel_id=1, source_target_pairs={{0,8},{4,12},{8,0},{12,4},{1,9},{5,13},{9,1},{13,5},{2,10},{6,14},... | collective-permute-start | bytes 589832 | tf_op jit(solution)/shard_map/ppermute | solution.py:33
  65.8 6.5 %shard_map.138 = (f32[128,256]{1,0:T(8,128)S(1)}, bf16[128,256]{1,0:T(8,128)(2,1)S(1)}, bf16[128,256]{1,0:T(8,128)(2,1)S(1)}, bf16[128,256]{1,0:T(8,128)(2,1)S(1)}) custom-call(s32[4]{0:T(128)S(1)} %copy-done.20, s32[1]{0:T(128)} %bitcast.place_ref, bf16[4,256,256]{2,1,0:T(8,128)(2,1)} %refs_0_.5, bf16[4,256,256]{2,1,0:T(8,128)(2,1)S(1)} %collective-permute-done.refs_1_, ...), custom_call_target="tpu_custom_call" | custom-call | flops 4294967296 | bytes 4194304 | tf_op jit(solution)/shard_map/pallas_call | solution.py:144
  72.4 3.2 %collective-permute-start.24 = (bf16[256,256]{1,0:T(8,128)(2,1)S(1)}, bf16[256,256]{1,0:T(8,128)(2,1)S(1)}, u32[]{:S(2)}, u32[]{:S(2)}) collective-permute-start(bf16[256,256]{1,0:T(8,128)(2,1)S(1)} %shard_map.135.refs_6_.refs_4_), channel_id=1, source_target_pairs={{0,2},{1,3},{2,0},{3,1},{4,6},{5,7},{6,4},{7,5},{8,10},{9,11},{10,... | collective-permute-start | bytes 393224 | tf_op jit(solution)/shard_map/ppermute | solution.py:33
  75.9 1.1 collective-permute-start.13
  77.1 1.6 %collective-permute-start.23 = (bf16[256,256]{1,0:T(8,128)(2,1)S(1)}, bf16[256,256]{1,0:T(8,128)(2,1)S(1)}, u32[]{:S(2)}, u32[]{:S(2)}) collective-permute-start(bf16[256,256]{1,0:T(8,128)(2,1)S(1)} %shard_map.135.refs_6_.refs_4_), channel_id=1, source_target_pairs={{0,1},{1,0},{2,3},{3,2},{4,5},{5,4},{6,7},{7,6},{8,9},{9,8},{10,11... | collective-permute-start | bytes 393224 | tf_op jit(solution)/shard_map/ppermute | solution.py:33
  79.4 1.0 collective-permute-done.12.refs_1_
  80.4 1.6 %collective-permute-start.21 = (bf16[256,256]{1,0:T(8,128)(2,1)S(1)}, bf16[256,256]{1,0:T(8,128)(2,1)S(1)}, u32[]{:S(2)}, u32[]{:S(2)}) collective-permute-start(bf16[256,256]{1,0:T(8,128)(2,1)S(1)} %shard_map.133.refs_6_.refs_0_), channel_id=1, source_target_pairs={{0,2},{1,3},{2,0},{3,1},{4,6},{5,7},{6,4},{7,5},{8,10},{9,11},{10,... | collective-permute-start | bytes 393224 | tf_op jit(solution)/shard_map/ppermute | solution.py:33
  82.8 2.8 %collective-permute-done.23.refs_5_ = bf16[256,256]{1,0:T(8,128)(2,1)S(1)} collective-permute-done((bf16[256,256]{1,0:T(8,128)(2,1)S(1)}, bf16[256,256]{1,0:T(8,128)(2,1)S(1)}, u32[]{:S(2)}, u32[]{:S(2)}) %collective-permute-start.23) | collective-permute-done | bytes 131104 | tf_op jit(solution)/shard_map/ppermute | solution.py:33
  86.8 11.9 %collective-permute-done.21.refs_2_ = bf16[256,256]{1,0:T(8,128)(2,1)S(1)} collective-permute-done((bf16[256,256]{1,0:T(8,128)(2,1)S(1)}, bf16[256,256]{1,0:T(8,128)(2,1)S(1)}, u32[]{:S(2)}, u32[]{:S(2)}) %collective-permute-start.21) | collective-permute-done | bytes 131104 | tf_op jit(solution)/shard_map/ppermute | solution.py:33
  100.1 2.0 %collective-permute-start.22 = (bf16[256,256]{1,0:T(8,128)(2,1)S(1)}, bf16[256,256]{1,0:T(8,128)(2,1)S(1)}, u32[]{:S(2)}, u32[]{:S(2)}) collective-permute-start(bf16[256,256]{1,0:T(8,128)(2,1)S(1)} %collective-permute-done.21.refs_2_), channel_id=1, source_target_pairs={{0,1},{1,0},{2,3},{3,2},{4,5},{5,4},{6,7},{7,6},{8,9},{9,8},{10,11... | collective-permute-start | bytes 393224 | tf_op jit(solution)/shard_map/ppermute | solution.py:33
  102.7 2.0 %collective-permute-start.16 = (bf16[384,256]{1,0:T(8,128)(2,1)S(1)}, bf16[384,256]{1,0:T(8,128)(2,1)}, u32[]{:S(2)}, u32[]{:S(2)}) collective-permute-start(bf16[384,256]{1,0:T(8,128)(2,1)S(1)} %collective-permute-done.15.refs_2_), channel_id=1, source_target_pairs={{0,1},{1,0},{2,3},{3,2},{4,5},{5,4},{6,7},{7,6},{8,9},{9,8},{10,11... | collective-permute-start | bytes 589832 | tf_op jit(solution)/shard_map/ppermute | solution.py:33
  105.7 2.1 %collective-permute-done.22.refs_3_ = bf16[256,256]{1,0:T(8,128)(2,1)S(1)} collective-permute-done((bf16[256,256]{1,0:T(8,128)(2,1)S(1)}, bf16[256,256]{1,0:T(8,128)(2,1)S(1)}, u32[]{:S(2)}, u32[]{:S(2)}) %collective-permute-start.22) | collective-permute-done | bytes 131104 | tf_op jit(solution)/shard_map/ppermute | solution.py:33
  109.1 0.9 copy-done.8
  110.0 0.9 copy-done.10
  110.9 0.9 copy-done.12
  111.8 0.9 copy-done.14
  112.7 0.9 copy-done.16
  113.6 0.9 copy-done.18
  115.3 1.9 %collective-permute-done.17.refs_5_ = bf16[128,256]{1,0:T(8,128)(2,1)} collective-permute-done((bf16[128,256]{1,0:T(8,128)(2,1)S(1)}, bf16[128,256]{1,0:T(8,128)(2,1)}, u32[]{:S(2)}, u32[]{:S(2)}) %collective-permute-start.17) | collective-permute-done | bytes 65568 | tf_op jit(solution)/shard_map/ppermute | solution.py:33
  117.9 3.6 %cand_sums.1 = (f32[2,512,256]{2,1,0:T(8,128)S(1)}, bf16[2,512,256]{2,1,0:T(8,128)(2,1)S(1)}) custom-call(s32[4]{0:T(128)S(1)} %copy-done.21, s32[1]{0:T(128)} %bitcast.place_ref, s32[1]{0:T(128)} %bitcast.4.col_ref, bf16[384,256]{1,0:T(8,128)(2,1)S(1)} %shard_map.137.refs_0_, bf16[384,256]{1,0:T(8,128)(2,1)S(1)} %collective-permute-done.14.refs_1_, ...), custom_call_target="tpu_custom_call" | custom-call | tf_op jit(solution)/shard_map/cand_sums/pallas_call | solution.py:268
  121.6 1.9 %collective-permute-done.29 = bf16[2,512,256]{2,1,0:T(8,128)(2,1)S(1)} collective-permute-done((bf16[2,512,256]{2,1,0:T(8,128)(2,1)S(1)}, bf16[2,512,256]{2,1,0:T(8,128)(2,1)S(1)}, u32[]{:S(2)}, u32[]{:S(2)}) %collective-permute-start.29) | collective-permute-done | bytes 524320 | tf_op jit(solution)/shard_map/ppermute | solution.py:33
  124.2 0.8 pad_maximum_fusion
  125.0 7.0 %collective-permute-done.30.refs_1_ = bf16[1,512,256]{2,1,0:T(8,128)(2,1)S(1)} collective-permute-done((bf16[1,512,256]{2,1,0:T(8,128)(2,1)S(1)}, bf16[1,512,256]{2,1,0:T(8,128)(2,1)S(1)}, u32[]{:S(2)}, u32[]{:S(2)}) %collective-permute-start.30) | collective-permute-done | bytes 262176 | tf_op jit(solution)/shard_map/ppermute | solution.py:33
  132.1 1.9 %gate_cands.1 = bf16[512,256]{1,0:T(8,128)(2,1)} custom-call(s32[4]{0:T(128)S(1)} %copy-done.21, s32[1]{0:T(128)} %bitcast.place_ref, f32[1,512,256]{2,1,0:T(8,128)S(1)} %slice.11.refs_0_, bf16[1,512,256]{2,1,0:T(8,128)(2,1)S(1)} %collective-permute-done.30.refs_1_, f32[1,256]{1,0:T(1,128)S(1)} %bitcast.14, bf16[512,256]{1,0:T(8,128)(2,1)S(1)} %copy-done.6), custom_call_target="tpu_custom_call" | custom-call | tf_op jit(solution)/shard_map/gate_cands/pallas_call | solution.py:309
  (92 shorter events, 12.0 us)
Async XLA Ops:
  0.6 16.0 %collective-permute-start.2 = (bf16[4,256,256]{2,1,0:T(8,128)(2,1)}, bf16[4,256,256]{2,1,0:T(8,128)(2,1)S(1)}, u32[]{:S(2)}, u32[]{:S(2)}) collective-permute-start(bf16[4,256,256]{2,1,0:T(8,128)(2,1)} %refs_0_.5), channel_id=1, source_target_pairs={{0,8},{4,12},{8,0},{12,4},{1,9},{5,13},{9,1},{13,5},{2,10},{6,14},... | collective-permute-start | bytes 1572872 | tf_op jit(solution)/shard_map/ppermute | solution.py:33
  3.7 13.0 %collective-permute-start = (bf16[4,256,256]{2,1,0:T(8,128)(2,1)}, bf16[4,256,256]{2,1,0:T(8,128)(2,1)S(1)}, u32[]{:S(2)}, u32[]{:S(2)}) collective-permute-start(bf16[4,256,256]{2,1,0:T(8,128)(2,1)} %refs_0_.5), channel_id=1, source_target_pairs={{0,4},{4,0},{8,12},{12,8},{1,5},{5,1},{9,13},{13,9},{2,6},{6,2},{1... | collective-permute-start | bytes 1572872 | tf_op jit(solution)/shard_map/ppermute | solution.py:33
  3.7 68.6 %collective-permute-start.27 = (bf16[512,256]{1,0:T(8,128)(2,1)}, bf16[512,256]{1,0:T(8,128)(2,1)S(1)}, u32[]{:S(2)}, u32[]{:S(2)}) collective-permute-start(bf16[512,256]{1,0:T(8,128)(2,1)} %refs_12_.1), channel_id=1, source_target_pairs={{0,8},{4,12},{8,0},{12,4},{1,9},{5,13},{9,1},{13,5},{2,10},{6,14},... | collective-permute-start | bytes 786440 | tf_op jit(solution)/shard_map/ppermute | solution.py:33
  3.9 68.6 %collective-permute-start.26 = (bf16[512,256]{1,0:T(8,128)(2,1)}, bf16[512,256]{1,0:T(8,128)(2,1)S(1)}, u32[]{:S(2)}, u32[]{:S(2)}) collective-permute-start(bf16[512,256]{1,0:T(8,128)(2,1)} %refs_12_.1), channel_id=1, source_target_pairs={{0,4},{4,0},{8,12},{12,8},{1,5},{5,1},{9,13},{13,9},{2,6},{6,2},{1... | collective-permute-start | bytes 786440 | tf_op jit(solution)/shard_map/ppermute | solution.py:33
  16.7 14.0 %collective-permute-start.3 = (bf16[4,256,256]{2,1,0:T(8,128)(2,1)S(1)}, bf16[4,256,256]{2,1,0:T(8,128)(2,1)S(1)}, u32[]{:S(2)}, u32[]{:S(2)}) collective-permute-start(bf16[4,256,256]{2,1,0:T(8,128)(2,1)S(1)} %collective-permute-done.2.refs_0_.refs_2_), channel_id=1, source_target_pairs={{0,4},{4,0},{8,12},{12,8},{1,5},{5,1},{9,13},{13,9},{2,6},{6,2},{1... | collective-permute-start | bytes 1572872 | tf_op jit(solution)/shard_map/ppermute | solution.py:33
  30.6 12.0 %collective-permute-start.1 = (bf16[512,256]{1,0:T(8,128)(2,1)S(1)}, bf16[512,256]{1,0:T(8,128)(2,1)S(1)}, u32[]{:S(2)}, u32[]{:S(2)}) collective-permute-start(bf16[512,256]{1,0:T(8,128)(2,1)S(1)} %get-tuple-element.21), channel_id=1, source_target_pairs={{0,4},{4,0},{8,12},{12,8},{1,5},{5,1},{9,13},{13,9},{2,6},{6,2},{1... | collective-permute-start | bytes 786440 | tf_op jit(solution)/shard_map/ppermute | solution.py:33
  36.4 8.2 %collective-permute-start.4 = (bf16[256,256]{1,0:T(8,128)(2,1)S(1)}, bf16[256,256]{1,0:T(8,128)(2,1)S(1)}, u32[]{:S(2)}, u32[]{:S(2)}) collective-permute-start(bf16[256,256]{1,0:T(8,128)(2,1)S(1)} %get-tuple-element.22.refs_4_), channel_id=1, source_target_pairs={{0,8},{4,12},{8,0},{12,4},{1,9},{5,13},{9,1},{13,5},{2,10},{6,14},... | collective-permute-start | bytes 393224 | tf_op jit(solution)/shard_map/ppermute | solution.py:33
  36.5 9.6 %collective-permute-start.5 = (bf16[256,256]{1,0:T(8,128)(2,1)S(1)}, bf16[256,256]{1,0:T(8,128)(2,1)S(1)}, u32[]{:S(2)}, u32[]{:S(2)}) collective-permute-start(bf16[256,256]{1,0:T(8,128)(2,1)S(1)} %get-tuple-element.23), channel_id=1, source_target_pairs={{0,12},{4,8},{8,4},{12,0},{1,13},{5,9},{9,5},{13,1},{2,14},{6,10},... | collective-permute-start | bytes 393224 | tf_op jit(solution)/shard_map/ppermute | solution.py:33
  42.7 21.0 %collective-permute-start.6 = (bf16[256,256]{1,0:T(8,128)(2,1)S(1)}, bf16[256,256]{1,0:T(8,128)(2,1)S(1)}, u32[]{:S(2)}, u32[]{:S(2)}) collective-permute-start(bf16[256,256]{1,0:T(8,128)(2,1)S(1)} %get-tuple-element.24.refs_7_), channel_id=1, source_target_pairs={{0,8},{4,12},{8,0},{12,4},{1,9},{5,13},{9,1},{13,5},{2,10},{6,14},... | collective-permute-start | bytes 393224 | tf_op jit(solution)/shard_map/ppermute | solution.py:33
  44.6 19.2 %collective-permute-start.7 = (bf16[256,256]{1,0:T(8,128)(2,1)S(1)}, bf16[256,256]{1,0:T(8,128)(2,1)S(1)}, u32[]{:S(2)}, u32[]{:S(2)}) collective-permute-start(bf16[256,256]{1,0:T(8,128)(2,1)S(1)} %get-tuple-element.25), channel_id=1, source_target_pairs={{0,12},{4,8},{8,4},{12,0},{1,13},{5,9},{9,5},{13,1},{2,14},{6,10},... | collective-permute-start | bytes 393224 | tf_op jit(solution)/shard_map/ppermute | solution.py:33
  63.3 12.3 %collective-permute-start.10 = (bf16[384,256]{1,0:T(8,128)(2,1)S(1)}, bf16[384,256]{1,0:T(8,128)(2,1)S(1)}, u32[]{:S(2)}, u32[]{:S(2)}) collective-permute-start(bf16[384,256]{1,0:T(8,128)(2,1)S(1)} %get-tuple-element.29), channel_id=1, source_target_pairs={{0,12},{4,8},{8,4},{12,0},{1,13},{5,9},{9,5},{13,1},{2,14},{6,10},... | collective-permute-start | bytes 589832 | tf_op jit(solution)/shard_map/ppermute | solution.py:33
  63.7 12.3 %collective-permute-start.8 = (bf16[384,256]{1,0:T(8,128)(2,1)S(1)}, bf16[384,256]{1,0:T(8,128)(2,1)S(1)}, u32[]{:S(2)}, u32[]{:S(2)}) collective-permute-start(bf16[384,256]{1,0:T(8,128)(2,1)S(1)} %get-tuple-element.27), channel_id=1, source_target_pairs={{0,4},{4,0},{8,12},{12,8},{1,5},{5,1},{9,13},{13,9},{2,6},{6,2},{1... | collective-permute-start | bytes 589832 | tf_op jit(solution)/shard_map/ppermute | solution.py:33
  63.9 13.2 %collective-permute-start.9 = (bf16[384,256]{1,0:T(8,128)(2,1)S(1)}, bf16[384,256]{1,0:T(8,128)(2,1)S(1)}, u32[]{:S(2)}, u32[]{:S(2)}) collective-permute-start(bf16[384,256]{1,0:T(8,128)(2,1)S(1)} %get-tuple-element.28), channel_id=1, source_target_pairs={{0,8},{4,12},{8,0},{12,4},{1,9},{5,13},{9,1},{13,5},{2,10},{6,14},... | collective-permute-start | bytes 589832 | tf_op jit(solution)/shard_map/ppermute | solution.py:33
  72.3 59.8 %copy-start.6 = (bf16[512,256]{1,0:T(8,128)(2,1)S(1)}, bf16[512,256]{1,0:T(8,128)(2,1)}, u32[]{:S(2)}) copy-start(bf16[512,256]{1,0:T(8,128)(2,1)} %refs_3_.7) | copy-start | bytes 786436
  72.3 6.7 %collective-permute-start.11 = (bf16[128,256]{1,0:T(8,128)(2,1)S(1)}, bf16[128,256]{1,0:T(8,128)(2,1)S(1)}, u32[]{:S(2)}, u32[]{:S(2)}) collective-permute-start(bf16[128,256]{1,0:T(8,128)(2,1)S(1)} %get-tuple-element.31), channel_id=1, source_target_pairs={{0,4},{4,0},{8,12},{12,8},{1,5},{5,1},{9,13},{13,9},{2,6},{6,2},{1... | collective-permute-start | bytes 196616 | tf_op jit(solution)/shard_map/ppermute | solution.py:33
  72.4 10.3 %collective-permute-start.24 = (bf16[256,256]{1,0:T(8,128)(2,1)S(1)}, bf16[256,256]{1,0:T(8,128)(2,1)S(1)}, u32[]{:S(2)}, u32[]{:S(2)}) collective-permute-start(bf16[256,256]{1,0:T(8,128)(2,1)S(1)} %shard_map.135.refs_6_.refs_4_), channel_id=1, source_target_pairs={{0,2},{1,3},{2,0},{3,1},{4,6},{5,7},{6,4},{7,5},{8,10},{9,11},{10,... | collective-permute-start | bytes 393224 | tf_op jit(solution)/shard_map/ppermute | solution.py:33
  75.6 4.8 %collective-permute-start.12 = (bf16[128,256]{1,0:T(8,128)(2,1)S(1)}, bf16[128,256]{1,0:T(8,128)(2,1)S(1)}, u32[]{:S(2)}, u32[]{:S(2)}) collective-permute-start(bf16[128,256]{1,0:T(8,128)(2,1)S(1)} %get-tuple-element.32), channel_id=1, source_target_pairs={{0,8},{4,12},{8,0},{12,4},{1,9},{5,13},{9,1},{13,5},{2,10},{6,14},... | collective-permute-start | bytes 196616 | tf_op jit(solution)/shard_map/ppermute | solution.py:33
  75.9 6.1 %collective-permute-start.13 = (bf16[128,256]{1,0:T(8,128)(2,1)S(1)}, bf16[128,256]{1,0:T(8,128)(2,1)S(1)}, u32[]{:S(2)}, u32[]{:S(2)}) collective-permute-start(bf16[128,256]{1,0:T(8,128)(2,1)S(1)} %get-tuple-element.33), channel_id=1, source_target_pairs={{0,12},{4,8},{8,4},{12,0},{1,13},{5,9},{9,5},{13,1},{2,14},{6,10},... | collective-permute-start | bytes 196616 | tf_op jit(solution)/shard_map/ppermute | solution.py:33
  77.1 8.6 %collective-permute-start.23 = (bf16[256,256]{1,0:T(8,128)(2,1)S(1)}, bf16[256,256]{1,0:T(8,128)(2,1)S(1)}, u32[]{:S(2)}, u32[]{:S(2)}) collective-permute-start(bf16[256,256]{1,0:T(8,128)(2,1)S(1)} %shard_map.135.refs_6_.refs_4_), channel_id=1, source_target_pairs={{0,1},{1,0},{2,3},{3,2},{4,5},{5,4},{6,7},{7,6},{8,9},{9,8},{10,11... | collective-permute-start | bytes 393224 | tf_op jit(solution)/shard_map/ppermute | solution.py:33
  79.0 23.7 %collective-permute-start.15 = (bf16[384,256]{1,0:T(8,128)(2,1)S(1)}, bf16[384,256]{1,0:T(8,128)(2,1)S(1)}, u32[]{:S(2)}, u32[]{:S(2)}) collective-permute-start(bf16[384,256]{1,0:T(8,128)(2,1)S(1)} %shard_map.137.refs_0_), channel_id=1, source_target_pairs={{0,2},{1,3},{2,0},{3,1},{4,6},{5,7},{6,4},{7,5},{8,10},{9,11},{10,... | collective-permute-start | bytes 589832 | tf_op jit(solution)/shard_map/ppermute | solution.py:33
  80.4 18.3 %collective-permute-start.21 = (bf16[256,256]{1,0:T(8,128)(2,1)S(1)}, bf16[256,256]{1,0:T(8,128)(2,1)S(1)}, u32[]{:S(2)}, u32[]{:S(2)}) collective-permute-start(bf16[256,256]{1,0:T(8,128)(2,1)S(1)} %shard_map.133.refs_6_.refs_0_), channel_id=1, source_target_pairs={{0,2},{1,3},{2,0},{3,1},{4,6},{5,7},{6,4},{7,5},{8,10},{9,11},{10,... | collective-permute-start | bytes 393224 | tf_op jit(solution)/shard_map/ppermute | solution.py:33
  82.0 17.4 %collective-permute-start.20 = (bf16[256,256]{1,0:T(8,128)(2,1)S(1)}, bf16[256,256]{1,0:T(8,128)(2,1)S(1)}, u32[]{:S(2)}, u32[]{:S(2)}) collective-permute-start(bf16[256,256]{1,0:T(8,128)(2,1)S(1)} %shard_map.133.refs_6_.refs_0_), channel_id=1, source_target_pairs={{0,1},{1,0},{2,3},{3,2},{4,5},{5,4},{6,7},{7,6},{8,9},{9,8},{10,11... | collective-permute-start | bytes 393224 | tf_op jit(solution)/shard_map/ppermute | solution.py:33
  82.7 32.6 %collective-permute-start.28 = (bf16[512,256]{1,0:T(8,128)(2,1)S(1)}, bf16[512,256]{1,0:T(8,128)(2,1)S(1)}, u32[]{:S(2)}, u32[]{:S(2)}) collective-permute-start(bf16[512,256]{1,0:T(8,128)(2,1)S(1)} %collective-permute-done.27.refs_14_), channel_id=1, source_target_pairs={{0,4},{4,0},{8,12},{12,8},{1,5},{5,1},{9,13},{13,9},{2,6},{6,2},{1... | collective-permute-start | bytes 786440 | tf_op jit(solution)/shard_map/ppermute | solution.py:33
  86.3 16.4 %collective-permute-start.18 = (bf16[128,256]{1,0:T(8,128)(2,1)S(1)}, bf16[128,256]{1,0:T(8,128)(2,1)}, u32[]{:S(2)}, u32[]{:S(2)}) collective-permute-start(bf16[128,256]{1,0:T(8,128)(2,1)S(1)} %shard_map.139.refs_4_), channel_id=1, source_target_pairs={{0,2},{1,3},{2,0},{3,1},{4,6},{5,7},{6,4},{7,5},{8,10},{9,11},{10,... | collective-permute-start | bytes 196616 | tf_op jit(solution)/shard_map/ppermute | solution.py:33
  98.7 6.3 %collective-permute-start.25 = (bf16[256,256]{1,0:T(8,128)(2,1)S(1)}, bf16[256,256]{1,0:T(8,128)(2,1)S(1)}, u32[]{:S(2)}, u32[]{:S(2)}) collective-permute-start(bf16[256,256]{1,0:T(8,128)(2,1)S(1)} %collective-permute-done.24.refs_6_), channel_id=1, source_target_pairs={{0,1},{1,0},{2,3},{3,2},{4,5},{5,4},{6,7},{7,6},{8,9},{9,8},{10,11... | collective-permute-start | bytes 393224 | tf_op jit(solution)/shard_map/ppermute | solution.py:33
  100.1 7.8 %collective-permute-start.22 = (bf16[256,256]{1,0:T(8,128)(2,1)S(1)}, bf16[256,256]{1,0:T(8,128)(2,1)S(1)}, u32[]{:S(2)}, u32[]{:S(2)}) collective-permute-start(bf16[256,256]{1,0:T(8,128)(2,1)S(1)} %collective-permute-done.21.refs_2_), channel_id=1, source_target_pairs={{0,1},{1,0},{2,3},{3,2},{4,5},{5,4},{6,7},{7,6},{8,9},{9,8},{10,11... | collective-permute-start | bytes 393224 | tf_op jit(solution)/shard_map/ppermute | solution.py:33
  102.7 15.1 %collective-permute-start.14 = (bf16[384,256]{1,0:T(8,128)(2,1)S(1)}, bf16[384,256]{1,0:T(8,128)(2,1)S(1)}, u32[]{:S(2)}, u32[]{:S(2)}) collective-permute-start(bf16[384,256]{1,0:T(8,128)(2,1)S(1)} %shard_map.137.refs_0_), channel_id=1, source_target_pairs={{0,1},{1,0},{2,3},{3,2},{4,5},{5,4},{6,7},{7,6},{8,9},{9,8},{10,11... | collective-permute-start | bytes 589832 | tf_op jit(solution)/shard_map/ppermute | solution.py:33
  102.7 15.1 %collective-permute-start.16 = (bf16[384,256]{1,0:T(8,128)(2,1)S(1)}, bf16[384,256]{1,0:T(8,128)(2,1)}, u32[]{:S(2)}, u32[]{:S(2)}) collective-permute-start(bf16[384,256]{1,0:T(8,128)(2,1)S(1)} %collective-permute-done.15.refs_2_), channel_id=1, source_target_pairs={{0,1},{1,0},{2,3},{3,2},{4,5},{5,4},{6,7},{7,6},{8,9},{9,8},{10,11... | collective-permute-start | bytes 589832 | tf_op jit(solution)/shard_map/ppermute | solution.py:33
  105.7 11.5 %collective-permute-start.17 = (bf16[128,256]{1,0:T(8,128)(2,1)S(1)}, bf16[128,256]{1,0:T(8,128)(2,1)}, u32[]{:S(2)}, u32[]{:S(2)}) collective-permute-start(bf16[128,256]{1,0:T(8,128)(2,1)S(1)} %shard_map.139.refs_4_), channel_id=1, source_target_pairs={{0,1},{1,0},{2,3},{3,2},{4,5},{5,4},{6,7},{7,6},{8,9},{9,8},{10,11... | collective-permute-start | bytes 196616 | tf_op jit(solution)/shard_map/ppermute | solution.py:33
  108.5 9.4 %collective-permute-start.19 = (bf16[128,256]{1,0:T(8,128)(2,1)}, bf16[128,256]{1,0:T(8,128)(2,1)}, u32[]{:S(2)}, u32[]{:S(2)}) collective-permute-start(bf16[128,256]{1,0:T(8,128)(2,1)} %collective-permute-done.18.refs_6_), channel_id=1, source_target_pairs={{0,1},{1,0},{2,3},{3,2},{4,5},{5,4},{6,7},{7,6},{8,9},{9,8},{10,11... | collective-permute-start | bytes 196616 | tf_op jit(solution)/shard_map/ppermute | solution.py:33
  121.5 2.0 %collective-permute-start.29 = (bf16[2,512,256]{2,1,0:T(8,128)(2,1)S(1)}, bf16[2,512,256]{2,1,0:T(8,128)(2,1)S(1)}, u32[]{:S(2)}, u32[]{:S(2)}) collective-permute-start(bf16[2,512,256]{2,1,0:T(8,128)(2,1)S(1)} %get-tuple-element.37), channel_id=1, source_target_pairs={{0,4},{4,0},{8,12},{12,8},{1,5},{5,1},{9,13},{13,9},{2,6},{6,2},{1... | collective-permute-start | bytes 1572872 | tf_op jit(solution)/shard_map/ppermute | solution.py:33
  123.7 8.4 %collective-permute-start.30 = (bf16[1,512,256]{2,1,0:T(8,128)(2,1)S(1)}, bf16[1,512,256]{2,1,0:T(8,128)(2,1)S(1)}, u32[]{:S(2)}, u32[]{:S(2)}) collective-permute-start(bf16[1,512,256]{2,1,0:T(8,128)(2,1)S(1)} %slice.14), channel_id=1, source_target_pairs={{0,8},{4,12},{8,0},{12,4},{1,9},{5,13},{9,1},{13,5},{2,10},{6,14},... | collective-permute-start | bytes 786440 | tf_op jit(solution)/shard_map/ppermute | solution.py:33
  (22 other events, 306.7 us)
where the time goes:
time: 134 us
  Pallas kernels  55.6 us (41%)
  waiting for transfers between devices  42.2 us (31%)
  starting transfers between devices  24.1 us (18%)
  local copies, waits for them, and re-layouts  10.1 us (8%)
    ppermute x31, waiting for transfers between devices, swap(): return lax.ppermute(x, axis, [(i, i ^ j) for i in range(size)])  42.2 us
    pallas_call x4, Pallas kernels, attend(): pl.pallas_call(kern, grid_spec=pltpu.PrefetchScalarGridSpec(num_scalar_pr...  35.1 us
    ppermute x31, starting transfers between devices, swap(): return lax.ppermute(x, axis, [(i, i ^ j) for i in range(size)])  24.1 us
    pallas_call x1, Pallas kernels, attend_near(): pl.pallas_call(kern, grid_spec=pltpu.PrefetchScalarGridSpec(num_scalar_pr...  13.3 us
    unnamed x46, local copies, waits for them, and re-layouts  10.1 us
    pallas_call x1, Pallas kernels, cand_sums(): pl.pallas_call(kern, grid_spec=pltpu.PrefetchScalarGridSpec(num_scalar_pr...  3.63 us
  transfers between devices with their start and end apart: 31, of which 10 were waited for; matrix products, arithmetic and copies ran while one was open for 1% of the time, Pallas kernels for 37%

commit v1 on v0

--- a/solution.py
+++ b/solution.py
@@ -233,54 +233,60 @@
     )(column, *flat, key_weight, value_weight)
 
 
-def cand_sums(n_users, early, chunks, cands, cand_count, place, column, key_weight, value_weight):
+def late_keys(refs, early_refs, chunks, column_ref, keys_out):
+    n_hd = len(chunks[0])
+    sizes = [c[0].shape[0] for c in chunks]
+    done = early_refs[0].shape[0]
+    n_flat = n_hd * len(chunks)
+    for out, early in zip(keys_out, early_refs):
+        out[:done, :] = early[...]
+    project(refs[:n_flat], n_hd, sizes, column_ref, *refs[n_flat : n_flat + 2], *keys_out, done)
+
+
+def cand_sums(n_users, source, chunks, cands, at, cand_count, place, column, weights):
     n = len(cands)
-    n_hd = len(chunks[0])
-    width = key_weight.shape[1]
+    width = cands[0].shape[1]
     flat = [p for c in chunks for p in c]
-    sizes = [c[0].shape[0] for c in chunks]
-    done = early[0].shape[0]
-    rows = (done + sum(sizes)) // n_users
+    extra = [*flat, *weights] if chunks else []
+    rows = (source[0].shape[0] + sum(c[0].shape[0] for c in chunks)) // n_users
     blocks = cands[0].shape[0] // BLOCK
 
     def kern(count_ref, place_ref, col_ref, *refs):
-        e_refs, refs = refs[: len(flat)], refs[len(flat) :]
-        wk, wv, early_k, early_v = refs[:4]
-        q_refs = refs[4 : 4 + n]
-        keep_ref, send_ref, k_ref, v_ref = refs[-4:]
-        k_ref[:done, :] = early_k[...]
-        v_ref[:done, :] = early_v[...]
-        project(e_refs, n_hd, sizes, col_ref, wk, wv, k_ref, v_ref, done)
-        for j in range(n):
-            o_ref = send_ref if j & 1 else keep_ref
+        q_refs, refs = refs[:n], refs[n:]
+        o_refs = refs[len(extra) + 2 :][:n]
+        k_ref, v_ref = refs[len(extra) :][:2]
+        if chunks:
+            keys_out = refs[-2:]
+            late_keys(refs, (k_ref, v_ref), chunks, col_ref, keys_out)
+            k_ref, v_ref = keys_out
+        for m, j in enumerate(at):
             for i in range(blocks):
                 user, _ = user_of((place_ref[0] ^ j) * blocks + i, count_ref, n_users)
                 rws = slice(i * BLOCK, (i + 1) * BLOCK)
                 own = pl.ds(pl.multiple_of(user * rows, rows), rows)
                 for h in range(width // HEAD):
                     cols = slice(h * HEAD, (h + 1) * HEAD)
-                    t = qk(q_refs[j][rws, cols], k_ref[own, cols]) * HALF
+                    t = qk(q_refs[m][rws, cols], k_ref[own, cols]) * HALF
                     w = (t + t * jnp.tanh(t)).astype(BF16)
                     o = jnp.dot(w, v_ref[own, cols], preferred_element_type=F32)
-                    o_ref[j // 2, rws, cols] = o.astype(o_ref.dtype)
-
-    shape = (max(n // 2, 1), blocks * BLOCK, width)
+                    o_refs[m][rws, cols] = o.astype(o_refs[m].dtype)
+
+    piece = cands[0].shape
+    shapes = [jax.ShapeDtypeStruct(piece, BF16 if j & 1 else F32) for j in at]
+    if chunks:
+        shapes += [jax.ShapeDtypeStruct((rows * n_users, width), BF16)] * 2
+    operands = [*cands, *extra, *source]
     return pl.pallas_call(
         kern,
         grid_spec=pltpu.PrefetchScalarGridSpec(
             num_scalar_prefetch=3,
             grid=(1,),
-            in_specs=[full(e.shape) for e in flat]
-            + [full(key_weight.shape)] * 2
-            + [full(early[0].shape)] * 2
-            + [full(c.shape) for c in cands],
-            out_specs=[full(shape)] * 2,
-            scratch_shapes=[pltpu.VMEM((rows * n_users, width), BF16)] * 2,
-        ),
-        out_shape=[jax.ShapeDtypeStruct(shape, F32), jax.ShapeDtypeStruct(shape, BF16)],
+            in_specs=[full(x.shape) for x in operands],
+            out_specs=[full(x.shape) for x in shapes],
+        ),
+        out_shape=shapes,
         compiler_params=SMALL,
-        name="cand_sums",
-    )(cand_count, place, column, *flat, key_weight, value_weight, *early, *cands)
+    )(cand_count, place, column, *operands)
 
 
 def gate_cands(own, others, cand_count, place, gain, gate):
@@ -298,20 +304,19 @@
             live = lax.broadcasted_iota(jnp.int32, (BLOCK, HEAD), 0) < limit
             for h in range(width // HEAD):
                 cols = slice(h * HEAD, (h + 1) * HEAD)
-                total = p_refs[0][0, rws, cols].astype(F32)
+                total = p_refs[0][rws, cols]
                 for p in p_refs[1:]:
-                    total = total + p[0, rws, cols].astype(F32)
+                    total = total + p[rws, cols].astype(F32)
                 out = head_norm(total, gain_ref[:, cols]) * gate_ref[rws, cols].astype(F32)
                 o_ref[rws, cols] = jnp.where(live, out, 0.0).astype(BF16)
 
-    part = pl.BlockSpec((1, rows, width), lambda i, *_: (0, 0, 0))
     block = full((rows, width))
     return pl.pallas_call(
         kern,
         grid_spec=pltpu.PrefetchScalarGridSpec(
             num_scalar_prefetch=2,
             grid=(1,),
-            in_specs=[part] * n + [full((1, width)), block],
+            in_specs=[block] * n + [full((1, width)), block],
             out_specs=block,
         ),
         out_shape=jax.ShapeDtypeStruct((rows, width), BF16),
@@ -373,29 +378,34 @@
         far1 = attend(1, (2,), half, 0, True, queries[2:], False, *hist, (far0[0],))
         got0, got1 = exchange(far0, 2), exchange(far1, 2)
         gated0 = gate_chunk((own01, 0), [(x, 0) for x in got01 + got0], 2, 0)
-        out2 = attend(2, (2, 1), half, 0, False, queries, True, *hist, (gated0, far1[0]))
+        out2 = attend(2, (2,), half, 0, False, queries, True, *hist, (gated0, far1[0]))
         gated1 = gate_chunk((own01, rows), [(x, rows) for x in got01] + [(x, 0) for x in got1], 2, 2)
-        out3 = attend(3, (1,), half, 1, True, queries, True, *hist, (gated1, out2[0]))
+        out3 = attend(3, (2,), half, 0, False, queries, True, *hist, (gated1, out2[0]))
         got2, got3 = exchange(out2[1:], 1), exchange(out3[1:], 1)
-        gated2 = gate_chunk((out2[0], 0), [(x, 0) for x in got2], 3, 4)
-        gated3 = gate_chunk((out3[0], 0), [(x, 0) for x in got3], 1, 7)
+        gated2 = gate_chunk((out2[0], 0), [(x, 0) for x in got2], 2, 4)
+        gated3 = gate_chunk((out3[0], 0), [(x, 0) for x in got3], 2, 6)
         gated = [gated0, gated1, gated2, gated3]
         all_columns = [gather_pieces(g, "hd", n_hd) for g in gated]
         early = early_keys(all_columns[:2], column, key_weight, value_weight)
-        keep, send = cand_sums(
-            n_users, early, all_columns[2:], cands, cand_count, place, column, key_weight, value_weight
-        )
-        if n_ev == 1:
-            cand_out = gate_cands(keep, [], cand_count, place, cand_gain, cand_gate)
-        else:
-            came = swap(send, "ev", n_ev, 1)
-            bit = 2
-            while bit < n_ev:
-                total = keep + came.astype(F32)
-                keep = total[0::2]
-                came = swap(total[1::2].astype(BF16), "ev", n_ev, bit)
-                bit *= 2
-            cand_out = gate_cands(keep, [came], cand_count, place, cand_gain, cand_gate)
+        weights = (key_weight, value_weight)
+        near = list(range(min(2, n_ev)))
+        far = list(range(2, n_ev))
+        common = (cand_count, place, column, weights)
+        *sums, all_keys, all_values = cand_sums(n_users, early, all_columns[2:], [cands[j] for j in far], far, *common)
+        done = (all_keys, all_values)
+        sums = [*cand_sums(n_users, done, [], [cands[j] for j in near], near, *common), *sums]
+        held = {j: [x] for j, x in enumerate(sums)}
+        bit = 1
+        while bit < n_ev:
+            for j in sorted(held, reverse=True):
+                if j & bit:
+                    first, *others = held.pop(j)
+                    for x in others:
+                        first = first + x.astype(F32)
+                    held[j ^ bit].append(swap(first.astype(BF16), "ev", n_ev, bit))
+            bit *= 2
+        own, *others = held[0]
+        cand_out = gate_cands(own, others, cand_count, place, cand_gain, cand_gate)
         event_out = jnp.concatenate(gated, axis=0)
         return event_out.reshape(n_users, rows, width), cand_out
 

time: 134 us -> 133 us (level)
  local copies, waits for them, and re-layouts: 10.1 us -> 2.26 us
  starting transfers between devices: 24.1 us -> 29.5 us
    unnamed x46 -> x26, local copies, waits for them, and re-layouts: 10.1 us -> 2.26 us
    ppermute x31 -> x32, starting transfers between devices: 24.1 us -> 29.5 us  [swap(): return lax.ppermute(x, axis, [(i, i ^ j) for i in range(size)])]
    ppermute x31 -> x32, waiting for transfers between devices: 42.2 us -> 43.3 us  [swap(): return lax.ppermute(x, axis, [(i, i ^ j) for i in range(size)])]
    pallas_call x1 -> x2, Pallas kernels: 3.63 us -> 4.66 us  [cand_sums(): pl.pallas_call(kern, grid_spec=pltpu.PrefetchScalarGridSpec(num_scalar_pr...]
  transfers between devices with their start and end apart: 31 -> 32, of which waited for: 10 -> 14; matrix products, arithmetic and copies ran while one was open for 1% -> 1% of each run, Pallas kernels for 37% -> 41%
where the time goes in v1:
time: 133 us
  Pallas kernels  56 us (42%)
  waiting for transfers between devices  43.3 us (33%)
  starting transfers between devices  29.5 us (22%)
  local copies, waits for them, and re-layouts  2.26 us (2%)
    ppermute x32, waiting for transfers between devices, swap(): return lax.ppermute(x, axis, [(i, i ^ j) for i in range(size)])  43.3 us
    pallas_call x4, Pallas kernels, attend(): pl.pallas_call(kern, grid_spec=pltpu.PrefetchScalarGridSpec(num_scalar_pr...  34.5 us
    ppermute x32, starting transfers between devices, swap(): return lax.ppermute(x, axis, [(i, i ^ j) for i in range(size)])  29.5 us
    pallas_call x1, Pallas kernels, attend_near(): pl.pallas_call(kern, grid_spec=pltpu.PrefetchScalarGridSpec(num_scalar_pr...  13.3 us
    pallas_call x2, Pallas kernels, cand_sums(): pl.pallas_call(kern, grid_spec=pltpu.PrefetchScalarGridSpec(num_scalar_pr...  4.66 us
  transfers between devices with their start and end apart: 32, of which 14 were waited for; matrix products, arithmetic and copies ran while one was open for 1% of the time, Pallas kernels for 41%

profile of v1, /device:TPU:0, one launch (start us, length us, event | category | flops | bytes accessed | tf_op | source)
XLA Modules:
  0.0 132.8 jit_solution(5604638178606627346)
XLA Ops:
  0.6 3.1 %collective-permute-start.2 = (bf16[4,256,256]{2,1,0:T(8,128)(2,1)}, bf16[4,256,256]{2,1,0:T(8,128)(2,1)S(1)}, u32[]{:S(2)}, u32[]{:S(2)}) collective-permute-start(bf16[4,256,256]{2,1,0:T(8,128)(2,1)} %refs_0_.6), channel_id=1, source_target_pairs={{0,8},{4,12},{8,0},{12,4},{1,9},{5,13},{9,1},{13,5},{2,10},{6,14},... | collective-permute-start | bytes 1572872 | tf_op jit(solution)/shard_map/ppermute | solution.py:33
  3.7 12.1 %collective-permute-done.2.refs_0_.refs_2_ = bf16[4,256,256]{2,1,0:T(8,128)(2,1)S(1)} collective-permute-done((bf16[4,256,256]{2,1,0:T(8,128)(2,1)}, bf16[4,256,256]{2,1,0:T(8,128)(2,1)S(1)}, u32[]{:S(2)}, u32[]{:S(2)}) %collective-permute-start.2) | collective-permute-done | bytes 524320 | tf_op jit(solution)/shard_map/ppermute | solution.py:33
  16.5 13.3 %shard_map.131 = (f32[512,256]{1,0:T(8,128)S(1)}, bf16[512,256]{1,0:T(8,128)(2,1)S(1)}) custom-call(s32[4]{0:T(128)S(1)} %copy-done.11, s32[1]{0:T(128)} %bitcast.place_ref, bf16[4,256,256]{2,1,0:T(8,128)(2,1)} %refs_0_.6, bf16[4,256,256]{2,1,0:T(8,128)(2,1)S(1)} %collective-permute-done.refs_1_, bf16[4,4096,256]{2,1,0:T(8,128)(2,1)} %refs_4_.4, ...), custom_call_target="tpu_custom_call" | custom-call | flops 8589934592 | bytes 8388608 | tf_op jit(solution)/shard_map/pallas_call | solution.py:90
  29.9 5.7 %shard_map.132 = (bf16[256,256]{1,0:T(8,128)(2,1)S(1)}, bf16[256,256]{1,0:T(8,128)(2,1)S(1)}) custom-call(s32[4]{0:T(128)S(1)} %copy-done.11, s32[1]{0:T(128)} %bitcast.place_ref, bf16[4,256,256]{2,1,0:T(8,128)(2,1)S(1)} %collective-permute-done.2.refs_0_.refs_2_, bf16[4,256,256]{2,1,0:T(8,128)(2,1)S(1)} %collective-permute-done.3.refs_1_.refs_3_, ...), custom_call_target="tpu_custom_call" | custom-call | flops 4294967296 | bytes 4194304 | tf_op jit(solution)/shard_map/pallas_call | solution.py:144
  35.6 5.8 %shard_map.134 = (bf16[256,256]{1,0:T(8,128)(2,1)S(1)}, bf16[256,256]{1,0:T(8,128)(2,1)S(1)}) custom-call(s32[4]{0:T(128)S(1)} %copy-done.11, s32[1]{0:T(128)} %bitcast.place_ref, bf16[4,256,256]{2,1,0:T(8,128)(2,1)S(1)} %collective-permute-done.2.refs_0_.refs_2_, bf16[4,256,256]{2,1,0:T(8,128)(2,1)S(1)} %collective-permute-done.3.refs_1_.refs_3_, ...), custom_call_target="tpu_custom_call" | custom-call | flops 4294967296 | bytes 4194304 | tf_op jit(solution)/shard_map/pallas_call | solution.py:144
  41.6 1.9 %collective-permute-start.4 = (bf16[256,256]{1,0:T(8,128)(2,1)S(1)}, bf16[256,256]{1,0:T(8,128)(2,1)S(1)}, u32[]{:S(2)}, u32[]{:S(2)}) collective-permute-start(bf16[256,256]{1,0:T(8,128)(2,1)S(1)} %get-tuple-element.26.refs_4_), channel_id=1, source_target_pairs={{0,8},{4,12},{8,0},{12,4},{1,9},{5,13},{9,1},{13,5},{2,10},{6,14},... | collective-permute-start | bytes 393224 | tf_op jit(solution)/shard_map/ppermute | solution.py:33
  43.5 1.5 %collective-permute-start.5 = (bf16[256,256]{1,0:T(8,128)(2,1)S(1)}, bf16[256,256]{1,0:T(8,128)(2,1)S(1)}, u32[]{:S(2)}, u32[]{:S(2)}) collective-permute-start(bf16[256,256]{1,0:T(8,128)(2,1)S(1)} %get-tuple-element.27), channel_id=1, source_target_pairs={{0,12},{4,8},{8,4},{12,0},{1,13},{5,9},{9,5},{13,1},{2,14},{6,10},... | collective-permute-start | bytes 393224 | tf_op jit(solution)/shard_map/ppermute | solution.py:33
  45.3 2.6 %collective-permute-done.6.refs_1_ = bf16[256,256]{1,0:T(8,128)(2,1)S(1)} collective-permute-done((bf16[256,256]{1,0:T(8,128)(2,1)S(1)}, bf16[256,256]{1,0:T(8,128)(2,1)S(1)}, u32[]{:S(2)}, u32[]{:S(2)}) %collective-permute-start.6) | collective-permute-done | bytes 131104 | tf_op jit(solution)/shard_map/ppermute | solution.py:33
  48.1 2.9 %collective-permute-start.27 = (bf16[256,256]{1,0:T(8,128)(2,1)S(1)}, bf16[256,256]{1,0:T(8,128)(2,1)S(1)}, u32[]{:S(2)}, u32[]{:S(2)}) collective-permute-start(bf16[256,256]{1,0:T(8,128)(2,1)S(1)} %shard_map.135.refs_6_.refs_4_), channel_id=1, source_target_pairs={{0,2},{1,3},{2,0},{3,1},{4,6},{5,7},{6,4},{7,5},{8,10},{9,11},{10,... | collective-permute-start | bytes 393224 | tf_op jit(solution)/shard_map/ppermute | solution.py:33
  51.0 2.5 %collective-permute-done.4.refs_1_ = bf16[256,256]{1,0:T(8,128)(2,1)S(1)} collective-permute-done((bf16[256,256]{1,0:T(8,128)(2,1)S(1)}, bf16[256,256]{1,0:T(8,128)(2,1)S(1)}, u32[]{:S(2)}, u32[]{:S(2)}) %collective-permute-start.4) | collective-permute-done | bytes 131104 | tf_op jit(solution)/shard_map/ppermute | solution.py:33
  53.8 2.9 %collective-permute-start.24 = (bf16[256,256]{1,0:T(8,128)(2,1)S(1)}, bf16[256,256]{1,0:T(8,128)(2,1)S(1)}, u32[]{:S(2)}, u32[]{:S(2)}) collective-permute-start(bf16[256,256]{1,0:T(8,128)(2,1)S(1)} %shard_map.133.refs_6_.refs_0_), channel_id=1, source_target_pairs={{0,2},{1,3},{2,0},{3,1},{4,6},{5,7},{6,4},{7,5},{8,10},{9,11},{10,... | collective-permute-start | bytes 393224 | tf_op jit(solution)/shard_map/ppermute | solution.py:33
  56.6 11.4 %shard_map.136 = (f32[256,256]{1,0:T(8,128)S(1)}, bf16[256,256]{1,0:T(8,128)(2,1)S(1)}, bf16[256,256]{1,0:T(8,128)(2,1)S(1)}, bf16[256,256]{1,0:T(8,128)(2,1)S(1)}) custom-call(s32[4]{0:T(128)S(1)} %copy-done.11, s32[1]{0:T(128)} %bitcast.place_ref, bf16[4,256,256]{2,1,0:T(8,128)(2,1)} %refs_0_.6, bf16[4,256,256]{2,1,0:T(8,128)(2,1)S(1)} %collective-permute-done.refs_1_, ...), custom_call_target="tpu_custom_call" | custom-call | flops 8589934592 | bytes 4194304 | tf_op jit(solution)/shard_map/pallas_call | solution.py:144
  68.9 1.7 %collective-permute-start.8 = (bf16[256,256]{1,0:T(8,128)(2,1)S(1)}, bf16[256,256]{1,0:T(8,128)(2,1)S(1)}, u32[]{:S(2)}, u32[]{:S(2)}) collective-permute-start(bf16[256,256]{1,0:T(8,128)(2,1)S(1)} %get-tuple-element.31), channel_id=1, source_target_pairs={{0,4},{4,0},{8,12},{12,8},{1,5},{5,1},{9,13},{13,9},{2,6},{6,2},{1... | collective-permute-start | bytes 393224 | tf_op jit(solution)/shard_map/ppermute | solution.py:33
  70.5 1.5 %collective-permute-start.9 = (bf16[256,256]{1,0:T(8,128)(2,1)S(1)}, bf16[256,256]{1,0:T(8,128)(2,1)S(1)}, u32[]{:S(2)}, u32[]{:S(2)}) collective-permute-start(bf16[256,256]{1,0:T(8,128)(2,1)S(1)} %get-tuple-element.32), channel_id=1, source_target_pairs={{0,8},{4,12},{8,0},{12,4},{1,9},{5,13},{9,1},{13,5},{2,10},{6,14},... | collective-permute-start | bytes 393224 | tf_op jit(solution)/shard_map/ppermute | solution.py:33
  72.1 11.6 %shard_map.138 = (f32[256,256]{1,0:T(8,128)S(1)}, bf16[256,256]{1,0:T(8,128)(2,1)S(1)}, bf16[256,256]{1,0:T(8,128)(2,1)S(1)}, bf16[256,256]{1,0:T(8,128)(2,1)S(1)}) custom-call(s32[4]{0:T(128)S(1)} %copy-done.11, s32[1]{0:T(128)} %bitcast.place_ref, bf16[4,256,256]{2,1,0:T(8,128)(2,1)} %refs_0_.6, bf16[4,256,256]{2,1,0:T(8,128)(2,1)S(1)} %collective-permute-done.refs_1_, ...), custom_call_target="tpu_custom_call" | custom-call | flops 8589934592 | bytes 4194304 | tf_op jit(solution)/shard_map/pallas_call | solution.py:144
  84.4 1.3 collective-permute-start.13
  85.6 1.9 %collective-permute-start.26 = (bf16[256,256]{1,0:T(8,128)(2,1)S(1)}, bf16[256,256]{1,0:T(8,128)(2,1)S(1)}, u32[]{:S(2)}, u32[]{:S(2)}) collective-permute-start(bf16[256,256]{1,0:T(8,128)(2,1)S(1)} %shard_map.135.refs_6_.refs_4_), channel_id=1, source_target_pairs={{0,1},{1,0},{2,3},{3,2},{4,5},{5,4},{6,7},{7,6},{8,9},{9,8},{10,11... | collective-permute-start | bytes 393224 | tf_op jit(solution)/shard_map/ppermute | solution.py:33
  88.1 2.2 %collective-permute-done.12.refs_1_ = bf16[256,256]{1,0:T(8,128)(2,1)S(1)} collective-permute-done((bf16[256,256]{1,0:T(8,128)(2,1)S(1)}, bf16[256,256]{1,0:T(8,128)(2,1)S(1)}, u32[]{:S(2)}, u32[]{:S(2)}) %collective-permute-start.12) | collective-permute-done | bytes 131104 | tf_op jit(solution)/shard_map/ppermute | solution.py:33
  90.4 1.9 %collective-permute-start.28 = (bf16[256,256]{1,0:T(8,128)(2,1)S(1)}, bf16[256,256]{1,0:T(8,128)(2,1)S(1)}, u32[]{:S(2)}, u32[]{:S(2)}) collective-permute-start(bf16[256,256]{1,0:T(8,128)(2,1)S(1)} %collective-permute-done.27.refs_6_), channel_id=1, source_target_pairs={{0,1},{1,0},{2,3},{3,2},{4,5},{5,4},{6,7},{7,6},{8,9},{9,8},{10,11... | collective-permute-start | bytes 393224 | tf_op jit(solution)/shard_map/ppermute | solution.py:33
  92.2 1.4 %collective-permute-start.25 = (bf16[256,256]{1,0:T(8,128)(2,1)S(1)}, bf16[256,256]{1,0:T(8,128)(2,1)S(1)}, u32[]{:S(2)}, u32[]{:S(2)}) collective-permute-start(bf16[256,256]{1,0:T(8,128)(2,1)S(1)} %collective-permute-done.24.refs_2_), channel_id=1, source_target_pairs={{0,1},{1,0},{2,3},{3,2},{4,5},{5,4},{6,7},{7,6},{8,9},{9,8},{10,11... | collective-permute-start | bytes 393224 | tf_op jit(solution)/shard_map/ppermute | solution.py:33
  94.8 2.1 %collective-permute-start.21 = (bf16[256,256]{1,0:T(8,128)(2,1)S(1)}, bf16[256,256]{1,0:T(8,128)(2,1)S(1)}, u32[]{:S(2)}, u32[]{:S(2)}) collective-permute-start(bf16[256,256]{1,0:T(8,128)(2,1)S(1)} %shard_map.139.refs_6_), channel_id=1, source_target_pairs={{0,2},{1,3},{2,0},{3,1},{4,6},{5,7},{6,4},{7,5},{8,10},{9,11},{10,... | collective-permute-start | bytes 393224 | tf_op jit(solution)/shard_map/ppermute | solution.py:33
  97.6 1.9 %collective-permute-start.17 = (bf16[256,256]{1,0:T(8,128)(2,1)S(1)}, bf16[256,256]{1,0:T(8,128)(2,1)}, u32[]{:S(2)}, u32[]{:S(2)}) collective-permute-start(bf16[256,256]{1,0:T(8,128)(2,1)S(1)} %shard_map.137.refs_2_), channel_id=1, source_target_pairs={{0,1},{1,0},{2,3},{3,2},{4,5},{5,4},{6,7},{7,6},{8,9},{9,8},{10,11... | collective-permute-start | bytes 393224 | tf_op jit(solution)/shard_map/ppermute | solution.py:33
  99.5 2.8 %collective-permute-done.25.refs_3_ = bf16[256,256]{1,0:T(8,128)(2,1)S(1)} collective-permute-done((bf16[256,256]{1,0:T(8,128)(2,1)S(1)}, bf16[256,256]{1,0:T(8,128)(2,1)S(1)}, u32[]{:S(2)}, u32[]{:S(2)}) %collective-permute-start.25) | collective-permute-done | bytes 131104 | tf_op jit(solution)/shard_map/ppermute | solution.py:33
  103.0 4.1 %collective-permute-done.18.refs_4_ = bf16[256,256]{1,0:T(8,128)(2,1)S(1)} collective-permute-done((bf16[256,256]{1,0:T(8,128)(2,1)S(1)}, bf16[256,256]{1,0:T(8,128)(2,1)S(1)}, u32[]{:S(2)}, u32[]{:S(2)}) %collective-permute-start.18) | collective-permute-done | bytes 131104 | tf_op jit(solution)/shard_map/ppermute | solution.py:33
  107.0 2.4 %collective-permute-done.21.refs_8_ = bf16[256,256]{1,0:T(8,128)(2,1)S(1)} collective-permute-done((bf16[256,256]{1,0:T(8,128)(2,1)S(1)}, bf16[256,256]{1,0:T(8,128)(2,1)S(1)}, u32[]{:S(2)}, u32[]{:S(2)}) %collective-permute-start.21) | collective-permute-done | bytes 131104 | tf_op jit(solution)/shard_map/ppermute | solution.py:33
  111.1 1.2 collective-permute-done.20.refs_7_
  112.3 2.8 %collective-permute-done.19.refs_5_ = bf16[256,256]{1,0:T(8,128)(2,1)} collective-permute-done((bf16[256,256]{1,0:T(8,128)(2,1)S(1)}, bf16[256,256]{1,0:T(8,128)(2,1)}, u32[]{:S(2)}, u32[]{:S(2)}) %collective-permute-start.19) | collective-permute-done | bytes 131104 | tf_op jit(solution)/shard_map/ppermute | solution.py:33
  115.1 2.2 %collective-permute-done.22.refs_9_ = bf16[256,256]{1,0:T(8,128)(2,1)} collective-permute-done((bf16[256,256]{1,0:T(8,128)(2,1)S(1)}, bf16[256,256]{1,0:T(8,128)(2,1)}, u32[]{:S(2)}, u32[]{:S(2)}) %collective-permute-start.22) | collective-permute-done | bytes 131104 | tf_op jit(solution)/shard_map/ppermute | solution.py:33
  117.3 3.2 %shard_map.140 = (f32[512,256]{1,0:T(8,128)S(1)}, bf16[512,256]{1,0:T(8,128)(2,1)S(1)}, bf16[1024,256]{1,0:T(8,128)(2,1)S(1)}, bf16[1024,256]{1,0:T(8,128)(2,1)S(1)}) custom-call(s32[4]{0:T(128)S(1)} %copy-done.10, s32[1]{0:T(128)} %bitcast.place_ref, s32[1]{0:T(128)} %bitcast.4.col_ref, bf16[512,256]{1,0:T(8,128)(2,1)S(1)} %collective-permute-done.15.refs_0_, ...), custom_call_target="tpu_custom_call" | custom-call | tf_op jit(solution)/shard_map/pallas_call | solution.py:279
  120.5 1.5 %shard_map.141 = (f32[512,256]{1,0:T(8,128)S(1)}, bf16[512,256]{1,0:T(8,128)(2,1)S(1)}) custom-call(s32[4]{0:T(128)S(1)} %copy-done.10, s32[1]{0:T(128)} %bitcast.place_ref, s32[1]{0:T(128)} %bitcast.4.col_ref, bf16[512,256]{1,0:T(8,128)(2,1)S(1)} %copy-done.5, bf16[512,256]{1,0:T(8,128)(2,1)S(1)} %collective-permute-done.14.refs_1_, ...), custom_call_target="tpu_custom_call" | custom-call | tf_op jit(solution)/shard_map/pallas_call | solution.py:279
  123.8 7.2 %collective-permute-done.31.refs_2_ = bf16[512,256]{1,0:T(8,128)(2,1)S(1)} collective-permute-done((bf16[512,256]{1,0:T(8,128)(2,1)S(1)}, bf16[512,256]{1,0:T(8,128)(2,1)S(1)}, u32[]{:S(2)}, u32[]{:S(2)}) %collective-permute-start.31) | collective-permute-done | bytes 262176 | tf_op jit(solution)/shard_map/ppermute | solution.py:33
  131.0 1.9 %gate_cands.1 = bf16[512,256]{1,0:T(8,128)(2,1)} custom-call(s32[4]{0:T(128)S(1)} %copy-done.10, s32[1]{0:T(128)} %bitcast.place_ref, f32[512,256]{1,0:T(8,128)S(1)} %get-tuple-element.42.refs_0_, bf16[512,256]{1,0:T(8,128)(2,1)S(1)} %collective-permute-done.29.refs_1_, bf16[512,256]{1,0:T(8,128)(2,1)S(1)} %collective-permute-done.31.refs_2_, ...), custom_call_target="tpu_custom_call" | custom-call | tf_op jit(solution)/shard_map/gate_cands/pallas_call | solution.py:314
  (73 shorter events, 9.8 us)
Async XLA Ops:
  0.6 15.2 %collective-permute-start.2 = (bf16[4,256,256]{2,1,0:T(8,128)(2,1)}, bf16[4,256,256]{2,1,0:T(8,128)(2,1)S(1)}, u32[]{:S(2)}, u32[]{:S(2)}) collective-permute-start(bf16[4,256,256]{2,1,0:T(8,128)(2,1)} %refs_0_.6), channel_id=1, source_target_pairs={{0,8},{4,12},{8,0},{12,4},{1,9},{5,13},{9,1},{13,5},{2,10},{6,14},... | collective-permute-start | bytes 1572872 | tf_op jit(solution)/shard_map/ppermute | solution.py:33
  3.7 12.1 %collective-permute-start = (bf16[4,256,256]{2,1,0:T(8,128)(2,1)}, bf16[4,256,256]{2,1,0:T(8,128)(2,1)S(1)}, u32[]{:S(2)}, u32[]{:S(2)}) collective-permute-start(bf16[4,256,256]{2,1,0:T(8,128)(2,1)} %refs_0_.6), channel_id=1, source_target_pairs={{0,4},{4,0},{8,12},{12,8},{1,5},{5,1},{9,13},{13,9},{2,6},{6,2},{1... | collective-permute-start | bytes 1572872 | tf_op jit(solution)/shard_map/ppermute | solution.py:33
  15.8 14.0 %collective-permute-start.3 = (bf16[4,256,256]{2,1,0:T(8,128)(2,1)S(1)}, bf16[4,256,256]{2,1,0:T(8,128)(2,1)S(1)}, u32[]{:S(2)}, u32[]{:S(2)}) collective-permute-start(bf16[4,256,256]{2,1,0:T(8,128)(2,1)S(1)} %collective-permute-done.2.refs_0_.refs_2_), channel_id=1, source_target_pairs={{0,4},{4,0},{8,12},{12,8},{1,5},{5,1},{9,13},{13,9},{2,6},{6,2},{1... | collective-permute-start | bytes 1572872 | tf_op jit(solution)/shard_map/ppermute | solution.py:33
  29.8 15.2 %collective-permute-start.1 = (bf16[512,256]{1,0:T(8,128)(2,1)S(1)}, bf16[512,256]{1,0:T(8,128)(2,1)S(1)}, u32[]{:S(2)}, u32[]{:S(2)}) collective-permute-start(bf16[512,256]{1,0:T(8,128)(2,1)S(1)} %get-tuple-element.25), channel_id=1, source_target_pairs={{0,4},{4,0},{8,12},{12,8},{1,5},{5,1},{9,13},{13,9},{2,6},{6,2},{1... | collective-permute-start | bytes 786440 | tf_op jit(solution)/shard_map/ppermute | solution.py:33
  41.4 6.4 %collective-permute-start.6 = (bf16[256,256]{1,0:T(8,128)(2,1)S(1)}, bf16[256,256]{1,0:T(8,128)(2,1)S(1)}, u32[]{:S(2)}, u32[]{:S(2)}) collective-permute-start(bf16[256,256]{1,0:T(8,128)(2,1)S(1)} %get-tuple-element.28.refs_7_), channel_id=1, source_target_pairs={{0,8},{4,12},{8,0},{12,4},{1,9},{5,13},{9,1},{13,5},{2,10},{6,14},... | collective-permute-start | bytes 393224 | tf_op jit(solution)/shard_map/ppermute | solution.py:33
  41.5 6.4 %collective-permute-start.7 = (bf16[256,256]{1,0:T(8,128)(2,1)S(1)}, bf16[256,256]{1,0:T(8,128)(2,1)S(1)}, u32[]{:S(2)}, u32[]{:S(2)}) collective-permute-start(bf16[256,256]{1,0:T(8,128)(2,1)S(1)} %get-tuple-element.29), channel_id=1, source_target_pairs={{0,12},{4,8},{8,4},{12,0},{1,13},{5,9},{9,5},{13,1},{2,14},{6,10},... | collective-permute-start | bytes 393224 | tf_op jit(solution)/shard_map/ppermute | solution.py:33
  41.6 11.9 %collective-permute-start.4 = (bf16[256,256]{1,0:T(8,128)(2,1)S(1)}, bf16[256,256]{1,0:T(8,128)(2,1)S(1)}, u32[]{:S(2)}, u32[]{:S(2)}) collective-permute-start(bf16[256,256]{1,0:T(8,128)(2,1)S(1)} %get-tuple-element.26.refs_4_), channel_id=1, source_target_pairs={{0,8},{4,12},{8,0},{12,4},{1,9},{5,13},{9,1},{13,5},{2,10},{6,14},... | collective-permute-start | bytes 393224 | tf_op jit(solution)/shard_map/ppermute | solution.py:33
  43.5 10.0 %collective-permute-start.5 = (bf16[256,256]{1,0:T(8,128)(2,1)S(1)}, bf16[256,256]{1,0:T(8,128)(2,1)S(1)}, u32[]{:S(2)}, u32[]{:S(2)}) collective-permute-start(bf16[256,256]{1,0:T(8,128)(2,1)S(1)} %get-tuple-element.27), channel_id=1, source_target_pairs={{0,12},{4,8},{8,4},{12,0},{1,13},{5,9},{9,5},{13,1},{2,14},{6,10},... | collective-permute-start | bytes 393224 | tf_op jit(solution)/shard_map/ppermute | solution.py:33
  45.0 25.5 %collective-permute-start.15 = (bf16[512,256]{1,0:T(8,128)(2,1)S(1)}, bf16[512,256]{1,0:T(8,128)(2,1)S(1)}, u32[]{:S(2)}, u32[]{:S(2)}) collective-permute-start(bf16[512,256]{1,0:T(8,128)(2,1)S(1)} %copy-done.5), channel_id=1, source_target_pairs={{0,8},{4,12},{8,0},{12,4},{1,9},{5,13},{9,1},{13,5},{2,10},{6,14},... | collective-permute-start | bytes 786440 | tf_op jit(solution)/shard_map/ppermute | solution.py:33
  48.1 35.5 %collective-permute-start.27 = (bf16[256,256]{1,0:T(8,128)(2,1)S(1)}, bf16[256,256]{1,0:T(8,128)(2,1)S(1)}, u32[]{:S(2)}, u32[]{:S(2)}) collective-permute-start(bf16[256,256]{1,0:T(8,128)(2,1)S(1)} %shard_map.135.refs_6_.refs_4_), channel_id=1, source_target_pairs={{0,2},{1,3},{2,0},{3,1},{4,6},{5,7},{6,4},{7,5},{8,10},{9,11},{10,... | collective-permute-start | bytes 393224 | tf_op jit(solution)/shard_map/ppermute | solution.py:33
  53.8 30.2 %collective-permute-start.24 = (bf16[256,256]{1,0:T(8,128)(2,1)S(1)}, bf16[256,256]{1,0:T(8,128)(2,1)S(1)}, u32[]{:S(2)}, u32[]{:S(2)}) collective-permute-start(bf16[256,256]{1,0:T(8,128)(2,1)S(1)} %shard_map.133.refs_6_.refs_0_), channel_id=1, source_target_pairs={{0,2},{1,3},{2,0},{3,1},{4,6},{5,7},{6,4},{7,5},{8,10},{9,11},{10,... | collective-permute-start | bytes 393224 | tf_op jit(solution)/shard_map/ppermute | solution.py:33
  68.0 16.4 %collective-permute-start.10 = (bf16[256,256]{1,0:T(8,128)(2,1)S(1)}, bf16[256,256]{1,0:T(8,128)(2,1)S(1)}, u32[]{:S(2)}, u32[]{:S(2)}) collective-permute-start(bf16[256,256]{1,0:T(8,128)(2,1)S(1)} %get-tuple-element.33), channel_id=1, source_target_pairs={{0,12},{4,8},{8,4},{12,0},{1,13},{5,9},{9,5},{13,1},{2,14},{6,10},... | collective-permute-start | bytes 393224 | tf_op jit(solution)/shard_map/ppermute | solution.py:33
  68.9 16.8 %collective-permute-start.8 = (bf16[256,256]{1,0:T(8,128)(2,1)S(1)}, bf16[256,256]{1,0:T(8,128)(2,1)S(1)}, u32[]{:S(2)}, u32[]{:S(2)}) collective-permute-start(bf16[256,256]{1,0:T(8,128)(2,1)S(1)} %get-tuple-element.31), channel_id=1, source_target_pairs={{0,4},{4,0},{8,12},{12,8},{1,5},{5,1},{9,13},{13,9},{2,6},{6,2},{1... | collective-permute-start | bytes 393224 | tf_op jit(solution)/shard_map/ppermute | solution.py:33
  70.5 17.0 %collective-permute-start.9 = (bf16[256,256]{1,0:T(8,128)(2,1)S(1)}, bf16[256,256]{1,0:T(8,128)(2,1)S(1)}, u32[]{:S(2)}, u32[]{:S(2)}) collective-permute-start(bf16[256,256]{1,0:T(8,128)(2,1)S(1)} %get-tuple-element.32), channel_id=1, source_target_pairs={{0,8},{4,12},{8,0},{12,4},{1,9},{5,13},{9,1},{13,5},{2,10},{6,14},... | collective-permute-start | bytes 393224 | tf_op jit(solution)/shard_map/ppermute | solution.py:33
  83.7 4.2 %collective-permute-start.11 = (bf16[256,256]{1,0:T(8,128)(2,1)S(1)}, bf16[256,256]{1,0:T(8,128)(2,1)S(1)}, u32[]{:S(2)}, u32[]{:S(2)}) collective-permute-start(bf16[256,256]{1,0:T(8,128)(2,1)S(1)} %get-tuple-element.35), channel_id=1, source_target_pairs={{0,4},{4,0},{8,12},{12,8},{1,5},{5,1},{9,13},{13,9},{2,6},{6,2},{1... | collective-permute-start | bytes 393224 | tf_op jit(solution)/shard_map/ppermute | solution.py:33
  84.0 6.4 %collective-permute-start.12 = (bf16[256,256]{1,0:T(8,128)(2,1)S(1)}, bf16[256,256]{1,0:T(8,128)(2,1)S(1)}, u32[]{:S(2)}, u32[]{:S(2)}) collective-permute-start(bf16[256,256]{1,0:T(8,128)(2,1)S(1)} %get-tuple-element.36), channel_id=1, source_target_pairs={{0,8},{4,12},{8,0},{12,4},{1,9},{5,13},{9,1},{13,5},{2,10},{6,14},... | collective-permute-start | bytes 393224 | tf_op jit(solution)/shard_map/ppermute | solution.py:33
  84.4 7.9 %collective-permute-start.13 = (bf16[256,256]{1,0:T(8,128)(2,1)S(1)}, bf16[256,256]{1,0:T(8,128)(2,1)S(1)}, u32[]{:S(2)}, u32[]{:S(2)}) collective-permute-start(bf16[256,256]{1,0:T(8,128)(2,1)S(1)} %get-tuple-element.37), channel_id=1, source_target_pairs={{0,12},{4,8},{8,4},{12,0},{1,13},{5,9},{9,5},{13,1},{2,14},{6,10},... | collective-permute-start | bytes 393224 | tf_op jit(solution)/shard_map/ppermute | solution.py:33
  85.6 8.3 %collective-permute-start.26 = (bf16[256,256]{1,0:T(8,128)(2,1)S(1)}, bf16[256,256]{1,0:T(8,128)(2,1)S(1)}, u32[]{:S(2)}, u32[]{:S(2)}) collective-permute-start(bf16[256,256]{1,0:T(8,128)(2,1)S(1)} %shard_map.135.refs_6_.refs_4_), channel_id=1, source_target_pairs={{0,1},{1,0},{2,3},{3,2},{4,5},{5,4},{6,7},{7,6},{8,9},{9,8},{10,11... | collective-permute-start | bytes 393224 | tf_op jit(solution)/shard_map/ppermute | solution.py:33
  87.5 7.3 %collective-permute-start.23 = (bf16[256,256]{1,0:T(8,128)(2,1)S(1)}, bf16[256,256]{1,0:T(8,128)(2,1)S(1)}, u32[]{:S(2)}, u32[]{:S(2)}) collective-permute-start(bf16[256,256]{1,0:T(8,128)(2,1)S(1)} %shard_map.133.refs_6_.refs_0_), channel_id=1, source_target_pairs={{0,1},{1,0},{2,3},{3,2},{4,5},{5,4},{6,7},{7,6},{8,9},{9,8},{10,11... | collective-permute-start | bytes 393224 | tf_op jit(solution)/shard_map/ppermute | solution.py:33
  87.9 23.1 %collective-permute-start.16 = (bf16[512,256]{1,0:T(8,128)(2,1)S(1)}, bf16[512,256]{1,0:T(8,128)(2,1)S(1)}, u32[]{:S(2)}, u32[]{:S(2)}) collective-permute-start(bf16[512,256]{1,0:T(8,128)(2,1)S(1)} %collective-permute-done.15.refs_0_), channel_id=1, source_target_pairs={{0,4},{4,0},{8,12},{12,8},{1,5},{5,1},{9,13},{13,9},{2,6},{6,2},{1... | collective-permute-start | bytes 786440 | tf_op jit(solution)/shard_map/ppermute | solution.py:33
  90.4 7.3 %collective-permute-start.28 = (bf16[256,256]{1,0:T(8,128)(2,1)S(1)}, bf16[256,256]{1,0:T(8,128)(2,1)S(1)}, u32[]{:S(2)}, u32[]{:S(2)}) collective-permute-start(bf16[256,256]{1,0:T(8,128)(2,1)S(1)} %collective-permute-done.27.refs_6_), channel_id=1, source_target_pairs={{0,1},{1,0},{2,3},{3,2},{4,5},{5,4},{6,7},{7,6},{8,9},{9,8},{10,11... | collective-permute-start | bytes 393224 | tf_op jit(solution)/shard_map/ppermute | solution.py:33
  92.2 10.1 %collective-permute-start.25 = (bf16[256,256]{1,0:T(8,128)(2,1)S(1)}, bf16[256,256]{1,0:T(8,128)(2,1)S(1)}, u32[]{:S(2)}, u32[]{:S(2)}) collective-permute-start(bf16[256,256]{1,0:T(8,128)(2,1)S(1)} %collective-permute-done.24.refs_2_), channel_id=1, source_target_pairs={{0,1},{1,0},{2,3},{3,2},{4,5},{5,4},{6,7},{7,6},{8,9},{9,8},{10,11... | collective-permute-start | bytes 393224 | tf_op jit(solution)/shard_map/ppermute | solution.py:33
  93.9 13.1 %collective-permute-start.18 = (bf16[256,256]{1,0:T(8,128)(2,1)S(1)}, bf16[256,256]{1,0:T(8,128)(2,1)S(1)}, u32[]{:S(2)}, u32[]{:S(2)}) collective-permute-start(bf16[256,256]{1,0:T(8,128)(2,1)S(1)} %shard_map.137.refs_2_), channel_id=1, source_target_pairs={{0,2},{1,3},{2,0},{3,1},{4,6},{5,7},{6,4},{7,5},{8,10},{9,11},{10,... | collective-permute-start | bytes 393224 | tf_op jit(solution)/shard_map/ppermute | solution.py:33
  94.8 14.6 %collective-permute-start.21 = (bf16[256,256]{1,0:T(8,128)(2,1)S(1)}, bf16[256,256]{1,0:T(8,128)(2,1)S(1)}, u32[]{:S(2)}, u32[]{:S(2)}) collective-permute-start(bf16[256,256]{1,0:T(8,128)(2,1)S(1)} %shard_map.139.refs_6_), channel_id=1, source_target_pairs={{0,2},{1,3},{2,0},{3,1},{4,6},{5,7},{6,4},{7,5},{8,10},{9,11},{10,... | collective-permute-start | bytes 393224 | tf_op jit(solution)/shard_map/ppermute | solution.py:33
  97.6 13.5 %collective-permute-start.17 = (bf16[256,256]{1,0:T(8,128)(2,1)S(1)}, bf16[256,256]{1,0:T(8,128)(2,1)}, u32[]{:S(2)}, u32[]{:S(2)}) collective-permute-start(bf16[256,256]{1,0:T(8,128)(2,1)S(1)} %shard_map.137.refs_2_), channel_id=1, source_target_pairs={{0,1},{1,0},{2,3},{3,2},{4,5},{5,4},{6,7},{7,6},{8,9},{9,8},{10,11... | collective-permute-start | bytes 393224 | tf_op jit(solution)/shard_map/ppermute | solution.py:33
  103.0 9.4 %collective-permute-start.20 = (bf16[256,256]{1,0:T(8,128)(2,1)S(1)}, bf16[256,256]{1,0:T(8,128)(2,1)}, u32[]{:S(2)}, u32[]{:S(2)}) collective-permute-start(bf16[256,256]{1,0:T(8,128)(2,1)S(1)} %shard_map.139.refs_6_), channel_id=1, source_target_pairs={{0,1},{1,0},{2,3},{3,2},{4,5},{5,4},{6,7},{7,6},{8,9},{9,8},{10,11... | collective-permute-start | bytes 393224 | tf_op jit(solution)/shard_map/ppermute | solution.py:33
  107.0 8.1 %collective-permute-start.19 = (bf16[256,256]{1,0:T(8,128)(2,1)S(1)}, bf16[256,256]{1,0:T(8,128)(2,1)}, u32[]{:S(2)}, u32[]{:S(2)}) collective-permute-start(bf16[256,256]{1,0:T(8,128)(2,1)S(1)} %collective-permute-done.18.refs_4_), channel_id=1, source_target_pairs={{0,1},{1,0},{2,3},{3,2},{4,5},{5,4},{6,7},{7,6},{8,9},{9,8},{10,11... | collective-permute-start | bytes 393224 | tf_op jit(solution)/shard_map/ppermute | solution.py:33
  109.4 7.9 %collective-permute-start.22 = (bf16[256,256]{1,0:T(8,128)(2,1)S(1)}, bf16[256,256]{1,0:T(8,128)(2,1)}, u32[]{:S(2)}, u32[]{:S(2)}) collective-permute-start(bf16[256,256]{1,0:T(8,128)(2,1)S(1)} %collective-permute-done.21.refs_8_), channel_id=1, source_target_pairs={{0,1},{1,0},{2,3},{3,2},{4,5},{5,4},{6,7},{7,6},{8,9},{9,8},{10,11... | collective-permute-start | bytes 393224 | tf_op jit(solution)/shard_map/ppermute | solution.py:33
  111.0 9.5 %collective-permute-start.14 = (bf16[512,256]{1,0:T(8,128)(2,1)S(1)}, bf16[512,256]{1,0:T(8,128)(2,1)S(1)}, u32[]{:S(2)}, u32[]{:S(2)}) collective-permute-start(bf16[512,256]{1,0:T(8,128)(2,1)S(1)} %copy-done.5), channel_id=1, source_target_pairs={{0,4},{4,0},{8,12},{12,8},{1,5},{5,1},{9,13},{13,9},{2,6},{6,2},{1... | collective-permute-start | bytes 786440 | tf_op jit(solution)/shard_map/ppermute | solution.py:33
  120.4 2.2 %collective-permute-start.30 = (bf16[512,256]{1,0:T(8,128)(2,1)S(1)}, bf16[512,256]{1,0:T(8,128)(2,1)S(1)}, u32[]{:S(2)}, u32[]{:S(2)}) collective-permute-start(bf16[512,256]{1,0:T(8,128)(2,1)S(1)} %get-tuple-element.45), channel_id=1, source_target_pairs={{0,4},{4,0},{8,12},{12,8},{1,5},{5,1},{9,13},{13,9},{2,6},{6,2},{1... | collective-permute-start | bytes 786440 | tf_op jit(solution)/shard_map/ppermute | solution.py:33
  122.0 1.7 %collective-permute-start.29 = (bf16[512,256]{1,0:T(8,128)(2,1)S(1)}, bf16[512,256]{1,0:T(8,128)(2,1)S(1)}, u32[]{:S(2)}, u32[]{:S(2)}) collective-permute-start(bf16[512,256]{1,0:T(8,128)(2,1)S(1)} %get-tuple-element.43), channel_id=1, source_target_pairs={{0,4},{4,0},{8,12},{12,8},{1,5},{5,1},{9,13},{13,9},{2,6},{6,2},{1... | collective-permute-start | bytes 786440 | tf_op jit(solution)/shard_map/ppermute | solution.py:33
  122.7 8.3 %collective-permute-start.31 = (bf16[512,256]{1,0:T(8,128)(2,1)S(1)}, bf16[512,256]{1,0:T(8,128)(2,1)S(1)}, u32[]{:S(2)}, u32[]{:S(2)}) collective-permute-start(bf16[512,256]{1,0:T(8,128)(2,1)S(1)} %add_convert_fusion), channel_id=1, source_target_pairs={{0,8},{4,12},{8,0},{12,4},{1,9},{5,13},{9,1},{13,5},{2,10},{6,14},... | collective-permute-start | bytes 786440 | tf_op jit(solution)/shard_map/ppermute | solution.py:33
  (13 other events, 277.6 us)

commit v2 on v1

--- a/solution.py
+++ b/solution.py
@@ -14,6 +14,7 @@
 BF16 = jnp.bfloat16
 F32 = jnp.float32
 ANY = pl.BlockSpec(memory_space=pl.ANY)
+INSIDE = pl.BlockSpec(memory_space=pltpu.VMEM)
 SMALL = pltpu.CompilerParams(vmem_limit_bytes=12 << 20)
 LARGE = pltpu.CompilerParams(vmem_limit_bytes=20 << 20)
 
@@ -101,58 +102,53 @@
     )(hist_len, place, *queries, keys, values)
 
 
-def attend(first_user, counts, half_rows, start, together, queries, own_first, hist_len, place, keys, values, after):
+def attend(user, heads, queries, own_first, hist_len, place, keys, values, after, earlier=(), looped=False):
     n = len(queries)
-    width = queries[0].shape[2]
+    _, rows, width = queries[0].shape
     hist_rows = keys.shape[1]
-    users = len(counts)
-    take = max(counts)
-    total = sum(counts) * half_rows
-    n_after = len(after)
-    block = width if together else HEAD
+    n_after = len(after) + len(earlier)
+    block = HEAD if looped else len(heads) * HEAD
+    at = heads[0] * HEAD // block
 
     def kern(len_ref, place_ref, *refs):
         q_refs, k_ref, v_ref = refs[:n], refs[n], refs[n + 1]
         o_refs = refs[n + 2 + n_after :]
-        for g in range(users):
-            user = first_user + g
-            rows = counts[g] * half_rows
-            at = sum(counts[:g]) * half_rows
-            left = len_ref[user] - place_ref[0] * hist_rows
-
-            @pl.when(left > 0)
-            def _(g=g, user=user, rows=rows, at=at, left=left):
-                for h in range(block // HEAD):
-                    cols = slice(h * HEAD, (h + 1) * HEAD)
-                    head = cols if together else pl.ds(pl.multiple_of(pl.program_id(0) * HEAD, HEAD), HEAD)
-                    q = join([r[g, :rows, cols] for r in q_refs])
-                    k = (lambda a, b, head=head: k_ref[user, a:b, head], hist_rows)
-                    v = (lambda a, b, head=head: v_ref[user, a:b, head], hist_rows)
-                    o = weigh(q, k, v, left)
-                    for m, o_ref in enumerate(o_refs):
-                        o_ref[at : at + rows, cols] = o[m * rows : (m + 1) * rows].astype(o_ref.dtype)
-
-            @pl.when(left <= 0)
-            def _(rows=rows, at=at):
-                for o_ref in o_refs:
-                    o_ref[at : at + rows, :] = jnp.zeros((rows, block), o_ref.dtype)
-
-    assert first_user % users == 0
-    piece = pl.BlockSpec((users, take * half_rows, block), lambda h, *_: (first_user // users, start, h))
+        left = len_ref[user] - place_ref[0] * hist_rows
+
+        @pl.when(left > 0)
+        def _():
+            for m in range(block // HEAD):
+                cols = slice(m * HEAD, (m + 1) * HEAD)
+                head = slice((heads[0] + m) * HEAD, (heads[0] + m + 1) * HEAD)
+                if looped:
+                    head = pl.ds(pl.multiple_of((heads[0] + pl.program_id(0)) * HEAD, HEAD), HEAD)
+                k = (lambda a, b, head=head: k_ref[user, a:b, head], hist_rows)
+                v = (lambda a, b, head=head: v_ref[user, a:b, head], hist_rows)
+                o = weigh(join([r[0, :, cols] for r in q_refs]), k, v, left)
+                for i, o_ref in enumerate(o_refs):
+                    o_ref[:, cols] = o[i * rows : (i + 1) * rows].astype(o_ref.dtype)
+
+        @pl.when(left <= 0)
+        def _():
+            for o_ref in o_refs:
+                o_ref[...] = jnp.zeros(o_ref.shape, o_ref.dtype)
+
+    piece = pl.BlockSpec((1, rows, block), lambda g, *_: (user, 0, at + g))
     resident = pl.BlockSpec(memory_space=pltpu.VMEM)
     kinds = [F32 if own_first and i == 0 else BF16 for i in range(n)]
     return pl.pallas_call(
         kern,
         grid_spec=pltpu.PrefetchScalarGridSpec(
             num_scalar_prefetch=2,
-            grid=(width // block,),
+            grid=(len(heads) * HEAD // block,),
             in_specs=[piece] * n + [resident, resident] + [ANY] * n_after,
-            out_specs=[pl.BlockSpec((total, block), lambda h, *_: (0, h))] * n,
-        ),
-        out_shape=[jax.ShapeDtypeStruct((total, width), kind) for kind in kinds],
-        cost_estimate=attend_cost(n * total, hist_rows, width, 4 * users * hist_rows * width),
+            out_specs=[pl.BlockSpec((rows, block), lambda g, *_: (0, at + g))] * n,
+        ),
+        out_shape=[jax.ShapeDtypeStruct((rows, width), kind) for kind in kinds],
+        input_output_aliases={4 + n + i: i for i in range(len(earlier))},
+        cost_estimate=attend_cost(n * rows, hist_rows, len(heads) * HEAD, 4 * hist_rows * len(heads) * HEAD),
         compiler_params=LARGE,
-    )(hist_len, place, *queries, keys, values, *after)
+    )(hist_len, place, *queries, keys, values, *earlier, *after)
 
 
 def gate_events(own, others, rows, gate_at, gain, gate):
@@ -224,7 +220,7 @@
         grid_spec=pltpu.PrefetchScalarGridSpec(
             num_scalar_prefetch=1,
             grid=(1,),
-            in_specs=[full(e.shape) for e in flat] + [full(key_weight.shape)] * 2,
+            in_specs=[INSIDE] * (len(flat) + 2),
             out_specs=[full(shape)] * 2,
         ),
         out_shape=[jax.ShapeDtypeStruct(shape, BF16)] * 2,
@@ -281,7 +277,7 @@
         grid_spec=pltpu.PrefetchScalarGridSpec(
             num_scalar_prefetch=3,
             grid=(1,),
-            in_specs=[full(x.shape) for x in operands],
+            in_specs=[INSIDE] * len(operands),
             out_specs=[full(x.shape) for x in shapes],
         ),
         out_shape=shapes,
@@ -316,7 +312,7 @@
         grid_spec=pltpu.PrefetchScalarGridSpec(
             num_scalar_prefetch=2,
             grid=(1,),
-            in_specs=[block] * n + [full((1, width)), block],
+            in_specs=[INSIDE] * (n + 2),
             out_specs=block,
         ),
         out_shape=jax.ShapeDtypeStruct((rows, width), BF16),
@@ -374,15 +370,28 @@
 
         own01, *near01 = attend_near(2, queries[:2], hist_len, place, *in_hbm)
         got01 = exchange(near01, 1)
-        far0 = attend(0, (2,), half, 0, True, queries[2:], False, *hist, (own01,))
-        far1 = attend(1, (2,), half, 0, True, queries[2:], False, *hist, (far0[0],))
+        heads = range(width // HEAD)
+        most = range((len(heads) + 1) // 2)
+        rest = range(len(most), len(heads))
+
+        def in_two(user, before, between):
+            sums = attend(user, most, queries, True, *hist, before)
+            middle = between(sums[0])
+            if len(rest):
+                sums = attend(user, rest, queries, True, *hist, (middle,), sums)
+            return sums, middle
+
+        far0 = attend(0, heads, queries[2:], False, *hist, (own01,), looped=True)
+        far1 = attend(1, heads, queries[2:], False, *hist, (far0[0],), looped=True)
         got0, got1 = exchange(far0, 2), exchange(far1, 2)
+        near1 = [(x, rows) for x in got01]
         gated0 = gate_chunk((own01, 0), [(x, 0) for x in got01 + got0], 2, 0)
-        out2 = attend(2, (2,), half, 0, False, queries, True, *hist, (gated0, far1[0]))
-        gated1 = gate_chunk((own01, rows), [(x, rows) for x in got01] + [(x, 0) for x in got1], 2, 2)
-        out3 = attend(3, (2,), half, 0, False, queries, True, *hist, (gated1, out2[0]))
-        got2, got3 = exchange(out2[1:], 1), exchange(out3[1:], 1)
-        gated2 = gate_chunk((out2[0], 0), [(x, 0) for x in got2], 2, 4)
+        out2, gated1 = in_two(
+            2, (gated0, far1[0]), lambda _: gate_chunk((own01, rows), near1 + [(x, 0) for x in got1], 2, 2)
+        )
+        got2 = exchange(out2[1:], 1)
+        out3, gated2 = in_two(3, (gated1, out2[0]), lambda _: gate_chunk((out2[0], 0), [(x, 0) for x in got2], 2, 4))
+        got3 = exchange(out3[1:], 1)
         gated3 = gate_chunk((out3[0], 0), [(x, 0) for x in got3], 2, 6)
         gated = [gated0, gated1, gated2, gated3]
         all_columns = [gather_pieces(g, "hd", n_hd) for g in gated]

time: 133 us -> 137 us (1.030)
  Pallas kernels: 56 us -> 59.6 us
  local copies, waits for them, and re-layouts: 2.26 us -> 0.71 us
    pallas_call x4 -> x6, Pallas kernels: 34.5 us -> 38 us  [attend(): pl.pallas_call(kern, grid_spec=pltpu.PrefetchScalarGridSpec(num_scalar_pr...]
    unnamed x26 -> x22, local copies, waits for them, and re-layouts: 2.26 us -> 0.71 us
  transfers between devices with their start and end apart: 32 -> 32, of which waited for: 14 -> 13; matrix products, arithmetic and copies ran while one was open for 1% -> 1% of each run, Pallas kernels for 41% -> 42%
where the time goes in v2:
time: 137 us
  Pallas kernels  59.6 us (44%)
  waiting for transfers between devices  44.2 us (32%)
  starting transfers between devices  30.3 us (22%)
    ppermute x32, waiting for transfers between devices, swap(): return lax.ppermute(x, axis, [(i, i ^ j) for i in range(size)])  44.2 us
    pallas_call x6, Pallas kernels, attend(): pl.pallas_call(kern, grid_spec=pltpu.PrefetchScalarGridSpec(num_scalar_pr...  38 us
    ppermute x32, starting transfers between devices, swap(): return lax.ppermute(x, axis, [(i, i ^ j) for i in range(size)])  30.3 us
    pallas_call x1, Pallas kernels, attend_near(): pl.pallas_call(kern, grid_spec=pltpu.PrefetchScalarGridSpec(num_scalar_pr...  13.3 us
    pallas_call x2, Pallas kernels, cand_sums(): pl.pallas_call(kern, grid_spec=pltpu.PrefetchScalarGridSpec(num_scalar_pr...  4.73 us
  transfers between devices with their start and end apart: 32, of which 13 were waited for; matrix products, arithmetic and copies ran while one was open for 1% of the time, Pallas kernels for 42%

profile of v2, /device:TPU:0, one launch (start us, length us, event | category | flops | bytes accessed | tf_op | source)
XLA Modules:
  0.0 136.6 jit_solution(9304037977390918228)
XLA Ops:
  0.6 3.1 %collective-permute-start.2 = (bf16[4,256,256]{2,1,0:T(8,128)(2,1)}, bf16[4,256,256]{2,1,0:T(8,128)(2,1)S(1)}, u32[]{:S(2)}, u32[]{:S(2)}) collective-permute-start(bf16[4,256,256]{2,1,0:T(8,128)(2,1)} %refs_0_.10), channel_id=1, source_target_pairs={{0,8},{4,12},{8,0},{12,4},{1,9},{5,13},{9,1},{13,5},{2,10},{6,14},... | collective-permute-start | bytes 1572872 | tf_op jit(solution)/shard_map/ppermute | solution.py:34
  3.7 12.1 %collective-permute-done.2.refs_0_.refs_2_ = bf16[4,256,256]{2,1,0:T(8,128)(2,1)S(1)} collective-permute-done((bf16[4,256,256]{2,1,0:T(8,128)(2,1)}, bf16[4,256,256]{2,1,0:T(8,128)(2,1)S(1)}, u32[]{:S(2)}, u32[]{:S(2)}) %collective-permute-start.2) | collective-permute-done | bytes 524320 | tf_op jit(solution)/shard_map/ppermute | solution.py:34
  16.5 13.3 %shard_map.131 = (f32[512,256]{1,0:T(8,128)S(1)}, bf16[512,256]{1,0:T(8,128)(2,1)S(1)}) custom-call(s32[4]{0:T(128)S(1)} %copy-done.7, s32[1]{0:T(128)} %bitcast.place_ref, bf16[4,256,256]{2,1,0:T(8,128)(2,1)} %refs_0_.10, bf16[4,256,256]{2,1,0:T(8,128)(2,1)S(1)} %collective-permute-done.refs_1_, bf16[4,4096,256]{2,1,0:T(8,128)(2,1)} %refs_4_.8, ...), custom_call_target="tpu_custom_call" | custom-call | flops 8589934592 | bytes 8388608 | tf_op jit(solution)/shard_map/pallas_call | solution.py:91
  29.9 6.1 %shard_map.132 = (bf16[256,256]{1,0:T(8,128)(2,1)S(1)}, bf16[256,256]{1,0:T(8,128)(2,1)S(1)}) custom-call(s32[4]{0:T(128)S(1)} %copy-done.7, s32[1]{0:T(128)} %bitcast.place_ref, bf16[4,256,256]{2,1,0:T(8,128)(2,1)S(1)} %collective-permute-done.2.refs_0_.refs_2_, bf16[4,256,256]{2,1,0:T(8,128)(2,1)S(1)} %collective-permute-done.3.refs_1_.refs_3_, ...), custom_call_target="tpu_custom_call" | custom-call | flops 4294967296 | bytes 4194304 | tf_op jit(solution)/shard_map/pallas_call | solution.py:139
  36.1 6.1 %shard_map.134 = (bf16[256,256]{1,0:T(8,128)(2,1)S(1)}, bf16[256,256]{1,0:T(8,128)(2,1)S(1)}) custom-call(s32[4]{0:T(128)S(1)} %copy-done.7, s32[1]{0:T(128)} %bitcast.place_ref, bf16[4,256,256]{2,1,0:T(8,128)(2,1)S(1)} %collective-permute-done.2.refs_0_.refs_2_, bf16[4,256,256]{2,1,0:T(8,128)(2,1)S(1)} %collective-permute-done.3.refs_1_.refs_3_, ...), custom_call_target="tpu_custom_call" | custom-call | flops 4294967296 | bytes 4194304 | tf_op jit(solution)/shard_map/pallas_call | solution.py:139
  42.4 1.9 %collective-permute-start.4 = (bf16[256,256]{1,0:T(8,128)(2,1)S(1)}, bf16[256,256]{1,0:T(8,128)(2,1)S(1)}, u32[]{:S(2)}, u32[]{:S(2)}) collective-permute-start(bf16[256,256]{1,0:T(8,128)(2,1)S(1)} %get-tuple-element.34.refs_4_), channel_id=1, source_target_pairs={{0,8},{4,12},{8,0},{12,4},{1,9},{5,13},{9,1},{13,5},{2,10},{6,14},... | collective-permute-start | bytes 393224 | tf_op jit(solution)/shard_map/ppermute | solution.py:34
  46.1 2.6 %collective-permute-done.6.refs_1_ = bf16[256,256]{1,0:T(8,128)(2,1)S(1)} collective-permute-done((bf16[256,256]{1,0:T(8,128)(2,1)S(1)}, bf16[256,256]{1,0:T(8,128)(2,1)S(1)}, u32[]{:S(2)}, u32[]{:S(2)}) %collective-permute-start.6) | collective-permute-done | bytes 131104 | tf_op jit(solution)/shard_map/ppermute | solution.py:34
  48.9 2.9 %collective-permute-start.27 = (bf16[256,256]{1,0:T(8,128)(2,1)S(1)}, bf16[256,256]{1,0:T(8,128)(2,1)S(1)}, u32[]{:S(2)}, u32[]{:S(2)}) collective-permute-start(bf16[256,256]{1,0:T(8,128)(2,1)S(1)} %shard_map.135.refs_10_.refs_6_.refs_4_), channel_id=1, source_target_pairs={{0,2},{1,3},{2,0},{3,1},{4,6},{5,7},{6,4},{7,5},{8,10},{9,11},{10,... | collective-permute-start | bytes 393224 | tf_op jit(solution)/shard_map/ppermute | solution.py:34
  51.8 2.5 %collective-permute-done.4.refs_1_ = bf16[256,256]{1,0:T(8,128)(2,1)S(1)} collective-permute-done((bf16[256,256]{1,0:T(8,128)(2,1)S(1)}, bf16[256,256]{1,0:T(8,128)(2,1)S(1)}, u32[]{:S(2)}, u32[]{:S(2)}) %collective-permute-start.4) | collective-permute-done | bytes 131104 | tf_op jit(solution)/shard_map/ppermute | solution.py:34
  54.5 6.4 %shard_map.136 = (f32[256,256]{1,0:T(8,128)S(1)}, bf16[256,256]{1,0:T(8,128)(2,1)S(1)}, bf16[256,256]{1,0:T(8,128)(2,1)S(1)}, bf16[256,256]{1,0:T(8,128)(2,1)S(1)}) custom-call(s32[4]{0:T(128)S(1)} %copy-done.7, s32[1]{0:T(128)} %bitcast.place_ref, bf16[4,256,256]{2,1,0:T(8,128)(2,1)} %refs_0_.10, bf16[4,256,256]{2,1,0:T(8,128)(2,1)S(1)} %collective-permute-done.refs_1_, ...), custom_call_target="tpu_custom_call" | custom-call | flops 4294967296 | bytes 2097152 | tf_op jit(solution)/shard_map/pallas_call | solution.py:139
  60.9 6.4 %shard_map.137 = (f32[256,256]{1,0:T(8,128)S(1)}, bf16[256,256]{1,0:T(8,128)(2,1)S(1)}, bf16[256,256]{1,0:T(8,128)(2,1)S(1)}, bf16[256,256]{1,0:T(8,128)(2,1)S(1)}) custom-call(s32[4]{0:T(128)S(1)} %copy-done.7, s32[1]{0:T(128)} %bitcast.place_ref, ...), custom_call_target="tpu_custom_call", output_to_operand_aliasing={{0}: (8, {}), {1}: (9, {}), {2}: (10, {}), {3}: (11, {})} | custom-call | flops 4294967296 | bytes 2097152 | tf_op jit(solution)/shard_map/pallas_call | solution.py:139
  68.4 1.6 %collective-permute-start.8 = (bf16[256,256]{1,0:T(8,128)(2,1)S(1)}, bf16[256,256]{1,0:T(8,128)(2,1)S(1)}, u32[]{:S(2)}, u32[]{:S(2)}) collective-permute-start(bf16[256,256]{1,0:T(8,128)(2,1)S(1)} %get-tuple-element.43), channel_id=1, source_target_pairs={{0,4},{4,0},{8,12},{12,8},{1,5},{5,1},{9,13},{13,9},{2,6},{6,2},{1... | collective-permute-start | bytes 393224 | tf_op jit(solution)/shard_map/ppermute | solution.py:34
  70.0 1.6 %collective-permute-start.9 = (bf16[256,256]{1,0:T(8,128)(2,1)S(1)}, bf16[256,256]{1,0:T(8,128)(2,1)S(1)}, u32[]{:S(2)}, u32[]{:S(2)}) collective-permute-start(bf16[256,256]{1,0:T(8,128)(2,1)S(1)} %get-tuple-element.44), channel_id=1, source_target_pairs={{0,8},{4,12},{8,0},{12,4},{1,9},{5,13},{9,1},{13,5},{2,10},{6,14},... | collective-permute-start | bytes 393224 | tf_op jit(solution)/shard_map/ppermute | solution.py:34
  71.6 6.4 %shard_map.139 = (f32[256,256]{1,0:T(8,128)S(1)}, bf16[256,256]{1,0:T(8,128)(2,1)S(1)}, bf16[256,256]{1,0:T(8,128)(2,1)S(1)}, bf16[256,256]{1,0:T(8,128)(2,1)S(1)}) custom-call(s32[4]{0:T(128)S(1)} %copy-done.7, s32[1]{0:T(128)} %bitcast.place_ref, bf16[4,256,256]{2,1,0:T(8,128)(2,1)} %refs_0_.10, bf16[4,256,256]{2,1,0:T(8,128)(2,1)S(1)} %collective-permute-done.refs_1_, ...), custom_call_target="tpu_custom_call" | custom-call | flops 4294967296 | bytes 2097152 | tf_op jit(solution)/shard_map/pallas_call | solution.py:139
  78.0 2.9 %collective-permute-start.24 = (bf16[256,256]{1,0:T(8,128)(2,1)S(1)}, bf16[256,256]{1,0:T(8,128)(2,1)S(1)}, u32[]{:S(2)}, u32[]{:S(2)}) collective-permute-start(bf16[256,256]{1,0:T(8,128)(2,1)S(1)} %shard_map.133.refs_6_.refs_0_), channel_id=1, source_target_pairs={{0,2},{1,3},{2,0},{3,1},{4,6},{5,7},{6,4},{7,5},{8,10},{9,11},{10,... | collective-permute-start | bytes 393224 | tf_op jit(solution)/shard_map/ppermute | solution.py:34
  81.2 6.6 %shard_map.140 = (f32[256,256]{1,0:T(8,128)S(1)}, bf16[256,256]{1,0:T(8,128)(2,1)S(1)}, bf16[256,256]{1,0:T(8,128)(2,1)S(1)}, bf16[256,256]{1,0:T(8,128)(2,1)S(1)}) custom-call(s32[4]{0:T(128)S(1)} %copy-done.7, s32[1]{0:T(128)} %bitcast.place_ref, ...), custom_call_target="tpu_custom_call", output_to_operand_aliasing={{0}: (8, {}), {1}: (9, {}), {2}: (10, {}), {3}: (11, {})} | custom-call | flops 4294967296 | bytes 2097152 | tf_op jit(solution)/shard_map/pallas_call | solution.py:139
  89.7 1.9 %collective-permute-start.26 = (bf16[256,256]{1,0:T(8,128)(2,1)S(1)}, bf16[256,256]{1,0:T(8,128)(2,1)S(1)}, u32[]{:S(2)}, u32[]{:S(2)}) collective-permute-start(bf16[256,256]{1,0:T(8,128)(2,1)S(1)} %shard_map.135.refs_10_.refs_6_.refs_4_), channel_id=1, source_target_pairs={{0,1},{1,0},{2,3},{3,2},{4,5},{5,4},{6,7},{7,6},{8,9},{9,8},{10,11... | collective-permute-start | bytes 393224 | tf_op jit(solution)/shard_map/ppermute | solution.py:34
  91.8 2.5 %collective-permute-done.12.refs_1_ = bf16[256,256]{1,0:T(8,128)(2,1)S(1)} collective-permute-done((bf16[256,256]{1,0:T(8,128)(2,1)S(1)}, bf16[256,256]{1,0:T(8,128)(2,1)S(1)}, u32[]{:S(2)}, u32[]{:S(2)}) %collective-permute-start.12) | collective-permute-done | bytes 131104 | tf_op jit(solution)/shard_map/ppermute | solution.py:34
  94.3 1.9 %collective-permute-start.28 = (bf16[256,256]{1,0:T(8,128)(2,1)S(1)}, bf16[256,256]{1,0:T(8,128)(2,1)S(1)}, u32[]{:S(2)}, u32[]{:S(2)}) collective-permute-start(bf16[256,256]{1,0:T(8,128)(2,1)S(1)} %collective-permute-done.27.refs_6_), channel_id=1, source_target_pairs={{0,1},{1,0},{2,3},{3,2},{4,5},{5,4},{6,7},{7,6},{8,9},{9,8},{10,11... | collective-permute-start | bytes 393224 | tf_op jit(solution)/shard_map/ppermute | solution.py:34
  96.2 1.7 %collective-permute-start.25 = (bf16[256,256]{1,0:T(8,128)(2,1)S(1)}, bf16[256,256]{1,0:T(8,128)(2,1)S(1)}, u32[]{:S(2)}, u32[]{:S(2)}) collective-permute-start(bf16[256,256]{1,0:T(8,128)(2,1)S(1)} %collective-permute-done.24.refs_2_), channel_id=1, source_target_pairs={{0,1},{1,0},{2,3},{3,2},{4,5},{5,4},{6,7},{7,6},{8,9},{9,8},{10,11... | collective-permute-start | bytes 393224 | tf_op jit(solution)/shard_map/ppermute | solution.py:34
  98.9 2.3 %collective-permute-start.21 = (bf16[256,256]{1,0:T(8,128)(2,1)S(1)}, bf16[256,256]{1,0:T(8,128)(2,1)}, u32[]{:S(2)}, u32[]{:S(2)}) collective-permute-start(bf16[256,256]{1,0:T(8,128)(2,1)S(1)} %shard_map.141.refs_6_), channel_id=1, source_target_pairs={{0,2},{1,3},{2,0},{3,1},{4,6},{5,7},{6,4},{7,5},{8,10},{9,11},{10,... | collective-permute-start | bytes 393224 | tf_op jit(solution)/shard_map/ppermute | solution.py:34
  101.7 1.9 %collective-permute-start.17 = (bf16[256,256]{1,0:T(8,128)(2,1)S(1)}, bf16[256,256]{1,0:T(8,128)(2,1)}, u32[]{:S(2)}, u32[]{:S(2)}) collective-permute-start(bf16[256,256]{1,0:T(8,128)(2,1)S(1)} %shard_map.138.refs_10_.refs_2_), channel_id=1, source_target_pairs={{0,1},{1,0},{2,3},{3,2},{4,5},{5,4},{6,7},{7,6},{8,9},{9,8},{10,11... | collective-permute-start | bytes 393224 | tf_op jit(solution)/shard_map/ppermute | solution.py:34
  103.6 2.5 %collective-permute-done.25.refs_3_ = bf16[256,256]{1,0:T(8,128)(2,1)S(1)} collective-permute-done((bf16[256,256]{1,0:T(8,128)(2,1)S(1)}, bf16[256,256]{1,0:T(8,128)(2,1)S(1)}, u32[]{:S(2)}, u32[]{:S(2)}) %collective-permute-start.25) | collective-permute-done | bytes 131104 | tf_op jit(solution)/shard_map/ppermute | solution.py:34
  106.4 4.9 %collective-permute-done.18.refs_4_ = bf16[256,256]{1,0:T(8,128)(2,1)S(1)} collective-permute-done((bf16[256,256]{1,0:T(8,128)(2,1)S(1)}, bf16[256,256]{1,0:T(8,128)(2,1)S(1)}, u32[]{:S(2)}, u32[]{:S(2)}) %collective-permute-start.18) | collective-permute-done | bytes 131104 | tf_op jit(solution)/shard_map/ppermute | solution.py:34
  111.3 2.3 %collective-permute-done.21.refs_8_ = bf16[256,256]{1,0:T(8,128)(2,1)} collective-permute-done((bf16[256,256]{1,0:T(8,128)(2,1)S(1)}, bf16[256,256]{1,0:T(8,128)(2,1)}, u32[]{:S(2)}, u32[]{:S(2)}) %collective-permute-start.21) | collective-permute-done | bytes 131104 | tf_op jit(solution)/shard_map/ppermute | solution.py:34
  114.4 1.8 %collective-permute-done.20.refs_7_ = bf16[256,256]{1,0:T(8,128)(2,1)} collective-permute-done((bf16[256,256]{1,0:T(8,128)(2,1)S(1)}, bf16[256,256]{1,0:T(8,128)(2,1)}, u32[]{:S(2)}, u32[]{:S(2)}) %collective-permute-start.20) | collective-permute-done | bytes 131104 | tf_op jit(solution)/shard_map/ppermute | solution.py:34
  116.3 2.8 %collective-permute-done.19.refs_5_ = bf16[256,256]{1,0:T(8,128)(2,1)} collective-permute-done((bf16[256,256]{1,0:T(8,128)(2,1)S(1)}, bf16[256,256]{1,0:T(8,128)(2,1)}, u32[]{:S(2)}, u32[]{:S(2)}) %collective-permute-start.19) | collective-permute-done | bytes 131104 | tf_op jit(solution)/shard_map/ppermute | solution.py:34
  119.1 1.9 %collective-permute-done.22.refs_9_ = bf16[256,256]{1,0:T(8,128)(2,1)} collective-permute-done((bf16[256,256]{1,0:T(8,128)(2,1)}, bf16[256,256]{1,0:T(8,128)(2,1)}, u32[]{:S(2)}, u32[]{:S(2)}) %collective-permute-start.22) | collective-permute-done | bytes 131104 | tf_op jit(solution)/shard_map/ppermute | solution.py:34
  121.0 3.2 %shard_map.142 = (f32[512,256]{1,0:T(8,128)S(1)}, bf16[512,256]{1,0:T(8,128)(2,1)S(1)}, bf16[1024,256]{1,0:T(8,128)(2,1)S(1)}, bf16[1024,256]{1,0:T(8,128)(2,1)S(1)}) custom-call(s32[4]{0:T(128)S(1)} %copy-done.9, s32[1]{0:T(128)} %bitcast.place_ref, s32[1]{0:T(128)} %bitcast.4.col_ref, bf16[512,256]{1,0:T(8,128)(2,1)S(1)} %collective-permute-done.15.refs_0_, ...), custom_call_target="tpu_custom_call" | custom-call | tf_op jit(solution)/shard_map/pallas_call | solution.py:275
  124.3 1.5 %shard_map.143 = (f32[512,256]{1,0:T(8,128)S(1)}, bf16[512,256]{1,0:T(8,128)(2,1)S(1)}) custom-call(s32[4]{0:T(128)S(1)} %copy-done.9, s32[1]{0:T(128)} %bitcast.place_ref, s32[1]{0:T(128)} %bitcast.4.col_ref, bf16[512,256]{1,0:T(8,128)(2,1)S(1)} %copy-done.5, bf16[512,256]{1,0:T(8,128)(2,1)S(1)} %collective-permute-done.14.refs_1_, ...), custom_call_target="tpu_custom_call" | custom-call | tf_op jit(solution)/shard_map/pallas_call | solution.py:275
  127.8 6.9 %collective-permute-done.31.refs_2_ = bf16[512,256]{1,0:T(8,128)(2,1)S(1)} collective-permute-done((bf16[512,256]{1,0:T(8,128)(2,1)S(1)}, bf16[512,256]{1,0:T(8,128)(2,1)S(1)}, u32[]{:S(2)}, u32[]{:S(2)}) %collective-permute-start.31) | collective-permute-done | bytes 262176 | tf_op jit(solution)/shard_map/ppermute | solution.py:34
  134.8 1.9 %gate_cands.1 = bf16[512,256]{1,0:T(8,128)(2,1)} custom-call(s32[4]{0:T(128)S(1)} %copy-done.9, s32[1]{0:T(128)} %bitcast.place_ref, f32[512,256]{1,0:T(8,128)S(1)} %get-tuple-element.58.refs_0_, bf16[512,256]{1,0:T(8,128)(2,1)S(1)} %collective-permute-done.29.refs_1_, bf16[512,256]{1,0:T(8,128)(2,1)S(1)} %collective-permute-done.31.refs_2_, ...), custom_call_target="tpu_custom_call" | custom-call | tf_op jit(solution)/shard_map/gate_cands/pallas_call | solution.py:310
  (71 shorter events, 11.3 us)
Async XLA Ops:
  0.6 15.2 %collective-permute-start.2 = (bf16[4,256,256]{2,1,0:T(8,128)(2,1)}, bf16[4,256,256]{2,1,0:T(8,128)(2,1)S(1)}, u32[]{:S(2)}, u32[]{:S(2)}) collective-permute-start(bf16[4,256,256]{2,1,0:T(8,128)(2,1)} %refs_0_.10), channel_id=1, source_target_pairs={{0,8},{4,12},{8,0},{12,4},{1,9},{5,13},{9,1},{13,5},{2,10},{6,14},... | collective-permute-start | bytes 1572872 | tf_op jit(solution)/shard_map/ppermute | solution.py:34
  3.7 12.1 %collective-permute-start = (bf16[4,256,256]{2,1,0:T(8,128)(2,1)}, bf16[4,256,256]{2,1,0:T(8,128)(2,1)S(1)}, u32[]{:S(2)}, u32[]{:S(2)}) collective-permute-start(bf16[4,256,256]{2,1,0:T(8,128)(2,1)} %refs_0_.10), channel_id=1, source_target_pairs={{0,4},{4,0},{8,12},{12,8},{1,5},{5,1},{9,13},{13,9},{2,6},{6,2},{1... | collective-permute-start | bytes 1572872 | tf_op jit(solution)/shard_map/ppermute | solution.py:34
  15.8 14.0 %collective-permute-start.3 = (bf16[4,256,256]{2,1,0:T(8,128)(2,1)S(1)}, bf16[4,256,256]{2,1,0:T(8,128)(2,1)S(1)}, u32[]{:S(2)}, u32[]{:S(2)}) collective-permute-start(bf16[4,256,256]{2,1,0:T(8,128)(2,1)S(1)} %collective-permute-done.2.refs_0_.refs_2_), channel_id=1, source_target_pairs={{0,4},{4,0},{8,12},{12,8},{1,5},{5,1},{9,13},{13,9},{2,6},{6,2},{1... | collective-permute-start | bytes 1572872 | tf_op jit(solution)/shard_map/ppermute | solution.py:34
  29.8 16.0 %collective-permute-start.1 = (bf16[512,256]{1,0:T(8,128)(2,1)S(1)}, bf16[512,256]{1,0:T(8,128)(2,1)S(1)}, u32[]{:S(2)}, u32[]{:S(2)}) collective-permute-start(bf16[512,256]{1,0:T(8,128)(2,1)S(1)} %get-tuple-element.33), channel_id=1, source_target_pairs={{0,4},{4,0},{8,12},{12,8},{1,5},{5,1},{9,13},{13,9},{2,6},{6,2},{1... | collective-permute-start | bytes 786440 | tf_op jit(solution)/shard_map/ppermute | solution.py:34
  42.2 6.4 %collective-permute-start.6 = (bf16[256,256]{1,0:T(8,128)(2,1)S(1)}, bf16[256,256]{1,0:T(8,128)(2,1)S(1)}, u32[]{:S(2)}, u32[]{:S(2)}) collective-permute-start(bf16[256,256]{1,0:T(8,128)(2,1)S(1)} %get-tuple-element.36.refs_7_), channel_id=1, source_target_pairs={{0,8},{4,12},{8,0},{12,4},{1,9},{5,13},{9,1},{13,5},{2,10},{6,14},... | collective-permute-start | bytes 393224 | tf_op jit(solution)/shard_map/ppermute | solution.py:34
  42.3 6.4 %collective-permute-start.7 = (bf16[256,256]{1,0:T(8,128)(2,1)S(1)}, bf16[256,256]{1,0:T(8,128)(2,1)S(1)}, u32[]{:S(2)}, u32[]{:S(2)}) collective-permute-start(bf16[256,256]{1,0:T(8,128)(2,1)S(1)} %get-tuple-element.37), channel_id=1, source_target_pairs={{0,12},{4,8},{8,4},{12,0},{1,13},{5,9},{9,5},{13,1},{2,14},{6,10},... | collective-permute-start | bytes 393224 | tf_op jit(solution)/shard_map/ppermute | solution.py:34
  42.4 11.9 %collective-permute-start.4 = (bf16[256,256]{1,0:T(8,128)(2,1)S(1)}, bf16[256,256]{1,0:T(8,128)(2,1)S(1)}, u32[]{:S(2)}, u32[]{:S(2)}) collective-permute-start(bf16[256,256]{1,0:T(8,128)(2,1)S(1)} %get-tuple-element.34.refs_4_), channel_id=1, source_target_pairs={{0,8},{4,12},{8,0},{12,4},{1,9},{5,13},{9,1},{13,5},{2,10},{6,14},... | collective-permute-start | bytes 393224 | tf_op jit(solution)/shard_map/ppermute | solution.py:34
  44.3 10.0 %collective-permute-start.5 = (bf16[256,256]{1,0:T(8,128)(2,1)S(1)}, bf16[256,256]{1,0:T(8,128)(2,1)S(1)}, u32[]{:S(2)}, u32[]{:S(2)}) collective-permute-start(bf16[256,256]{1,0:T(8,128)(2,1)S(1)} %get-tuple-element.35), channel_id=1, source_target_pairs={{0,12},{4,8},{8,4},{12,0},{1,13},{5,9},{9,5},{13,1},{2,14},{6,10},... | collective-permute-start | bytes 393224 | tf_op jit(solution)/shard_map/ppermute | solution.py:34
  45.8 42.6 %collective-permute-start.15 = (bf16[512,256]{1,0:T(8,128)(2,1)S(1)}, bf16[512,256]{1,0:T(8,128)(2,1)S(1)}, u32[]{:S(2)}, u32[]{:S(2)}) collective-permute-start(bf16[512,256]{1,0:T(8,128)(2,1)S(1)} %copy-done.5), channel_id=1, source_target_pairs={{0,8},{4,12},{8,0},{12,4},{1,9},{5,13},{9,1},{13,5},{2,10},{6,14},... | collective-permute-start | bytes 786440 | tf_op jit(solution)/shard_map/ppermute | solution.py:34
  48.9 40.8 %collective-permute-start.27 = (bf16[256,256]{1,0:T(8,128)(2,1)S(1)}, bf16[256,256]{1,0:T(8,128)(2,1)S(1)}, u32[]{:S(2)}, u32[]{:S(2)}) collective-permute-start(bf16[256,256]{1,0:T(8,128)(2,1)S(1)} %shard_map.135.refs_10_.refs_6_.refs_4_), channel_id=1, source_target_pairs={{0,2},{1,3},{2,0},{3,1},{4,6},{5,7},{6,4},{7,5},{8,10},{9,11},{10,... | collective-permute-start | bytes 393224 | tf_op jit(solution)/shard_map/ppermute | solution.py:34
  67.3 10.7 %collective-permute-start.10 = (bf16[256,256]{1,0:T(8,128)(2,1)S(1)}, bf16[256,256]{1,0:T(8,128)(2,1)S(1)}, u32[]{:S(2)}, u32[]{:S(2)}) collective-permute-start(bf16[256,256]{1,0:T(8,128)(2,1)S(1)} %get-tuple-element.45), channel_id=1, source_target_pairs={{0,12},{4,8},{8,4},{12,0},{1,13},{5,9},{9,5},{13,1},{2,14},{6,10},... | collective-permute-start | bytes 393224 | tf_op jit(solution)/shard_map/ppermute | solution.py:34
  68.4 12.4 %collective-permute-start.8 = (bf16[256,256]{1,0:T(8,128)(2,1)S(1)}, bf16[256,256]{1,0:T(8,128)(2,1)S(1)}, u32[]{:S(2)}, u32[]{:S(2)}) collective-permute-start(bf16[256,256]{1,0:T(8,128)(2,1)S(1)} %get-tuple-element.43), channel_id=1, source_target_pairs={{0,4},{4,0},{8,12},{12,8},{1,5},{5,1},{9,13},{13,9},{2,6},{6,2},{1... | collective-permute-start | bytes 393224 | tf_op jit(solution)/shard_map/ppermute | solution.py:34
  70.0 10.8 %collective-permute-start.9 = (bf16[256,256]{1,0:T(8,128)(2,1)S(1)}, bf16[256,256]{1,0:T(8,128)(2,1)S(1)}, u32[]{:S(2)}, u32[]{:S(2)}) collective-permute-start(bf16[256,256]{1,0:T(8,128)(2,1)S(1)} %get-tuple-element.44), channel_id=1, source_target_pairs={{0,8},{4,12},{8,0},{12,4},{1,9},{5,13},{9,1},{13,5},{2,10},{6,14},... | collective-permute-start | bytes 393224 | tf_op jit(solution)/shard_map/ppermute | solution.py:34
  78.0 13.6 %collective-permute-start.24 = (bf16[256,256]{1,0:T(8,128)(2,1)S(1)}, bf16[256,256]{1,0:T(8,128)(2,1)S(1)}, u32[]{:S(2)}, u32[]{:S(2)}) collective-permute-start(bf16[256,256]{1,0:T(8,128)(2,1)S(1)} %shard_map.133.refs_6_.refs_0_), channel_id=1, source_target_pairs={{0,2},{1,3},{2,0},{3,1},{4,6},{5,7},{6,4},{7,5},{8,10},{9,11},{10,... | collective-permute-start | bytes 393224 | tf_op jit(solution)/shard_map/ppermute | solution.py:34
  87.8 4.0 %collective-permute-start.11 = (bf16[256,256]{1,0:T(8,128)(2,1)S(1)}, bf16[256,256]{1,0:T(8,128)(2,1)S(1)}, u32[]{:S(2)}, u32[]{:S(2)}) collective-permute-start(bf16[256,256]{1,0:T(8,128)(2,1)S(1)} %get-tuple-element.51), channel_id=1, source_target_pairs={{0,4},{4,0},{8,12},{12,8},{1,5},{5,1},{9,13},{13,9},{2,6},{6,2},{1... | collective-permute-start | bytes 393224 | tf_op jit(solution)/shard_map/ppermute | solution.py:34
  87.9 6.4 %collective-permute-start.12 = (bf16[256,256]{1,0:T(8,128)(2,1)S(1)}, bf16[256,256]{1,0:T(8,128)(2,1)S(1)}, u32[]{:S(2)}, u32[]{:S(2)}) collective-permute-start(bf16[256,256]{1,0:T(8,128)(2,1)S(1)} %get-tuple-element.52), channel_id=1, source_target_pairs={{0,8},{4,12},{8,0},{12,4},{1,9},{5,13},{9,1},{13,5},{2,10},{6,14},... | collective-permute-start | bytes 393224 | tf_op jit(solution)/shard_map/ppermute | solution.py:34
  88.4 7.8 %collective-permute-start.13 = (bf16[256,256]{1,0:T(8,128)(2,1)S(1)}, bf16[256,256]{1,0:T(8,128)(2,1)S(1)}, u32[]{:S(2)}, u32[]{:S(2)}) collective-permute-start(bf16[256,256]{1,0:T(8,128)(2,1)S(1)} %get-tuple-element.53), channel_id=1, source_target_pairs={{0,12},{4,8},{8,4},{12,0},{1,13},{5,9},{9,5},{13,1},{2,14},{6,10},... | collective-permute-start | bytes 393224 | tf_op jit(solution)/shard_map/ppermute | solution.py:34
  89.7 8.4 %collective-permute-start.26 = (bf16[256,256]{1,0:T(8,128)(2,1)S(1)}, bf16[256,256]{1,0:T(8,128)(2,1)S(1)}, u32[]{:S(2)}, u32[]{:S(2)}) collective-permute-start(bf16[256,256]{1,0:T(8,128)(2,1)S(1)} %shard_map.135.refs_10_.refs_6_.refs_4_), channel_id=1, source_target_pairs={{0,1},{1,0},{2,3},{3,2},{4,5},{5,4},{6,7},{7,6},{8,9},{9,8},{10,11... | collective-permute-start | bytes 393224 | tf_op jit(solution)/shard_map/ppermute | solution.py:34
  91.6 7.3 %collective-permute-start.23 = (bf16[256,256]{1,0:T(8,128)(2,1)S(1)}, bf16[256,256]{1,0:T(8,128)(2,1)S(1)}, u32[]{:S(2)}, u32[]{:S(2)}) collective-permute-start(bf16[256,256]{1,0:T(8,128)(2,1)S(1)} %shard_map.133.refs_6_.refs_0_), channel_id=1, source_target_pairs={{0,1},{1,0},{2,3},{3,2},{4,5},{5,4},{6,7},{7,6},{8,9},{9,8},{10,11... | collective-permute-start | bytes 393224 | tf_op jit(solution)/shard_map/ppermute | solution.py:34
  91.8 22.6 %collective-permute-start.16 = (bf16[512,256]{1,0:T(8,128)(2,1)S(1)}, bf16[512,256]{1,0:T(8,128)(2,1)S(1)}, u32[]{:S(2)}, u32[]{:S(2)}) collective-permute-start(bf16[512,256]{1,0:T(8,128)(2,1)S(1)} %collective-permute-done.15.refs_0_), channel_id=1, source_target_pairs={{0,4},{4,0},{8,12},{12,8},{1,5},{5,1},{9,13},{13,9},{2,6},{6,2},{1... | collective-permute-start | bytes 786440 | tf_op jit(solution)/shard_map/ppermute | solution.py:34
  94.3 7.4 %collective-permute-start.28 = (bf16[256,256]{1,0:T(8,128)(2,1)S(1)}, bf16[256,256]{1,0:T(8,128)(2,1)S(1)}, u32[]{:S(2)}, u32[]{:S(2)}) collective-permute-start(bf16[256,256]{1,0:T(8,128)(2,1)S(1)} %collective-permute-done.27.refs_6_), channel_id=1, source_target_pairs={{0,1},{1,0},{2,3},{3,2},{4,5},{5,4},{6,7},{7,6},{8,9},{9,8},{10,11... | collective-permute-start | bytes 393224 | tf_op jit(solution)/shard_map/ppermute | solution.py:34
  96.2 9.9 %collective-permute-start.25 = (bf16[256,256]{1,0:T(8,128)(2,1)S(1)}, bf16[256,256]{1,0:T(8,128)(2,1)S(1)}, u32[]{:S(2)}, u32[]{:S(2)}) collective-permute-start(bf16[256,256]{1,0:T(8,128)(2,1)S(1)} %collective-permute-done.24.refs_2_), channel_id=1, source_target_pairs={{0,1},{1,0},{2,3},{3,2},{4,5},{5,4},{6,7},{7,6},{8,9},{9,8},{10,11... | collective-permute-start | bytes 393224 | tf_op jit(solution)/shard_map/ppermute | solution.py:34
  98.2 13.1 %collective-permute-start.18 = (bf16[256,256]{1,0:T(8,128)(2,1)S(1)}, bf16[256,256]{1,0:T(8,128)(2,1)S(1)}, u32[]{:S(2)}, u32[]{:S(2)}) collective-permute-start(bf16[256,256]{1,0:T(8,128)(2,1)S(1)} %shard_map.138.refs_10_.refs_2_), channel_id=1, source_target_pairs={{0,2},{1,3},{2,0},{3,1},{4,6},{5,7},{6,4},{7,5},{8,10},{9,11},{10,... | collective-permute-start | bytes 393224 | tf_op jit(solution)/shard_map/ppermute | solution.py:34
  98.9 14.7 %collective-permute-start.21 = (bf16[256,256]{1,0:T(8,128)(2,1)S(1)}, bf16[256,256]{1,0:T(8,128)(2,1)}, u32[]{:S(2)}, u32[]{:S(2)}) collective-permute-start(bf16[256,256]{1,0:T(8,128)(2,1)S(1)} %shard_map.141.refs_6_), channel_id=1, source_target_pairs={{0,2},{1,3},{2,0},{3,1},{4,6},{5,7},{6,4},{7,5},{8,10},{9,11},{10,... | collective-permute-start | bytes 393224 | tf_op jit(solution)/shard_map/ppermute | solution.py:34
  101.7 12.7 %collective-permute-start.17 = (bf16[256,256]{1,0:T(8,128)(2,1)S(1)}, bf16[256,256]{1,0:T(8,128)(2,1)}, u32[]{:S(2)}, u32[]{:S(2)}) collective-permute-start(bf16[256,256]{1,0:T(8,128)(2,1)S(1)} %shard_map.138.refs_10_.refs_2_), channel_id=1, source_target_pairs={{0,1},{1,0},{2,3},{3,2},{4,5},{5,4},{6,7},{7,6},{8,9},{9,8},{10,11... | collective-permute-start | bytes 393224 | tf_op jit(solution)/shard_map/ppermute | solution.py:34
  106.2 10.1 %collective-permute-start.20 = (bf16[256,256]{1,0:T(8,128)(2,1)S(1)}, bf16[256,256]{1,0:T(8,128)(2,1)}, u32[]{:S(2)}, u32[]{:S(2)}) collective-permute-start(bf16[256,256]{1,0:T(8,128)(2,1)S(1)} %shard_map.141.refs_6_), channel_id=1, source_target_pairs={{0,1},{1,0},{2,3},{3,2},{4,5},{5,4},{6,7},{7,6},{8,9},{9,8},{10,11... | collective-permute-start | bytes 393224 | tf_op jit(solution)/shard_map/ppermute | solution.py:34
  111.3 7.8 %collective-permute-start.19 = (bf16[256,256]{1,0:T(8,128)(2,1)S(1)}, bf16[256,256]{1,0:T(8,128)(2,1)}, u32[]{:S(2)}, u32[]{:S(2)}) collective-permute-start(bf16[256,256]{1,0:T(8,128)(2,1)S(1)} %collective-permute-done.18.refs_4_), channel_id=1, source_target_pairs={{0,1},{1,0},{2,3},{3,2},{4,5},{5,4},{6,7},{7,6},{8,9},{9,8},{10,11... | collective-permute-start | bytes 393224 | tf_op jit(solution)/shard_map/ppermute | solution.py:34
  113.6 7.4 %collective-permute-start.22 = (bf16[256,256]{1,0:T(8,128)(2,1)}, bf16[256,256]{1,0:T(8,128)(2,1)}, u32[]{:S(2)}, u32[]{:S(2)}) collective-permute-start(bf16[256,256]{1,0:T(8,128)(2,1)} %collective-permute-done.21.refs_8_), channel_id=1, source_target_pairs={{0,1},{1,0},{2,3},{3,2},{4,5},{5,4},{6,7},{7,6},{8,9},{9,8},{10,11... | collective-permute-start | bytes 393224 | tf_op jit(solution)/shard_map/ppermute | solution.py:34
  114.4 10.0 %collective-permute-start.14 = (bf16[512,256]{1,0:T(8,128)(2,1)S(1)}, bf16[512,256]{1,0:T(8,128)(2,1)S(1)}, u32[]{:S(2)}, u32[]{:S(2)}) collective-permute-start(bf16[512,256]{1,0:T(8,128)(2,1)S(1)} %copy-done.5), channel_id=1, source_target_pairs={{0,4},{4,0},{8,12},{12,8},{1,5},{5,1},{9,13},{13,9},{2,6},{6,2},{1... | collective-permute-start | bytes 786440 | tf_op jit(solution)/shard_map/ppermute | solution.py:34
  124.3 2.2 %collective-permute-start.30 = (bf16[512,256]{1,0:T(8,128)(2,1)S(1)}, bf16[512,256]{1,0:T(8,128)(2,1)S(1)}, u32[]{:S(2)}, u32[]{:S(2)}) collective-permute-start(bf16[512,256]{1,0:T(8,128)(2,1)S(1)} %get-tuple-element.61), channel_id=1, source_target_pairs={{0,4},{4,0},{8,12},{12,8},{1,5},{5,1},{9,13},{13,9},{2,6},{6,2},{1... | collective-permute-start | bytes 786440 | tf_op jit(solution)/shard_map/ppermute | solution.py:34
  125.9 2.0 %collective-permute-start.29 = (bf16[512,256]{1,0:T(8,128)(2,1)S(1)}, bf16[512,256]{1,0:T(8,128)(2,1)S(1)}, u32[]{:S(2)}, u32[]{:S(2)}) collective-permute-start(bf16[512,256]{1,0:T(8,128)(2,1)S(1)} %get-tuple-element.59), channel_id=1, source_target_pairs={{0,4},{4,0},{8,12},{12,8},{1,5},{5,1},{9,13},{13,9},{2,6},{6,2},{1... | collective-permute-start | bytes 786440 | tf_op jit(solution)/shard_map/ppermute | solution.py:34
  126.5 8.3 %collective-permute-start.31 = (bf16[512,256]{1,0:T(8,128)(2,1)S(1)}, bf16[512,256]{1,0:T(8,128)(2,1)S(1)}, u32[]{:S(2)}, u32[]{:S(2)}) collective-permute-start(bf16[512,256]{1,0:T(8,128)(2,1)S(1)} %add_convert_fusion), channel_id=1, source_target_pairs={{0,8},{4,12},{8,0},{12,4},{1,9},{5,13},{9,1},{13,5},{2,10},{6,14},... | collective-permute-start | bytes 786440 | tf_op jit(solution)/shard_map/ppermute | solution.py:34
  (11 other events, 261.3 us)

commit v3 on v2

--- a/solution.py
+++ b/solution.py
@@ -63,20 +63,23 @@
     )
 
 
-def attend_near(users, queries, hist_len, place, keys, values):
+def attend_first(users, queries, own_first, resident, hist_len, place, keys, values, after=()):
     n = len(queries)
     _, rows, width = queries[0].shape
     hist_rows = keys.shape[1]
 
     def kern(len_ref, place_ref, *refs):
-        q_refs, k_ref, v_ref, o_refs = refs[:n], refs[n], refs[n + 1], refs[n + 2 :]
+        q_refs, k_ref, v_ref, o_refs = refs[:n], refs[n], refs[n + 1], refs[n + 2 + len(after) :]
+        user, head = 0, slice(None)
+        if resident:
+            user, head = pl.program_id(1), pl.ds(pl.multiple_of(pl.program_id(0) * HEAD, HEAD), HEAD)
         left = len_ref[pl.program_id(1)] - place_ref[0] * hist_rows
 
         @pl.when(left > 0)
         def _():
             q = join([r[0] for r in q_refs])
-            k = (lambda a, b: k_ref[0, a:b], hist_rows)
-            v = (lambda a, b: v_ref[0, a:b], hist_rows)
+            k = (lambda a, b: k_ref[user, a:b, head], hist_rows)
+            v = (lambda a, b: v_ref[user, a:b, head], hist_rows)
             o = weigh(q, k, v, left)
             for m, o_ref in enumerate(o_refs):
                 o_ref[...] = o[m * rows : (m + 1) * rows].astype(o_ref.dtype)
@@ -87,19 +90,19 @@
                 o_ref[...] = jnp.zeros(o_ref.shape, o_ref.dtype)
 
     piece = pl.BlockSpec((1, rows, HEAD), lambda h, g, *_: (g, 0, h))
-    hist = pl.BlockSpec((1, hist_rows, HEAD), lambda h, g, *_: (g, 0, h))
+    hist = INSIDE if resident else pl.BlockSpec((1, hist_rows, HEAD), lambda h, g, *_: (g, 0, h))
     return pl.pallas_call(
         kern,
         grid_spec=pltpu.PrefetchScalarGridSpec(
             num_scalar_prefetch=2,
             grid=(width // HEAD, users),
-            in_specs=[piece] * n + [hist, hist],
+            in_specs=[piece] * n + [hist, hist] + [ANY] * len(after),
             out_specs=[pl.BlockSpec((rows, HEAD), lambda h, g, *_: (g, h))] * n,
         ),
-        out_shape=[jax.ShapeDtypeStruct((users * rows, width), BF16 if i else F32) for i in range(n)],
+        out_shape=[jax.ShapeDtypeStruct((users * rows, width), F32 if own_first and i == 0 else BF16) for i in range(n)],
         cost_estimate=attend_cost(users * n * rows, hist_rows, width, 4 * users * hist_rows * width),
         compiler_params=LARGE,
-    )(hist_len, place, *queries, keys, values)
+    )(hist_len, place, *queries, keys, values, *after)
 
 
 def attend(user, heads, queries, own_first, hist_len, place, keys, values, after, earlier=(), looped=False):
@@ -368,39 +371,26 @@
         def gate_chunk(own, others, halves, gate_at):
             return gate_events(own, others, halves * half, gate_at * half, event_gain, gates)
 
-        own01, *near01 = attend_near(2, queries[:2], hist_len, place, *in_hbm)
+        heads = range(width // HEAD)
+        own01, *near01 = attend_first(2, queries[:2], True, False, hist_len, place, *in_hbm)
         got01 = exchange(near01, 1)
-        heads = range(width // HEAD)
-        most = range((len(heads) + 1) // 2)
-        rest = range(len(most), len(heads))
-
-        def in_two(user, before, between):
-            sums = attend(user, most, queries, True, *hist, before)
-            middle = between(sums[0])
-            if len(rest):
-                sums = attend(user, rest, queries, True, *hist, (middle,), sums)
-            return sums, middle
-
-        far0 = attend(0, heads, queries[2:], False, *hist, (own01,), looped=True)
-        far1 = attend(1, heads, queries[2:], False, *hist, (far0[0],), looped=True)
-        got0, got1 = exchange(far0, 2), exchange(far1, 2)
-        near1 = [(x, rows) for x in got01]
-        gated0 = gate_chunk((own01, 0), [(x, 0) for x in got01 + got0], 2, 0)
-        out2, gated1 = in_two(
-            2, (gated0, far1[0]), lambda _: gate_chunk((own01, rows), near1 + [(x, 0) for x in got1], 2, 2)
-        )
+        far01 = attend_first(2, queries[2:], False, True, *hist, (own01,))
+        got01 = got01 + exchange(far01, 2)
+        out2 = attend(2, heads, queries, True, *hist, (far01[0],))
         got2 = exchange(out2[1:], 1)
-        out3, gated2 = in_two(3, (gated1, out2[0]), lambda _: gate_chunk((out2[0], 0), [(x, 0) for x in got2], 2, 4))
+        gated01 = gate_chunk((own01, 0), [(x, 0) for x in got01], 4, 0)
+        out3 = attend(3, heads, queries, True, *hist, (gated01, out2[0]))
         got3 = exchange(out3[1:], 1)
+        gated2 = gate_chunk((out2[0], 0), [(x, 0) for x in got2], 2, 4)
         gated3 = gate_chunk((out3[0], 0), [(x, 0) for x in got3], 2, 6)
-        gated = [gated0, gated1, gated2, gated3]
+        gated = [gated01, gated2, gated3]
         all_columns = [gather_pieces(g, "hd", n_hd) for g in gated]
-        early = early_keys(all_columns[:2], column, key_weight, value_weight)
+        early = early_keys(all_columns[:1], column, key_weight, value_weight)
         weights = (key_weight, value_weight)
         near = list(range(min(2, n_ev)))
         far = list(range(2, n_ev))
         common = (cand_count, place, column, weights)
-        *sums, all_keys, all_values = cand_sums(n_users, early, all_columns[2:], [cands[j] for j in far], far, *common)
+        *sums, all_keys, all_values = cand_sums(n_users, early, all_columns[1:], [cands[j] for j in far], far, *common)
         done = (all_keys, all_values)
         sums = [*cand_sums(n_users, done, [], [cands[j] for j in near], near, *common), *sums]
         held = {j: [x] for j, x in enumerate(sums)}

time: 137 us -> 122 us (0.89)
  starting transfers between devices: 30.3 us -> 21.7 us
  Pallas kernels: 59.6 us -> 55.1 us
  waiting for transfers between devices: 44.2 us -> 42.7 us
    pallas_call x6 -> x2, Pallas kernels: 38 us -> 21.9 us  [attend(): pl.pallas_call(kern, grid_spec=pltpu.PrefetchScalarGridSpec(num_scalar_pr...]
    pallas_call x1 -> x2, Pallas kernels: 13.3 us -> 25 us  [attend_first(): pl.pallas_call(kern, grid_spec=pltpu.PrefetchScalarGridSpec(num_scalar_pr...]
    ppermute x32 -> x27, starting transfers between devices: 30.3 us -> 21.7 us  [swap(): return lax.ppermute(x, axis, [(i, i ^ j) for i in range(size)])]
    ppermute x32 -> x27, waiting for transfers between devices: 44.2 us -> 42.7 us  [swap(): return lax.ppermute(x, axis, [(i, i ^ j) for i in range(size)])]
  transfers between devices with their start and end apart: 32 -> 27, of which waited for: 13 -> 9; matrix products, arithmetic and copies ran while one was open for 1% -> 1% of each run, Pallas kernels for 42% -> 44%
where the time goes in v3:
time: 122 us
  Pallas kernels  55.1 us (45%)
  waiting for transfers between devices  42.7 us (35%)
  starting transfers between devices  21.7 us (18%)
    ppermute x27, waiting for transfers between devices, swap(): return lax.ppermute(x, axis, [(i, i ^ j) for i in range(size)])  42.7 us
    pallas_call x2, Pallas kernels, attend_first(): pl.pallas_call(kern, grid_spec=pltpu.PrefetchScalarGridSpec(num_scalar_pr...  25 us
    pallas_call x2, Pallas kernels, attend(): pl.pallas_call(kern, grid_spec=pltpu.PrefetchScalarGridSpec(num_scalar_pr...  21.9 us
    ppermute x27, starting transfers between devices, swap(): return lax.ppermute(x, axis, [(i, i ^ j) for i in range(size)])  21.7 us
    pallas_call x2, Pallas kernels, cand_sums(): pl.pallas_call(kern, grid_spec=pltpu.PrefetchScalarGridSpec(num_scalar_pr...  4.74 us
  transfers between devices with their start and end apart: 27, of which 9 were waited for; matrix products, arithmetic and copies ran while one was open for 1% of the time, Pallas kernels for 44%

profile of v3, /device:TPU:0, one launch (start us, length us, event | category | flops | bytes accessed | tf_op | source)
XLA Modules:
  0.0 122.0 jit_solution(14605476464992459170)
XLA Ops:
  0.6 3.1 %collective-permute-start.2 = (bf16[4,256,256]{2,1,0:T(8,128)(2,1)}, bf16[4,256,256]{2,1,0:T(8,128)(2,1)S(1)}, u32[]{:S(2)}, u32[]{:S(2)}) collective-permute-start(bf16[4,256,256]{2,1,0:T(8,128)(2,1)} %refs_0_.6), channel_id=1, source_target_pairs={{0,8},{4,12},{8,0},{12,4},{1,9},{5,13},{9,1},{13,5},{2,10},{6,14},... | collective-permute-start | bytes 1572872 | tf_op jit(solution)/shard_map/ppermute | solution.py:34
  3.9 12.8 %collective-permute-done.2.refs_0_.refs_2_ = bf16[4,256,256]{2,1,0:T(8,128)(2,1)S(1)} collective-permute-done((bf16[4,256,256]{2,1,0:T(8,128)(2,1)}, bf16[4,256,256]{2,1,0:T(8,128)(2,1)S(1)}, u32[]{:S(2)}, u32[]{:S(2)}) %collective-permute-start.2) | collective-permute-done | bytes 524320 | tf_op jit(solution)/shard_map/ppermute | solution.py:34
  16.7 0.7 copy-done.10
  17.3 13.3 %shard_map.131 = (f32[512,256]{1,0:T(8,128)S(1)}, bf16[512,256]{1,0:T(8,128)(2,1)S(1)}) custom-call(s32[4]{0:T(128)S(1)} %copy-done.10, s32[1]{0:T(128)} %bitcast.place_ref, bf16[4,256,256]{2,1,0:T(8,128)(2,1)} %refs_0_.6, bf16[4,256,256]{2,1,0:T(8,128)(2,1)S(1)} %collective-permute-done.refs_1_, bf16[4,4096,256]{2,1,0:T(8,128)(2,1)} %refs_4_.5, ...), custom_call_target="tpu_custom_call" | custom-call | flops 8589934592 | bytes 8388608 | tf_op jit(solution)/shard_map/pallas_call | solution.py:94
  30.8 11.7 %shard_map.132 = (bf16[512,256]{1,0:T(8,128)(2,1)S(1)}, bf16[512,256]{1,0:T(8,128)(2,1)S(1)}) custom-call(s32[4]{0:T(128)S(1)} %copy-done.10, s32[1]{0:T(128)} %bitcast.place_ref, bf16[4,256,256]{2,1,0:T(8,128)(2,1)S(1)} %collective-permute-done.2.refs_0_.refs_2_, bf16[4,256,256]{2,1,0:T(8,128)(2,1)S(1)} %collective-permute-done.3.refs_1_.refs_3_, ...), custom_call_target="tpu_custom_call" | custom-call | flops 8589934592 | bytes 8388608 | tf_op jit(solution)/shard_map/pallas_call | solution.py:94
  42.6 10.8 %shard_map.134 = (f32[256,256]{1,0:T(8,128)S(1)}, bf16[256,256]{1,0:T(8,128)(2,1)S(1)}, bf16[256,256]{1,0:T(8,128)(2,1)S(1)}, bf16[256,256]{1,0:T(8,128)(2,1)S(1)}) custom-call(s32[4]{0:T(128)S(1)} %copy-done.10, s32[1]{0:T(128)} %bitcast.place_ref, bf16[4,256,256]{2,1,0:T(8,128)(2,1)} %refs_0_.6, bf16[4,256,256]{2,1,0:T(8,128)(2,1)S(1)} %collective-permute-done.refs_1_, ...), custom_call_target="tpu_custom_call" | custom-call | flops 8589934592 | bytes 4194304 | tf_op jit(solution)/shard_map/pallas_call | solution.py:142
  53.4 2.1 %collective-permute-start.6 = (bf16[256,256]{1,0:T(8,128)(2,1)S(1)}, bf16[256,256]{1,0:T(8,128)(2,1)S(1)}, u32[]{:S(2)}, u32[]{:S(2)}) collective-permute-start(bf16[256,256]{1,0:T(8,128)(2,1)S(1)} %get-tuple-element.27), channel_id=1, source_target_pairs={{0,4},{4,0},{8,12},{12,8},{1,5},{5,1},{9,13},{13,9},{2,6},{6,2},{1... | collective-permute-start | bytes 393224 | tf_op jit(solution)/shard_map/ppermute | solution.py:34
  55.6 1.3 %collective-permute-start.8 = (bf16[256,256]{1,0:T(8,128)(2,1)S(1)}, bf16[256,256]{1,0:T(8,128)(2,1)S(1)}, u32[]{:S(2)}, u32[]{:S(2)}) collective-permute-start(bf16[256,256]{1,0:T(8,128)(2,1)S(1)} %get-tuple-element.29), channel_id=1, source_target_pairs={{0,12},{4,8},{8,4},{12,0},{1,13},{5,9},{9,5},{13,1},{2,14},{6,10},... | collective-permute-start | bytes 393224 | tf_op jit(solution)/shard_map/ppermute | solution.py:34
  57.4 3.2 %collective-permute-start.22 = (bf16[512,256]{1,0:T(8,128)(2,1)S(1)}, bf16[512,256]{1,0:T(8,128)(2,1)S(1)}, u32[]{:S(2)}, u32[]{:S(2)}) collective-permute-start(bf16[512,256]{1,0:T(8,128)(2,1)S(1)} %shard_map.133.refs_6_.refs_0_), channel_id=1, source_target_pairs={{0,2},{1,3},{2,0},{3,1},{4,6},{5,7},{6,4},{7,5},{8,10},{9,11},{10,... | collective-permute-start | bytes 786440 | tf_op jit(solution)/shard_map/ppermute | solution.py:34
  60.6 11.1 %shard_map.136 = (f32[256,256]{1,0:T(8,128)S(1)}, bf16[256,256]{1,0:T(8,128)(2,1)S(1)}, bf16[256,256]{1,0:T(8,128)(2,1)S(1)}, bf16[256,256]{1,0:T(8,128)(2,1)S(1)}) custom-call(s32[4]{0:T(128)S(1)} %copy-done.10, s32[1]{0:T(128)} %bitcast.place_ref, bf16[4,256,256]{2,1,0:T(8,128)(2,1)} %refs_0_.6, bf16[4,256,256]{2,1,0:T(8,128)(2,1)S(1)} %collective-permute-done.refs_1_, ...), custom_call_target="tpu_custom_call" | custom-call | flops 8589934592 | bytes 4194304 | tf_op jit(solution)/shard_map/pallas_call | solution.py:142
  71.7 0.7 collective-permute-start.10
  72.4 1.2 collective-permute-start.11
  73.9 1.6 %collective-permute-start.21 = (bf16[512,256]{1,0:T(8,128)(2,1)S(1)}, bf16[512,256]{1,0:T(8,128)(2,1)S(1)}, u32[]{:S(2)}, u32[]{:S(2)}) collective-permute-start(bf16[512,256]{1,0:T(8,128)(2,1)S(1)} %shard_map.133.refs_6_.refs_0_), channel_id=1, source_target_pairs={{0,1},{1,0},{2,3},{3,2},{4,5},{5,4},{6,7},{7,6},{8,9},{9,8},{10,11... | collective-permute-start | bytes 786440 | tf_op jit(solution)/shard_map/ppermute | solution.py:34
  76.2 1.9 %collective-permute-done.10.refs_1_ = bf16[256,256]{1,0:T(8,128)(2,1)S(1)} collective-permute-done((bf16[256,256]{1,0:T(8,128)(2,1)S(1)}, bf16[256,256]{1,0:T(8,128)(2,1)S(1)}, u32[]{:S(2)}, u32[]{:S(2)}) %collective-permute-start.10) | collective-permute-done | bytes 131104 | tf_op jit(solution)/shard_map/ppermute | solution.py:34
  78.1 1.7 %collective-permute-done.11.refs_2_ = bf16[256,256]{1,0:T(8,128)(2,1)S(1)} collective-permute-done((bf16[256,256]{1,0:T(8,128)(2,1)S(1)}, bf16[256,256]{1,0:T(8,128)(2,1)S(1)}, u32[]{:S(2)}, u32[]{:S(2)}) %collective-permute-start.11) | collective-permute-done | bytes 131104 | tf_op jit(solution)/shard_map/ppermute | solution.py:34
  79.8 0.6 collective-permute-start.16
  80.7 2.4 %collective-permute-start.19 = (bf16[256,256]{1,0:T(8,128)(2,1)S(1)}, bf16[256,256]{1,0:T(8,128)(2,1)}, u32[]{:S(2)}, u32[]{:S(2)}) collective-permute-start(bf16[256,256]{1,0:T(8,128)(2,1)S(1)} %shard_map.137.refs_6_), channel_id=1, source_target_pairs={{0,2},{1,3},{2,0},{3,1},{4,6},{5,7},{6,4},{7,5},{8,10},{9,11},{10,... | collective-permute-start | bytes 393224 | tf_op jit(solution)/shard_map/ppermute | solution.py:34
  83.1 7.5 %collective-permute-done.16.refs_4_ = bf16[256,256]{1,0:T(8,128)(2,1)S(1)} collective-permute-done((bf16[256,256]{1,0:T(8,128)(2,1)S(1)}, bf16[256,256]{1,0:T(8,128)(2,1)S(1)}, u32[]{:S(2)}, u32[]{:S(2)}) %collective-permute-start.16) | collective-permute-done | bytes 131104 | tf_op jit(solution)/shard_map/ppermute | solution.py:34
  90.6 1.1 collective-permute-start.15
  91.7 3.8 %collective-permute-done.19.refs_8_ = bf16[256,256]{1,0:T(8,128)(2,1)} collective-permute-done((bf16[256,256]{1,0:T(8,128)(2,1)S(1)}, bf16[256,256]{1,0:T(8,128)(2,1)}, u32[]{:S(2)}, u32[]{:S(2)}) %collective-permute-start.19) | collective-permute-done | bytes 131104 | tf_op jit(solution)/shard_map/ppermute | solution.py:34
  95.5 2.0 %collective-permute-start.18 = (bf16[256,256]{1,0:T(8,128)(2,1)S(1)}, bf16[256,256]{1,0:T(8,128)(2,1)}, u32[]{:S(2)}, u32[]{:S(2)}) collective-permute-start(bf16[256,256]{1,0:T(8,128)(2,1)S(1)} %shard_map.137.refs_6_), channel_id=1, source_target_pairs={{0,1},{1,0},{2,3},{3,2},{4,5},{5,4},{6,7},{7,6},{8,9},{9,8},{10,11... | collective-permute-start | bytes 393224 | tf_op jit(solution)/shard_map/ppermute | solution.py:34
  97.6 0.7 early_keys.1
  98.4 3.5 %collective-permute-done.17.refs_5_ = bf16[256,256]{1,0:T(8,128)(2,1)} collective-permute-done((bf16[256,256]{1,0:T(8,128)(2,1)S(1)}, bf16[256,256]{1,0:T(8,128)(2,1)}, u32[]{:S(2)}, u32[]{:S(2)}) %collective-permute-start.17) | collective-permute-done | bytes 131104 | tf_op jit(solution)/shard_map/ppermute | solution.py:34
  102.0 2.8 %collective-permute-done.18.refs_7_ = bf16[256,256]{1,0:T(8,128)(2,1)} collective-permute-done((bf16[256,256]{1,0:T(8,128)(2,1)S(1)}, bf16[256,256]{1,0:T(8,128)(2,1)}, u32[]{:S(2)}, u32[]{:S(2)}) %collective-permute-start.18) | collective-permute-done | bytes 131104 | tf_op jit(solution)/shard_map/ppermute | solution.py:34
  104.8 1.6 %collective-permute-done.20.refs_9_ = bf16[256,256]{1,0:T(8,128)(2,1)} collective-permute-done((bf16[256,256]{1,0:T(8,128)(2,1)}, bf16[256,256]{1,0:T(8,128)(2,1)}, u32[]{:S(2)}, u32[]{:S(2)}) %collective-permute-start.20) | collective-permute-done | bytes 131104 | tf_op jit(solution)/shard_map/ppermute | solution.py:34
  106.3 3.2 %shard_map.138 = (f32[512,256]{1,0:T(8,128)S(1)}, bf16[512,256]{1,0:T(8,128)(2,1)S(1)}, bf16[1024,256]{1,0:T(8,128)(2,1)S(1)}, bf16[1024,256]{1,0:T(8,128)(2,1)S(1)}) custom-call(s32[4]{0:T(128)S(1)} %copy-done.6, s32[1]{0:T(128)} %bitcast.place_ref, s32[1]{0:T(128)} %bitcast.4.col_ref, bf16[512,256]{1,0:T(8,128)(2,1)S(1)} %collective-permute-done.13.refs_0_, ...), custom_call_target="tpu_custom_call" | custom-call | tf_op jit(solution)/shard_map/pallas_call | solution.py:278
  109.6 1.5 %shard_map.139 = (f32[512,256]{1,0:T(8,128)S(1)}, bf16[512,256]{1,0:T(8,128)(2,1)S(1)}) custom-call(s32[4]{0:T(128)S(1)} %copy-done.6, s32[1]{0:T(128)} %bitcast.place_ref, s32[1]{0:T(128)} %bitcast.4.col_ref, bf16[512,256]{1,0:T(8,128)(2,1)S(1)} %copy-done.3, bf16[512,256]{1,0:T(8,128)(2,1)S(1)} %collective-permute-done.12.refs_1_, ...), custom_call_target="tpu_custom_call" | custom-call | tf_op jit(solution)/shard_map/pallas_call | solution.py:278
  111.2 0.6 collective-permute-start.24
  111.8 0.5 collective-permute-start.26
  112.3 0.8 pad_maximum_fusion
  113.1 6.9 %collective-permute-done.26.refs_2_ = bf16[512,256]{1,0:T(8,128)(2,1)S(1)} collective-permute-done((bf16[512,256]{1,0:T(8,128)(2,1)S(1)}, bf16[512,256]{1,0:T(8,128)(2,1)S(1)}, u32[]{:S(2)}, u32[]{:S(2)}) %collective-permute-start.26) | collective-permute-done | bytes 262176 | tf_op jit(solution)/shard_map/ppermute | solution.py:34
  120.1 1.9 %gate_cands.1 = bf16[512,256]{1,0:T(8,128)(2,1)} custom-call(s32[4]{0:T(128)S(1)} %copy-done.6, s32[1]{0:T(128)} %bitcast.place_ref, f32[512,256]{1,0:T(8,128)S(1)} %get-tuple-element.38.refs_0_, bf16[512,256]{1,0:T(8,128)(2,1)S(1)} %collective-permute-done.24.refs_1_, bf16[512,256]{1,0:T(8,128)(2,1)S(1)} %collective-permute-done.26.refs_2_, ...), custom_call_target="tpu_custom_call" | custom-call | tf_op jit(solution)/shard_map/gate_cands/pallas_call | solution.py:313
  (57 shorter events, 2.6 us)
Async XLA Ops:
  0.6 16.0 %collective-permute-start.2 = (bf16[4,256,256]{2,1,0:T(8,128)(2,1)}, bf16[4,256,256]{2,1,0:T(8,128)(2,1)S(1)}, u32[]{:S(2)}, u32[]{:S(2)}) collective-permute-start(bf16[4,256,256]{2,1,0:T(8,128)(2,1)} %refs_0_.6), channel_id=1, source_target_pairs={{0,8},{4,12},{8,0},{12,4},{1,9},{5,13},{9,1},{13,5},{2,10},{6,14},... | collective-permute-start | bytes 1572872 | tf_op jit(solution)/shard_map/ppermute | solution.py:34
  3.7 13.0 %collective-permute-start = (bf16[4,256,256]{2,1,0:T(8,128)(2,1)}, bf16[4,256,256]{2,1,0:T(8,128)(2,1)S(1)}, u32[]{:S(2)}, u32[]{:S(2)}) collective-permute-start(bf16[4,256,256]{2,1,0:T(8,128)(2,1)} %refs_0_.6), channel_id=1, source_target_pairs={{0,4},{4,0},{8,12},{12,8},{1,5},{5,1},{9,13},{13,9},{2,6},{6,2},{1... | collective-permute-start | bytes 1572872 | tf_op jit(solution)/shard_map/ppermute | solution.py:34
  3.7 68.0 %collective-permute-start.13 = (bf16[512,256]{1,0:T(8,128)(2,1)}, bf16[512,256]{1,0:T(8,128)(2,1)S(1)}, u32[]{:S(2)}, u32[]{:S(2)}) collective-permute-start(bf16[512,256]{1,0:T(8,128)(2,1)} %refs_0_.7), channel_id=1, source_target_pairs={{0,8},{4,12},{8,0},{12,4},{1,9},{5,13},{9,1},{13,5},{2,10},{6,14},... | collective-permute-start | bytes 786440 | tf_op jit(solution)/shard_map/ppermute | solution.py:34
  16.7 14.0 %collective-permute-start.3 = (bf16[4,256,256]{2,1,0:T(8,128)(2,1)S(1)}, bf16[4,256,256]{2,1,0:T(8,128)(2,1)S(1)}, u32[]{:S(2)}, u32[]{:S(2)}) collective-permute-start(bf16[4,256,256]{2,1,0:T(8,128)(2,1)S(1)} %collective-permute-done.2.refs_0_.refs_2_), channel_id=1, source_target_pairs={{0,4},{4,0},{8,12},{12,8},{1,5},{5,1},{9,13},{13,9},{2,6},{6,2},{1... | collective-permute-start | bytes 1572872 | tf_op jit(solution)/shard_map/ppermute | solution.py:34
  30.6 24.9 %collective-permute-start.1 = (bf16[512,256]{1,0:T(8,128)(2,1)S(1)}, bf16[512,256]{1,0:T(8,128)(2,1)S(1)}, u32[]{:S(2)}, u32[]{:S(2)}) collective-permute-start(bf16[512,256]{1,0:T(8,128)(2,1)S(1)} %get-tuple-element.23), channel_id=1, source_target_pairs={{0,4},{4,0},{8,12},{12,8},{1,5},{5,1},{9,13},{13,9},{2,6},{6,2},{1... | collective-permute-start | bytes 786440 | tf_op jit(solution)/shard_map/ppermute | solution.py:34
  42.4 13.2 %collective-permute-start.4 = (bf16[512,256]{1,0:T(8,128)(2,1)S(1)}, bf16[512,256]{1,0:T(8,128)(2,1)S(1)}, u32[]{:S(2)}, u32[]{:S(2)}) collective-permute-start(bf16[512,256]{1,0:T(8,128)(2,1)S(1)} %get-tuple-element.24.refs_6_), channel_id=1, source_target_pairs={{0,8},{4,12},{8,0},{12,4},{1,9},{5,13},{9,1},{13,5},{2,10},{6,14},... | collective-permute-start | bytes 786440 | tf_op jit(solution)/shard_map/ppermute | solution.py:34
  42.5 14.4 %collective-permute-start.5 = (bf16[512,256]{1,0:T(8,128)(2,1)S(1)}, bf16[512,256]{1,0:T(8,128)(2,1)S(1)}, u32[]{:S(2)}, u32[]{:S(2)}) collective-permute-start(bf16[512,256]{1,0:T(8,128)(2,1)S(1)} %get-tuple-element.25), channel_id=1, source_target_pairs={{0,12},{4,8},{8,4},{12,0},{1,13},{5,9},{9,5},{13,1},{2,14},{6,10},... | collective-permute-start | bytes 786440 | tf_op jit(solution)/shard_map/ppermute | solution.py:34
  53.4 18.9 %collective-permute-start.6 = (bf16[256,256]{1,0:T(8,128)(2,1)S(1)}, bf16[256,256]{1,0:T(8,128)(2,1)S(1)}, u32[]{:S(2)}, u32[]{:S(2)}) collective-permute-start(bf16[256,256]{1,0:T(8,128)(2,1)S(1)} %get-tuple-element.27), channel_id=1, source_target_pairs={{0,4},{4,0},{8,12},{12,8},{1,5},{5,1},{9,13},{13,9},{2,6},{6,2},{1... | collective-permute-start | bytes 393224 | tf_op jit(solution)/shard_map/ppermute | solution.py:34
  55.5 18.0 %collective-permute-start.7 = (bf16[256,256]{1,0:T(8,128)(2,1)S(1)}, bf16[256,256]{1,0:T(8,128)(2,1)S(1)}, u32[]{:S(2)}, u32[]{:S(2)}) collective-permute-start(bf16[256,256]{1,0:T(8,128)(2,1)S(1)} %get-tuple-element.28), channel_id=1, source_target_pairs={{0,8},{4,12},{8,0},{12,4},{1,9},{5,13},{9,1},{13,5},{2,10},{6,14},... | collective-permute-start | bytes 393224 | tf_op jit(solution)/shard_map/ppermute | solution.py:34
  55.6 18.3 %collective-permute-start.8 = (bf16[256,256]{1,0:T(8,128)(2,1)S(1)}, bf16[256,256]{1,0:T(8,128)(2,1)S(1)}, u32[]{:S(2)}, u32[]{:S(2)}) collective-permute-start(bf16[256,256]{1,0:T(8,128)(2,1)S(1)} %get-tuple-element.29), channel_id=1, source_target_pairs={{0,12},{4,8},{8,4},{12,0},{1,13},{5,9},{9,5},{13,1},{2,14},{6,10},... | collective-permute-start | bytes 393224 | tf_op jit(solution)/shard_map/ppermute | solution.py:34
  57.4 18.1 %collective-permute-start.22 = (bf16[512,256]{1,0:T(8,128)(2,1)S(1)}, bf16[512,256]{1,0:T(8,128)(2,1)S(1)}, u32[]{:S(2)}, u32[]{:S(2)}) collective-permute-start(bf16[512,256]{1,0:T(8,128)(2,1)S(1)} %shard_map.133.refs_6_.refs_0_), channel_id=1, source_target_pairs={{0,2},{1,3},{2,0},{3,1},{4,6},{5,7},{6,4},{7,5},{8,10},{9,11},{10,... | collective-permute-start | bytes 786440 | tf_op jit(solution)/shard_map/ppermute | solution.py:34
  60.6 37.0 %copy-start.2 = (bf16[1024,256]{1,0:T(8,128)(2,1)S(1)}, bf16[1024,256]{1,0:T(8,128)(2,1)}, u32[]{:S(2)}) copy-start(bf16[1024,256]{1,0:T(8,128)(2,1)} %refs_11_.1) | copy-start | bytes 1572868
  60.6 37.8 %copy-start.3 = (bf16[512,256]{1,0:T(8,128)(2,1)S(1)}, bf16[512,256]{1,0:T(8,128)(2,1)}, u32[]{:S(2)}) copy-start(bf16[512,256]{1,0:T(8,128)(2,1)} %refs_0_.7) | copy-start | bytes 786436
  60.6 45.8 %copy-start.6 = (s32[4]{0:T(128)S(1)}, s32[4]{0:T(128)}, u32[]{:S(2)}) copy-start(s32[4]{0:T(128)} %count_ref.5) | copy-start | bytes 52
  71.7 48.4 %copy-start.4 = (bf16[512,256]{1,0:T(8,128)(2,1)S(1)}, bf16[512,256]{1,0:T(8,128)(2,1)}, u32[]{:S(2)}) copy-start(bf16[512,256]{1,0:T(8,128)(2,1)} %refs_4_.7) | copy-start | bytes 786436
  71.7 48.4 %copy-start.7 = (f32[256]{0:T(256)S(1)}, f32[256]{0:T(256)}, u32[]{:S(2)}) copy-start(f32[256]{0:T(256)} %param.23) | copy-start | bytes 3076
  71.7 6.4 %collective-permute-start.10 = (bf16[256,256]{1,0:T(8,128)(2,1)S(1)}, bf16[256,256]{1,0:T(8,128)(2,1)S(1)}, u32[]{:S(2)}, u32[]{:S(2)}) collective-permute-start(bf16[256,256]{1,0:T(8,128)(2,1)S(1)} %get-tuple-element.32), channel_id=1, source_target_pairs={{0,8},{4,12},{8,0},{12,4},{1,9},{5,13},{9,1},{13,5},{2,10},{6,14},... | collective-permute-start | bytes 393224 | tf_op jit(solution)/shard_map/ppermute | solution.py:34
  72.4 7.5 %collective-permute-start.11 = (bf16[256,256]{1,0:T(8,128)(2,1)S(1)}, bf16[256,256]{1,0:T(8,128)(2,1)S(1)}, u32[]{:S(2)}, u32[]{:S(2)}) collective-permute-start(bf16[256,256]{1,0:T(8,128)(2,1)S(1)} %get-tuple-element.33), channel_id=1, source_target_pairs={{0,12},{4,8},{8,4},{12,0},{1,13},{5,9},{9,5},{13,1},{2,14},{6,10},... | collective-permute-start | bytes 393224 | tf_op jit(solution)/shard_map/ppermute | solution.py:34
  73.5 6.9 %collective-permute-start.9 = (bf16[256,256]{1,0:T(8,128)(2,1)S(1)}, bf16[256,256]{1,0:T(8,128)(2,1)S(1)}, u32[]{:S(2)}, u32[]{:S(2)}) collective-permute-start(bf16[256,256]{1,0:T(8,128)(2,1)S(1)} %get-tuple-element.31), channel_id=1, source_target_pairs={{0,4},{4,0},{8,12},{12,8},{1,5},{5,1},{9,13},{13,9},{2,6},{6,2},{1... | collective-permute-start | bytes 393224 | tf_op jit(solution)/shard_map/ppermute | solution.py:34
  73.9 21.6 %collective-permute-start.21 = (bf16[512,256]{1,0:T(8,128)(2,1)S(1)}, bf16[512,256]{1,0:T(8,128)(2,1)S(1)}, u32[]{:S(2)}, u32[]{:S(2)}) collective-permute-start(bf16[512,256]{1,0:T(8,128)(2,1)S(1)} %shard_map.133.refs_6_.refs_0_), channel_id=1, source_target_pairs={{0,1},{1,0},{2,3},{3,2},{4,5},{5,4},{6,7},{7,6},{8,9},{9,8},{10,11... | collective-permute-start | bytes 786440 | tf_op jit(solution)/shard_map/ppermute | solution.py:34
  75.5 22.0 %collective-permute-start.23 = (bf16[512,256]{1,0:T(8,128)(2,1)S(1)}, bf16[512,256]{1,0:T(8,128)(2,1)S(1)}, u32[]{:S(2)}, u32[]{:S(2)}) collective-permute-start(bf16[512,256]{1,0:T(8,128)(2,1)S(1)} %collective-permute-done.22.refs_2_), channel_id=1, source_target_pairs={{0,1},{1,0},{2,3},{3,2},{4,5},{5,4},{6,7},{7,6},{8,9},{9,8},{10,11... | collective-permute-start | bytes 786440 | tf_op jit(solution)/shard_map/ppermute | solution.py:34
  78.1 20.2 %collective-permute-start.14 = (bf16[512,256]{1,0:T(8,128)(2,1)S(1)}, bf16[512,256]{1,0:T(8,128)(2,1)S(1)}, u32[]{:S(2)}, u32[]{:S(2)}) collective-permute-start(bf16[512,256]{1,0:T(8,128)(2,1)S(1)} %collective-permute-done.13.refs_0_), channel_id=1, source_target_pairs={{0,4},{4,0},{8,12},{12,8},{1,5},{5,1},{9,13},{13,9},{2,6},{6,2},{1... | collective-permute-start | bytes 786440 | tf_op jit(solution)/shard_map/ppermute | solution.py:34
  79.8 10.8 %collective-permute-start.16 = (bf16[256,256]{1,0:T(8,128)(2,1)S(1)}, bf16[256,256]{1,0:T(8,128)(2,1)S(1)}, u32[]{:S(2)}, u32[]{:S(2)}) collective-permute-start(bf16[256,256]{1,0:T(8,128)(2,1)S(1)} %shard_map.135.refs_2_), channel_id=1, source_target_pairs={{0,2},{1,3},{2,0},{3,1},{4,6},{5,7},{6,4},{7,5},{8,10},{9,11},{10,... | collective-permute-start | bytes 393224 | tf_op jit(solution)/shard_map/ppermute | solution.py:34
  80.7 14.8 %collective-permute-start.19 = (bf16[256,256]{1,0:T(8,128)(2,1)S(1)}, bf16[256,256]{1,0:T(8,128)(2,1)}, u32[]{:S(2)}, u32[]{:S(2)}) collective-permute-start(bf16[256,256]{1,0:T(8,128)(2,1)S(1)} %shard_map.137.refs_6_), channel_id=1, source_target_pairs={{0,2},{1,3},{2,0},{3,1},{4,6},{5,7},{6,4},{7,5},{8,10},{9,11},{10,... | collective-permute-start | bytes 393224 | tf_op jit(solution)/shard_map/ppermute | solution.py:34
  90.6 7.8 %collective-permute-start.15 = (bf16[256,256]{1,0:T(8,128)(2,1)S(1)}, bf16[256,256]{1,0:T(8,128)(2,1)}, u32[]{:S(2)}, u32[]{:S(2)}) collective-permute-start(bf16[256,256]{1,0:T(8,128)(2,1)S(1)} %shard_map.135.refs_2_), channel_id=1, source_target_pairs={{0,1},{1,0},{2,3},{3,2},{4,5},{5,4},{6,7},{7,6},{8,9},{9,8},{10,11... | collective-permute-start | bytes 393224 | tf_op jit(solution)/shard_map/ppermute | solution.py:34
  95.5 6.5 %collective-permute-start.17 = (bf16[256,256]{1,0:T(8,128)(2,1)S(1)}, bf16[256,256]{1,0:T(8,128)(2,1)}, u32[]{:S(2)}, u32[]{:S(2)}) collective-permute-start(bf16[256,256]{1,0:T(8,128)(2,1)S(1)} %collective-permute-done.16.refs_4_), channel_id=1, source_target_pairs={{0,1},{1,0},{2,3},{3,2},{4,5},{5,4},{6,7},{7,6},{8,9},{9,8},{10,11... | collective-permute-start | bytes 393224 | tf_op jit(solution)/shard_map/ppermute | solution.py:34
  95.5 9.3 %collective-permute-start.18 = (bf16[256,256]{1,0:T(8,128)(2,1)S(1)}, bf16[256,256]{1,0:T(8,128)(2,1)}, u32[]{:S(2)}, u32[]{:S(2)}) collective-permute-start(bf16[256,256]{1,0:T(8,128)(2,1)S(1)} %shard_map.137.refs_6_), channel_id=1, source_target_pairs={{0,1},{1,0},{2,3},{3,2},{4,5},{5,4},{6,7},{7,6},{8,9},{9,8},{10,11... | collective-permute-start | bytes 393224 | tf_op jit(solution)/shard_map/ppermute | solution.py:34
  97.5 8.8 %collective-permute-start.20 = (bf16[256,256]{1,0:T(8,128)(2,1)}, bf16[256,256]{1,0:T(8,128)(2,1)}, u32[]{:S(2)}, u32[]{:S(2)}) collective-permute-start(bf16[256,256]{1,0:T(8,128)(2,1)} %collective-permute-done.19.refs_8_), channel_id=1, source_target_pairs={{0,1},{1,0},{2,3},{3,2},{4,5},{5,4},{6,7},{7,6},{8,9},{9,8},{10,11... | collective-permute-start | bytes 393224 | tf_op jit(solution)/shard_map/ppermute | solution.py:34
  98.3 11.3 %collective-permute-start.12 = (bf16[512,256]{1,0:T(8,128)(2,1)S(1)}, bf16[512,256]{1,0:T(8,128)(2,1)S(1)}, u32[]{:S(2)}, u32[]{:S(2)}) collective-permute-start(bf16[512,256]{1,0:T(8,128)(2,1)S(1)} %copy-done.3), channel_id=1, source_target_pairs={{0,4},{4,0},{8,12},{12,8},{1,5},{5,1},{9,13},{13,9},{2,6},{6,2},{1... | collective-permute-start | bytes 786440 | tf_op jit(solution)/shard_map/ppermute | solution.py:34
  109.6 2.2 %collective-permute-start.25 = (bf16[512,256]{1,0:T(8,128)(2,1)S(1)}, bf16[512,256]{1,0:T(8,128)(2,1)S(1)}, u32[]{:S(2)}, u32[]{:S(2)}) collective-permute-start(bf16[512,256]{1,0:T(8,128)(2,1)S(1)} %get-tuple-element.41), channel_id=1, source_target_pairs={{0,4},{4,0},{8,12},{12,8},{1,5},{5,1},{9,13},{13,9},{2,6},{6,2},{1... | collective-permute-start | bytes 786440 | tf_op jit(solution)/shard_map/ppermute | solution.py:34
  111.2 2.0 %collective-permute-start.24 = (bf16[512,256]{1,0:T(8,128)(2,1)S(1)}, bf16[512,256]{1,0:T(8,128)(2,1)S(1)}, u32[]{:S(2)}, u32[]{:S(2)}) collective-permute-start(bf16[512,256]{1,0:T(8,128)(2,1)S(1)} %get-tuple-element.39), channel_id=1, source_target_pairs={{0,4},{4,0},{8,12},{12,8},{1,5},{5,1},{9,13},{13,9},{2,6},{6,2},{1... | collective-permute-start | bytes 786440 | tf_op jit(solution)/shard_map/ppermute | solution.py:34
  111.8 8.3 %collective-permute-start.26 = (bf16[512,256]{1,0:T(8,128)(2,1)S(1)}, bf16[512,256]{1,0:T(8,128)(2,1)S(1)}, u32[]{:S(2)}, u32[]{:S(2)}) collective-permute-start(bf16[512,256]{1,0:T(8,128)(2,1)S(1)} %add_convert_fusion), channel_id=1, source_target_pairs={{0,8},{4,12},{8,0},{12,4},{1,9},{5,13},{9,1},{13,5},{2,10},{6,14},... | collective-permute-start | bytes 786440 | tf_op jit(solution)/shard_map/ppermute | solution.py:34
  (6 other events, 93.4 us)

commit v4 on v3

--- a/solution.py
+++ b/solution.py
@@ -16,7 +16,7 @@
 ANY = pl.BlockSpec(memory_space=pl.ANY)
 INSIDE = pl.BlockSpec(memory_space=pltpu.VMEM)
 SMALL = pltpu.CompilerParams(vmem_limit_bytes=12 << 20)
-LARGE = pltpu.CompilerParams(vmem_limit_bytes=20 << 20)
+LARGE = pltpu.CompilerParams(vmem_limit_bytes=14 << 20)
 
 
 def qk(q, k):
@@ -376,10 +376,11 @@
         got01 = exchange(near01, 1)
         far01 = attend_first(2, queries[2:], False, True, *hist, (own01,))
         got01 = got01 + exchange(far01, 2)
-        out2 = attend(2, heads, queries, True, *hist, (far01[0],))
+        late = [pltpu.with_memory_space_constraint(q, pltpu.HBM) for q in queries]
+        out2 = attend(2, heads, late, True, *hist, (far01[0],))
         got2 = exchange(out2[1:], 1)
         gated01 = gate_chunk((own01, 0), [(x, 0) for x in got01], 4, 0)
-        out3 = attend(3, heads, queries, True, *hist, (gated01, out2[0]))
+        out3 = attend(3, heads, late, True, *hist, (gated01, out2[0]))
         got3 = exchange(out3[1:], 1)
         gated2 = gate_chunk((out2[0], 0), [(x, 0) for x in got2], 2, 4)
         gated3 = gate_chunk((out3[0], 0), [(x, 0) for x in got3], 2, 6)

time: 122 us -> 123 us (level)
  no operation moved by 1% of the time
where the time goes in v4:
time: 123 us; the launch traced here: 122 us
  Pallas kernels  55.4 us (45%)
  waiting for transfers between devices  42.7 us (35%)
  starting transfers between devices  21.7 us (18%)
    ppermute x27, waiting for transfers between devices, swap(): return lax.ppermute(x, axis, [(i, i ^ j) for i in range(size)])  42.7 us
    pallas_call x2, Pallas kernels, attend_first(): pl.pallas_call(kern, grid_spec=pltpu.PrefetchScalarGridSpec(num_scalar_pr...  25 us
    pallas_call x2, Pallas kernels, attend(): pl.pallas_call(kern, grid_spec=pltpu.PrefetchScalarGridSpec(num_scalar_pr...  22.2 us
    ppermute x27, starting transfers between devices, swap(): return lax.ppermute(x, axis, [(i, i ^ j) for i in range(size)])  21.7 us
    pallas_call x2, Pallas kernels, cand_sums(): pl.pallas_call(kern, grid_spec=pltpu.PrefetchScalarGridSpec(num_scalar_pr...  4.74 us
  transfers between devices with their start and end apart: 27, of which 9 were waited for; matrix products, arithmetic and copies ran while one was open for 1% of the time, Pallas kernels for 44%

profile of v4, /device:TPU:0, one launch (start us, length us, event | category | flops | bytes accessed | tf_op | source)
XLA Modules:
  0.0 122.4 jit_solution(14336819009035279832)
XLA Ops:
  0.6 3.1 %collective-permute-start.2 = (bf16[4,256,256]{2,1,0:T(8,128)(2,1)}, bf16[4,256,256]{2,1,0:T(8,128)(2,1)S(1)}, u32[]{:S(2)}, u32[]{:S(2)}) collective-permute-start(bf16[4,256,256]{2,1,0:T(8,128)(2,1)} %refs_0_.6), channel_id=1, source_target_pairs={{0,8},{4,12},{8,0},{12,4},{1,9},{5,13},{9,1},{13,5},{2,10},{6,14},... | collective-permute-start | bytes 1572872 | tf_op jit(solution)/shard_map/ppermute | solution.py:34
  3.9 12.8 %collective-permute-done.2.refs_0_.refs_2_ = bf16[4,256,256]{2,1,0:T(8,128)(2,1)S(1)} collective-permute-done((bf16[4,256,256]{2,1,0:T(8,128)(2,1)}, bf16[4,256,256]{2,1,0:T(8,128)(2,1)S(1)}, u32[]{:S(2)}, u32[]{:S(2)}) %collective-permute-start.2) | collective-permute-done | bytes 524320 | tf_op jit(solution)/shard_map/ppermute | solution.py:34
  16.7 0.7 copy-done.13
  17.4 13.3 %shard_map.131 = (f32[512,256]{1,0:T(8,128)S(1)}, bf16[512,256]{1,0:T(8,128)(2,1)S(1)}) custom-call(s32[4]{0:T(128)S(1)} %copy-done.13, s32[1]{0:T(128)} %bitcast.place_ref, bf16[4,256,256]{2,1,0:T(8,128)(2,1)} %refs_0_.6, bf16[4,256,256]{2,1,0:T(8,128)(2,1)S(1)} %collective-permute-done.refs_1_, bf16[4,4096,256]{2,1,0:T(8,128)(2,1)} %refs_4_.5, ...), custom_call_target="tpu_custom_call" | custom-call | flops 8589934592 | bytes 8388608 | tf_op jit(solution)/shard_map/pallas_call | solution.py:94
  30.8 11.7 %shard_map.132 = (bf16[512,256]{1,0:T(8,128)(2,1)S(1)}, bf16[512,256]{1,0:T(8,128)(2,1)S(1)}) custom-call(s32[4]{0:T(128)S(1)} %copy-done.13, s32[1]{0:T(128)} %bitcast.place_ref, bf16[4,256,256]{2,1,0:T(8,128)(2,1)S(1)} %collective-permute-done.2.refs_0_.refs_2_, bf16[4,256,256]{2,1,0:T(8,128)(2,1)S(1)} %collective-permute-done.3.refs_1_.refs_3_, ...), custom_call_target="tpu_custom_call" | custom-call | flops 8589934592 | bytes 8388608 | tf_op jit(solution)/shard_map/pallas_call | solution.py:94
  42.7 11.0 %shard_map.134 = (f32[256,256]{1,0:T(8,128)S(1)}, bf16[256,256]{1,0:T(8,128)(2,1)S(1)}, bf16[256,256]{1,0:T(8,128)(2,1)S(1)}, bf16[256,256]{1,0:T(8,128)(2,1)S(1)}) custom-call(s32[4]{0:T(128)S(1)} %copy-done.13, s32[1]{0:T(128)} %bitcast.place_ref, bf16[4,256,256]{2,1,0:T(8,128)(2,1)} %refs_0_.6, bf16[4,256,256]{2,1,0:T(8,128)(2,1)} %copy-done.11, ...), custom_call_target="tpu_custom_call" | custom-call | flops 8589934592 | bytes 4194304 | tf_op jit(solution)/shard_map/pallas_call | solution.py:142
  53.7 2.1 %collective-permute-start.6 = (bf16[256,256]{1,0:T(8,128)(2,1)S(1)}, bf16[256,256]{1,0:T(8,128)(2,1)S(1)}, u32[]{:S(2)}, u32[]{:S(2)}) collective-permute-start(bf16[256,256]{1,0:T(8,128)(2,1)S(1)} %get-tuple-element.27), channel_id=1, source_target_pairs={{0,4},{4,0},{8,12},{12,8},{1,5},{5,1},{9,13},{13,9},{2,6},{6,2},{1... | collective-permute-start | bytes 393224 | tf_op jit(solution)/shard_map/ppermute | solution.py:34
  55.9 1.3 %collective-permute-start.8 = (bf16[256,256]{1,0:T(8,128)(2,1)S(1)}, bf16[256,256]{1,0:T(8,128)(2,1)S(1)}, u32[]{:S(2)}, u32[]{:S(2)}) collective-permute-start(bf16[256,256]{1,0:T(8,128)(2,1)S(1)} %get-tuple-element.29), channel_id=1, source_target_pairs={{0,12},{4,8},{8,4},{12,0},{1,13},{5,9},{9,5},{13,1},{2,14},{6,10},... | collective-permute-start | bytes 393224 | tf_op jit(solution)/shard_map/ppermute | solution.py:34
  57.7 3.2 %collective-permute-start.22 = (bf16[512,256]{1,0:T(8,128)(2,1)S(1)}, bf16[512,256]{1,0:T(8,128)(2,1)S(1)}, u32[]{:S(2)}, u32[]{:S(2)}) collective-permute-start(bf16[512,256]{1,0:T(8,128)(2,1)S(1)} %shard_map.133.refs_6_.refs_0_), channel_id=1, source_target_pairs={{0,2},{1,3},{2,0},{3,1},{4,6},{5,7},{6,4},{7,5},{8,10},{9,11},{10,... | collective-permute-start | bytes 786440 | tf_op jit(solution)/shard_map/ppermute | solution.py:34
  60.8 11.2 %shard_map.136 = (f32[256,256]{1,0:T(8,128)S(1)}, bf16[256,256]{1,0:T(8,128)(2,1)S(1)}, bf16[256,256]{1,0:T(8,128)(2,1)S(1)}, bf16[256,256]{1,0:T(8,128)(2,1)S(1)}) custom-call(s32[4]{0:T(128)S(1)} %copy-done.13, s32[1]{0:T(128)} %bitcast.place_ref, bf16[4,256,256]{2,1,0:T(8,128)(2,1)} %refs_0_.6, bf16[4,256,256]{2,1,0:T(8,128)(2,1)} %copy-done.11, ...), custom_call_target="tpu_custom_call" | custom-call | flops 8589934592 | bytes 4194304 | tf_op jit(solution)/shard_map/pallas_call | solution.py:142
  72.1 0.7 collective-permute-start.10
  72.8 1.2 collective-permute-start.11
  74.3 1.6 %collective-permute-start.21 = (bf16[512,256]{1,0:T(8,128)(2,1)S(1)}, bf16[512,256]{1,0:T(8,128)(2,1)S(1)}, u32[]{:S(2)}, u32[]{:S(2)}) collective-permute-start(bf16[512,256]{1,0:T(8,128)(2,1)S(1)} %shard_map.133.refs_6_.refs_0_), channel_id=1, source_target_pairs={{0,1},{1,0},{2,3},{3,2},{4,5},{5,4},{6,7},{7,6},{8,9},{9,8},{10,11... | collective-permute-start | bytes 786440 | tf_op jit(solution)/shard_map/ppermute | solution.py:34
  76.6 1.9 %collective-permute-done.10.refs_1_ = bf16[256,256]{1,0:T(8,128)(2,1)S(1)} collective-permute-done((bf16[256,256]{1,0:T(8,128)(2,1)S(1)}, bf16[256,256]{1,0:T(8,128)(2,1)S(1)}, u32[]{:S(2)}, u32[]{:S(2)}) %collective-permute-start.10) | collective-permute-done | bytes 131104 | tf_op jit(solution)/shard_map/ppermute | solution.py:34
  78.6 1.7 %collective-permute-done.11.refs_2_ = bf16[256,256]{1,0:T(8,128)(2,1)S(1)} collective-permute-done((bf16[256,256]{1,0:T(8,128)(2,1)S(1)}, bf16[256,256]{1,0:T(8,128)(2,1)S(1)}, u32[]{:S(2)}, u32[]{:S(2)}) %collective-permute-start.11) | collective-permute-done | bytes 131104 | tf_op jit(solution)/shard_map/ppermute | solution.py:34
  80.3 0.6 collective-permute-start.16
  81.1 2.4 %collective-permute-start.19 = (bf16[256,256]{1,0:T(8,128)(2,1)S(1)}, bf16[256,256]{1,0:T(8,128)(2,1)}, u32[]{:S(2)}, u32[]{:S(2)}) collective-permute-start(bf16[256,256]{1,0:T(8,128)(2,1)S(1)} %shard_map.137.refs_6_), channel_id=1, source_target_pairs={{0,2},{1,3},{2,0},{3,1},{4,6},{5,7},{6,4},{7,5},{8,10},{9,11},{10,... | collective-permute-start | bytes 393224 | tf_op jit(solution)/shard_map/ppermute | solution.py:34
  83.5 7.5 %collective-permute-done.16.refs_4_ = bf16[256,256]{1,0:T(8,128)(2,1)S(1)} collective-permute-done((bf16[256,256]{1,0:T(8,128)(2,1)S(1)}, bf16[256,256]{1,0:T(8,128)(2,1)S(1)}, u32[]{:S(2)}, u32[]{:S(2)}) %collective-permute-start.16) | collective-permute-done | bytes 131104 | tf_op jit(solution)/shard_map/ppermute | solution.py:34
  91.0 1.1 collective-permute-start.15
  92.1 3.8 %collective-permute-done.19.refs_8_ = bf16[256,256]{1,0:T(8,128)(2,1)} collective-permute-done((bf16[256,256]{1,0:T(8,128)(2,1)S(1)}, bf16[256,256]{1,0:T(8,128)(2,1)}, u32[]{:S(2)}, u32[]{:S(2)}) %collective-permute-start.19) | collective-permute-done | bytes 131104 | tf_op jit(solution)/shard_map/ppermute | solution.py:34
  95.9 2.0 %collective-permute-start.18 = (bf16[256,256]{1,0:T(8,128)(2,1)S(1)}, bf16[256,256]{1,0:T(8,128)(2,1)}, u32[]{:S(2)}, u32[]{:S(2)}) collective-permute-start(bf16[256,256]{1,0:T(8,128)(2,1)S(1)} %shard_map.137.refs_6_), channel_id=1, source_target_pairs={{0,1},{1,0},{2,3},{3,2},{4,5},{5,4},{6,7},{7,6},{8,9},{9,8},{10,11... | collective-permute-start | bytes 393224 | tf_op jit(solution)/shard_map/ppermute | solution.py:34
  98.0 0.7 early_keys.1
  98.9 3.5 %collective-permute-done.17.refs_5_ = bf16[256,256]{1,0:T(8,128)(2,1)} collective-permute-done((bf16[256,256]{1,0:T(8,128)(2,1)S(1)}, bf16[256,256]{1,0:T(8,128)(2,1)}, u32[]{:S(2)}, u32[]{:S(2)}) %collective-permute-start.17) | collective-permute-done | bytes 131104 | tf_op jit(solution)/shard_map/ppermute | solution.py:34
  102.4 2.8 %collective-permute-done.18.refs_7_ = bf16[256,256]{1,0:T(8,128)(2,1)} collective-permute-done((bf16[256,256]{1,0:T(8,128)(2,1)S(1)}, bf16[256,256]{1,0:T(8,128)(2,1)}, u32[]{:S(2)}, u32[]{:S(2)}) %collective-permute-start.18) | collective-permute-done | bytes 131104 | tf_op jit(solution)/shard_map/ppermute | solution.py:34
  105.2 1.6 %collective-permute-done.20.refs_9_ = bf16[256,256]{1,0:T(8,128)(2,1)} collective-permute-done((bf16[256,256]{1,0:T(8,128)(2,1)}, bf16[256,256]{1,0:T(8,128)(2,1)}, u32[]{:S(2)}, u32[]{:S(2)}) %collective-permute-start.20) | collective-permute-done | bytes 131104 | tf_op jit(solution)/shard_map/ppermute | solution.py:34
  106.8 3.2 %shard_map.138 = (f32[512,256]{1,0:T(8,128)S(1)}, bf16[512,256]{1,0:T(8,128)(2,1)S(1)}, bf16[1024,256]{1,0:T(8,128)(2,1)S(1)}, bf16[1024,256]{1,0:T(8,128)(2,1)S(1)}) custom-call(s32[4]{0:T(128)S(1)} %copy-done.6, s32[1]{0:T(128)} %bitcast.place_ref, s32[1]{0:T(128)} %bitcast.4.col_ref, bf16[512,256]{1,0:T(8,128)(2,1)S(1)} %collective-permute-done.13.refs_0_, ...), custom_call_target="tpu_custom_call" | custom-call | tf_op jit(solution)/shard_map/pallas_call | solution.py:278
  110.1 1.5 %shard_map.139 = (f32[512,256]{1,0:T(8,128)S(1)}, bf16[512,256]{1,0:T(8,128)(2,1)S(1)}) custom-call(s32[4]{0:T(128)S(1)} %copy-done.6, s32[1]{0:T(128)} %bitcast.place_ref, s32[1]{0:T(128)} %bitcast.4.col_ref, bf16[512,256]{1,0:T(8,128)(2,1)S(1)} %copy-done.3, bf16[512,256]{1,0:T(8,128)(2,1)S(1)} %collective-permute-done.12.refs_1_, ...), custom_call_target="tpu_custom_call" | custom-call | tf_op jit(solution)/shard_map/pallas_call | solution.py:278
  111.6 0.6 collective-permute-start.24
  112.2 0.5 collective-permute-start.26
  112.8 0.8 pad_maximum_fusion
  113.6 6.9 %collective-permute-done.26.refs_2_ = bf16[512,256]{1,0:T(8,128)(2,1)S(1)} collective-permute-done((bf16[512,256]{1,0:T(8,128)(2,1)S(1)}, bf16[512,256]{1,0:T(8,128)(2,1)S(1)}, u32[]{:S(2)}, u32[]{:S(2)}) %collective-permute-start.26) | collective-permute-done | bytes 262176 | tf_op jit(solution)/shard_map/ppermute | solution.py:34
  120.5 1.9 %gate_cands.1 = bf16[512,256]{1,0:T(8,128)(2,1)} custom-call(s32[4]{0:T(128)S(1)} %copy-done.6, s32[1]{0:T(128)} %bitcast.place_ref, f32[512,256]{1,0:T(8,128)S(1)} %get-tuple-element.38.refs_0_, bf16[512,256]{1,0:T(8,128)(2,1)S(1)} %collective-permute-done.24.refs_1_, bf16[512,256]{1,0:T(8,128)(2,1)S(1)} %collective-permute-done.26.refs_2_, ...), custom_call_target="tpu_custom_call" | custom-call | tf_op jit(solution)/shard_map/gate_cands/pallas_call | solution.py:313
  (63 shorter events, 2.6 us)
Async XLA Ops:
  0.6 16.0 %collective-permute-start.2 = (bf16[4,256,256]{2,1,0:T(8,128)(2,1)}, bf16[4,256,256]{2,1,0:T(8,128)(2,1)S(1)}, u32[]{:S(2)}, u32[]{:S(2)}) collective-permute-start(bf16[4,256,256]{2,1,0:T(8,128)(2,1)} %refs_0_.6), channel_id=1, source_target_pairs={{0,8},{4,12},{8,0},{12,4},{1,9},{5,13},{9,1},{13,5},{2,10},{6,14},... | collective-permute-start | bytes 1572872 | tf_op jit(solution)/shard_map/ppermute | solution.py:34
  3.7 13.0 %collective-permute-start = (bf16[4,256,256]{2,1,0:T(8,128)(2,1)}, bf16[4,256,256]{2,1,0:T(8,128)(2,1)S(1)}, u32[]{:S(2)}, u32[]{:S(2)}) collective-permute-start(bf16[4,256,256]{2,1,0:T(8,128)(2,1)} %refs_0_.6), channel_id=1, source_target_pairs={{0,4},{4,0},{8,12},{12,8},{1,5},{5,1},{9,13},{13,9},{2,6},{6,2},{1... | collective-permute-start | bytes 1572872 | tf_op jit(solution)/shard_map/ppermute | solution.py:34
  3.7 68.4 %collective-permute-start.13 = (bf16[512,256]{1,0:T(8,128)(2,1)}, bf16[512,256]{1,0:T(8,128)(2,1)S(1)}, u32[]{:S(2)}, u32[]{:S(2)}) collective-permute-start(bf16[512,256]{1,0:T(8,128)(2,1)} %refs_0_.7), channel_id=1, source_target_pairs={{0,8},{4,12},{8,0},{12,4},{1,9},{5,13},{9,1},{13,5},{2,10},{6,14},... | collective-permute-start | bytes 786440 | tf_op jit(solution)/shard_map/ppermute | solution.py:34
  16.7 14.1 %collective-permute-start.3 = (bf16[4,256,256]{2,1,0:T(8,128)(2,1)S(1)}, bf16[4,256,256]{2,1,0:T(8,128)(2,1)S(1)}, u32[]{:S(2)}, u32[]{:S(2)}) collective-permute-start(bf16[4,256,256]{2,1,0:T(8,128)(2,1)S(1)} %collective-permute-done.2.refs_0_.refs_2_), channel_id=1, source_target_pairs={{0,4},{4,0},{8,12},{12,8},{1,5},{5,1},{9,13},{13,9},{2,6},{6,2},{1... | collective-permute-start | bytes 1572872 | tf_op jit(solution)/shard_map/ppermute | solution.py:34
  30.7 25.1 %collective-permute-start.1 = (bf16[512,256]{1,0:T(8,128)(2,1)S(1)}, bf16[512,256]{1,0:T(8,128)(2,1)S(1)}, u32[]{:S(2)}, u32[]{:S(2)}) collective-permute-start(bf16[512,256]{1,0:T(8,128)(2,1)S(1)} %get-tuple-element.23), channel_id=1, source_target_pairs={{0,4},{4,0},{8,12},{12,8},{1,5},{5,1},{9,13},{13,9},{2,6},{6,2},{1... | collective-permute-start | bytes 786440 | tf_op jit(solution)/shard_map/ppermute | solution.py:34
  42.5 13.4 %collective-permute-start.4 = (bf16[512,256]{1,0:T(8,128)(2,1)S(1)}, bf16[512,256]{1,0:T(8,128)(2,1)S(1)}, u32[]{:S(2)}, u32[]{:S(2)}) collective-permute-start(bf16[512,256]{1,0:T(8,128)(2,1)S(1)} %get-tuple-element.24.refs_6_), channel_id=1, source_target_pairs={{0,8},{4,12},{8,0},{12,4},{1,9},{5,13},{9,1},{13,5},{2,10},{6,14},... | collective-permute-start | bytes 786440 | tf_op jit(solution)/shard_map/ppermute | solution.py:34
  42.6 14.6 %collective-permute-start.5 = (bf16[512,256]{1,0:T(8,128)(2,1)S(1)}, bf16[512,256]{1,0:T(8,128)(2,1)S(1)}, u32[]{:S(2)}, u32[]{:S(2)}) collective-permute-start(bf16[512,256]{1,0:T(8,128)(2,1)S(1)} %get-tuple-element.25), channel_id=1, source_target_pairs={{0,12},{4,8},{8,4},{12,0},{1,13},{5,9},{9,5},{13,1},{2,14},{6,10},... | collective-permute-start | bytes 786440 | tf_op jit(solution)/shard_map/ppermute | solution.py:34
  53.7 19.1 %collective-permute-start.6 = (bf16[256,256]{1,0:T(8,128)(2,1)S(1)}, bf16[256,256]{1,0:T(8,128)(2,1)S(1)}, u32[]{:S(2)}, u32[]{:S(2)}) collective-permute-start(bf16[256,256]{1,0:T(8,128)(2,1)S(1)} %get-tuple-element.27), channel_id=1, source_target_pairs={{0,4},{4,0},{8,12},{12,8},{1,5},{5,1},{9,13},{13,9},{2,6},{6,2},{1... | collective-permute-start | bytes 393224 | tf_op jit(solution)/shard_map/ppermute | solution.py:34
  55.8 18.2 %collective-permute-start.7 = (bf16[256,256]{1,0:T(8,128)(2,1)S(1)}, bf16[256,256]{1,0:T(8,128)(2,1)S(1)}, u32[]{:S(2)}, u32[]{:S(2)}) collective-permute-start(bf16[256,256]{1,0:T(8,128)(2,1)S(1)} %get-tuple-element.28), channel_id=1, source_target_pairs={{0,8},{4,12},{8,0},{12,4},{1,9},{5,13},{9,1},{13,5},{2,10},{6,14},... | collective-permute-start | bytes 393224 | tf_op jit(solution)/shard_map/ppermute | solution.py:34
  55.9 18.4 %collective-permute-start.8 = (bf16[256,256]{1,0:T(8,128)(2,1)S(1)}, bf16[256,256]{1,0:T(8,128)(2,1)S(1)}, u32[]{:S(2)}, u32[]{:S(2)}) collective-permute-start(bf16[256,256]{1,0:T(8,128)(2,1)S(1)} %get-tuple-element.29), channel_id=1, source_target_pairs={{0,12},{4,8},{8,4},{12,0},{1,13},{5,9},{9,5},{13,1},{2,14},{6,10},... | collective-permute-start | bytes 393224 | tf_op jit(solution)/shard_map/ppermute | solution.py:34
  57.7 18.3 %collective-permute-start.22 = (bf16[512,256]{1,0:T(8,128)(2,1)S(1)}, bf16[512,256]{1,0:T(8,128)(2,1)S(1)}, u32[]{:S(2)}, u32[]{:S(2)}) collective-permute-start(bf16[512,256]{1,0:T(8,128)(2,1)S(1)} %shard_map.133.refs_6_.refs_0_), channel_id=1, source_target_pairs={{0,2},{1,3},{2,0},{3,1},{4,6},{5,7},{6,4},{7,5},{8,10},{9,11},{10,... | collective-permute-start | bytes 786440 | tf_op jit(solution)/shard_map/ppermute | solution.py:34
  60.8 37.2 %copy-start.2 = (bf16[1024,256]{1,0:T(8,128)(2,1)S(1)}, bf16[1024,256]{1,0:T(8,128)(2,1)}, u32[]{:S(2)}) copy-start(bf16[1024,256]{1,0:T(8,128)(2,1)} %refs_11_.1) | copy-start | bytes 1572868
  60.8 37.9 %copy-start.3 = (bf16[512,256]{1,0:T(8,128)(2,1)S(1)}, bf16[512,256]{1,0:T(8,128)(2,1)}, u32[]{:S(2)}) copy-start(bf16[512,256]{1,0:T(8,128)(2,1)} %refs_0_.7) | copy-start | bytes 786436
  60.8 45.9 %copy-start.6 = (s32[4]{0:T(128)S(1)}, s32[4]{0:T(128)}, u32[]{:S(2)}) copy-start(s32[4]{0:T(128)} %count_ref.5) | copy-start | bytes 52
  72.1 48.4 %copy-start.4 = (bf16[512,256]{1,0:T(8,128)(2,1)S(1)}, bf16[512,256]{1,0:T(8,128)(2,1)}, u32[]{:S(2)}) copy-start(bf16[512,256]{1,0:T(8,128)(2,1)} %refs_4_.7) | copy-start | bytes 786436
  72.1 48.4 %copy-start.7 = (f32[256]{0:T(256)S(1)}, f32[256]{0:T(256)}, u32[]{:S(2)}) copy-start(f32[256]{0:T(256)} %param.23) | copy-start | bytes 3076
  72.1 6.4 %collective-permute-start.10 = (bf16[256,256]{1,0:T(8,128)(2,1)S(1)}, bf16[256,256]{1,0:T(8,128)(2,1)S(1)}, u32[]{:S(2)}, u32[]{:S(2)}) collective-permute-start(bf16[256,256]{1,0:T(8,128)(2,1)S(1)} %get-tuple-element.32), channel_id=1, source_target_pairs={{0,8},{4,12},{8,0},{12,4},{1,9},{5,13},{9,1},{13,5},{2,10},{6,14},... | collective-permute-start | bytes 393224 | tf_op jit(solution)/shard_map/ppermute | solution.py:34
  72.8 7.5 %collective-permute-start.11 = (bf16[256,256]{1,0:T(8,128)(2,1)S(1)}, bf16[256,256]{1,0:T(8,128)(2,1)S(1)}, u32[]{:S(2)}, u32[]{:S(2)}) collective-permute-start(bf16[256,256]{1,0:T(8,128)(2,1)S(1)} %get-tuple-element.33), channel_id=1, source_target_pairs={{0,12},{4,8},{8,4},{12,0},{1,13},{5,9},{9,5},{13,1},{2,14},{6,10},... | collective-permute-start | bytes 393224 | tf_op jit(solution)/shard_map/ppermute | solution.py:34
  74.0 6.9 %collective-permute-start.9 = (bf16[256,256]{1,0:T(8,128)(2,1)S(1)}, bf16[256,256]{1,0:T(8,128)(2,1)S(1)}, u32[]{:S(2)}, u32[]{:S(2)}) collective-permute-start(bf16[256,256]{1,0:T(8,128)(2,1)S(1)} %get-tuple-element.31), channel_id=1, source_target_pairs={{0,4},{4,0},{8,12},{12,8},{1,5},{5,1},{9,13},{13,9},{2,6},{6,2},{1... | collective-permute-start | bytes 393224 | tf_op jit(solution)/shard_map/ppermute | solution.py:34
  74.3 21.6 %collective-permute-start.21 = (bf16[512,256]{1,0:T(8,128)(2,1)S(1)}, bf16[512,256]{1,0:T(8,128)(2,1)S(1)}, u32[]{:S(2)}, u32[]{:S(2)}) collective-permute-start(bf16[512,256]{1,0:T(8,128)(2,1)S(1)} %shard_map.133.refs_6_.refs_0_), channel_id=1, source_target_pairs={{0,1},{1,0},{2,3},{3,2},{4,5},{5,4},{6,7},{7,6},{8,9},{9,8},{10,11... | collective-permute-start | bytes 786440 | tf_op jit(solution)/shard_map/ppermute | solution.py:34
  75.9 22.0 %collective-permute-start.23 = (bf16[512,256]{1,0:T(8,128)(2,1)S(1)}, bf16[512,256]{1,0:T(8,128)(2,1)S(1)}, u32[]{:S(2)}, u32[]{:S(2)}) collective-permute-start(bf16[512,256]{1,0:T(8,128)(2,1)S(1)} %collective-permute-done.22.refs_2_), channel_id=1, source_target_pairs={{0,1},{1,0},{2,3},{3,2},{4,5},{5,4},{6,7},{7,6},{8,9},{9,8},{10,11... | collective-permute-start | bytes 786440 | tf_op jit(solution)/shard_map/ppermute | solution.py:34
  78.6 20.2 %collective-permute-start.14 = (bf16[512,256]{1,0:T(8,128)(2,1)S(1)}, bf16[512,256]{1,0:T(8,128)(2,1)S(1)}, u32[]{:S(2)}, u32[]{:S(2)}) collective-permute-start(bf16[512,256]{1,0:T(8,128)(2,1)S(1)} %collective-permute-done.13.refs_0_), channel_id=1, source_target_pairs={{0,4},{4,0},{8,12},{12,8},{1,5},{5,1},{9,13},{13,9},{2,6},{6,2},{1... | collective-permute-start | bytes 786440 | tf_op jit(solution)/shard_map/ppermute | solution.py:34
  80.3 10.8 %collective-permute-start.16 = (bf16[256,256]{1,0:T(8,128)(2,1)S(1)}, bf16[256,256]{1,0:T(8,128)(2,1)S(1)}, u32[]{:S(2)}, u32[]{:S(2)}) collective-permute-start(bf16[256,256]{1,0:T(8,128)(2,1)S(1)} %shard_map.135.refs_2_), channel_id=1, source_target_pairs={{0,2},{1,3},{2,0},{3,1},{4,6},{5,7},{6,4},{7,5},{8,10},{9,11},{10,... | collective-permute-start | bytes 393224 | tf_op jit(solution)/shard_map/ppermute | solution.py:34
  81.1 14.8 %collective-permute-start.19 = (bf16[256,256]{1,0:T(8,128)(2,1)S(1)}, bf16[256,256]{1,0:T(8,128)(2,1)}, u32[]{:S(2)}, u32[]{:S(2)}) collective-permute-start(bf16[256,256]{1,0:T(8,128)(2,1)S(1)} %shard_map.137.refs_6_), channel_id=1, source_target_pairs={{0,2},{1,3},{2,0},{3,1},{4,6},{5,7},{6,4},{7,5},{8,10},{9,11},{10,... | collective-permute-start | bytes 393224 | tf_op jit(solution)/shard_map/ppermute | solution.py:34
  91.0 7.8 %collective-permute-start.15 = (bf16[256,256]{1,0:T(8,128)(2,1)S(1)}, bf16[256,256]{1,0:T(8,128)(2,1)}, u32[]{:S(2)}, u32[]{:S(2)}) collective-permute-start(bf16[256,256]{1,0:T(8,128)(2,1)S(1)} %shard_map.135.refs_2_), channel_id=1, source_target_pairs={{0,1},{1,0},{2,3},{3,2},{4,5},{5,4},{6,7},{7,6},{8,9},{9,8},{10,11... | collective-permute-start | bytes 393224 | tf_op jit(solution)/shard_map/ppermute | solution.py:34
  95.9 6.5 %collective-permute-start.17 = (bf16[256,256]{1,0:T(8,128)(2,1)S(1)}, bf16[256,256]{1,0:T(8,128)(2,1)}, u32[]{:S(2)}, u32[]{:S(2)}) collective-permute-start(bf16[256,256]{1,0:T(8,128)(2,1)S(1)} %collective-permute-done.16.refs_4_), channel_id=1, source_target_pairs={{0,1},{1,0},{2,3},{3,2},{4,5},{5,4},{6,7},{7,6},{8,9},{9,8},{10,11... | collective-permute-start | bytes 393224 | tf_op jit(solution)/shard_map/ppermute | solution.py:34
  95.9 9.3 %collective-permute-start.18 = (bf16[256,256]{1,0:T(8,128)(2,1)S(1)}, bf16[256,256]{1,0:T(8,128)(2,1)}, u32[]{:S(2)}, u32[]{:S(2)}) collective-permute-start(bf16[256,256]{1,0:T(8,128)(2,1)S(1)} %shard_map.137.refs_6_), channel_id=1, source_target_pairs={{0,1},{1,0},{2,3},{3,2},{4,5},{5,4},{6,7},{7,6},{8,9},{9,8},{10,11... | collective-permute-start | bytes 393224 | tf_op jit(solution)/shard_map/ppermute | solution.py:34
  98.0 8.8 %collective-permute-start.20 = (bf16[256,256]{1,0:T(8,128)(2,1)}, bf16[256,256]{1,0:T(8,128)(2,1)}, u32[]{:S(2)}, u32[]{:S(2)}) collective-permute-start(bf16[256,256]{1,0:T(8,128)(2,1)} %collective-permute-done.19.refs_8_), channel_id=1, source_target_pairs={{0,1},{1,0},{2,3},{3,2},{4,5},{5,4},{6,7},{7,6},{8,9},{9,8},{10,11... | collective-permute-start | bytes 393224 | tf_op jit(solution)/shard_map/ppermute | solution.py:34
  98.8 11.3 %collective-permute-start.12 = (bf16[512,256]{1,0:T(8,128)(2,1)S(1)}, bf16[512,256]{1,0:T(8,128)(2,1)S(1)}, u32[]{:S(2)}, u32[]{:S(2)}) collective-permute-start(bf16[512,256]{1,0:T(8,128)(2,1)S(1)} %copy-done.3), channel_id=1, source_target_pairs={{0,4},{4,0},{8,12},{12,8},{1,5},{5,1},{9,13},{13,9},{2,6},{6,2},{1... | collective-permute-start | bytes 786440 | tf_op jit(solution)/shard_map/ppermute | solution.py:34
  110.0 2.2 %collective-permute-start.25 = (bf16[512,256]{1,0:T(8,128)(2,1)S(1)}, bf16[512,256]{1,0:T(8,128)(2,1)S(1)}, u32[]{:S(2)}, u32[]{:S(2)}) collective-permute-start(bf16[512,256]{1,0:T(8,128)(2,1)S(1)} %get-tuple-element.41), channel_id=1, source_target_pairs={{0,4},{4,0},{8,12},{12,8},{1,5},{5,1},{9,13},{13,9},{2,6},{6,2},{1... | collective-permute-start | bytes 786440 | tf_op jit(solution)/shard_map/ppermute | solution.py:34
  111.6 2.0 %collective-permute-start.24 = (bf16[512,256]{1,0:T(8,128)(2,1)S(1)}, bf16[512,256]{1,0:T(8,128)(2,1)S(1)}, u32[]{:S(2)}, u32[]{:S(2)}) collective-permute-start(bf16[512,256]{1,0:T(8,128)(2,1)S(1)} %get-tuple-element.39), channel_id=1, source_target_pairs={{0,4},{4,0},{8,12},{12,8},{1,5},{5,1},{9,13},{13,9},{2,6},{6,2},{1... | collective-permute-start | bytes 786440 | tf_op jit(solution)/shard_map/ppermute | solution.py:34
  112.2 8.3 %collective-permute-start.26 = (bf16[512,256]{1,0:T(8,128)(2,1)S(1)}, bf16[512,256]{1,0:T(8,128)(2,1)S(1)}, u32[]{:S(2)}, u32[]{:S(2)}) collective-permute-start(bf16[512,256]{1,0:T(8,128)(2,1)S(1)} %add_convert_fusion), channel_id=1, source_target_pairs={{0,8},{4,12},{8,0},{12,4},{1,9},{5,13},{9,1},{13,5},{2,10},{6,14},... | collective-permute-start | bytes 786440 | tf_op jit(solution)/shard_map/ppermute | solution.py:34
  (9 other events, 133.9 us)
